TPU v7x, 512 devices: a whole 4x8x8 slice. The times are simulated.
512 devices in a mesh: dp: 8 (over z_hi, x), expert: 64 (over y, z_lo, core).
Axes of the slice: x: 4, y: 8, z: 8 (z_hi: 2, z_lo: 4; z = z_hi * 4 + z_lo), core: 2. Of those that a mesh axis runs over, the one named last changes fastest.
Arguments:
- tokens: bfloat16 [65536, 1024], P(('dp', 'expert')), may hold values from -6 to 6
- cotangent: bfloat16 [65536, 1024], P(('dp', 'expert')), may hold values from -6 to 6
- pick_lists: int32 [8, 64, 128], P('dp'), may hold values from 0 to 8191, as said below
- combine: float32 [8, 64, 128], P('dp'), may hold values from 0.1 to 1
- w_gate: bfloat16 [64, 1024, 1024], P('expert', 'dp'), may hold values from -0.1875 to 0.1875
- w_up: bfloat16 [64, 1024, 1024], P('expert', 'dp'), may hold values from -0.1875 to 0.1875
- w_down: bfloat16 [64, 1024, 1024], P('expert', 'dp'), may hold values from -0.1875 to 0.1875
Outputs:
- layer_out: bfloat16 [65536, 1024], P(('dp', 'expert'))
- tokens_grad: bfloat16 [65536, 1024], P(('dp', 'expert'))
- grad_gate: bfloat16 [64, 1024, 1024], P('expert', 'dp')
- grad_up: bfloat16 [64, 1024, 1024], P('expert', 'dp')
- grad_down: bfloat16 [64, 1024, 1024], P('expert', 'dp')
Inputs may be any that keep to these rules, and one draw needn't show every extreme that they name: Each list pick_lists[r, e] names 128 distinct tokens of replica r. Token numbers j * 128 to (j + 1) * 128 - 1 are those of the device with index j on the expert axis; at most 4 picks of one expert in one replica fall among one device's tokens, and for every expert and replica exactly 4 fall among some device's.
All inputs are finite; a program needn't handle non-finite values.
Results may differ from a plain program's by a relative error of at most 0.013.
Values may be sent and summed in bfloat16 or wider, within the bound.
No kernel may reach another device: no remote copies, remote signals or barrier semaphores. Data moves between devices by JAX's collectives and lax.ppermute only.
A program may use at most 64 MiB of HBM per device.

v0:
```python
import jax
import jax.numpy as jnp
from jax import lax
from jax.sharding import PartitionSpec as P


def silu_parts(gate_pre):
    sigma_gate = jax.nn.sigmoid(gate_pre)
    return (gate_pre * sigma_gate, sigma_gate)


def project_hidden(row_block, gate_w, up_w):
    dims = (((1,), (1,)), ((), ()))
    gate_pre = lax.dot_general(row_block, gate_w, dims, preferred_element_type=jnp.float32)
    up_pre = lax.dot_general(row_block, up_w, dims, preferred_element_type=jnp.float32)
    silu_gate, sigma_gate = silu_parts(gate_pre)
    hidden = (silu_gate * up_pre).astype(jnp.bfloat16)
    return (gate_pre, up_pre, silu_gate, sigma_gate, hidden)


def backward_terms(grad_block, gate_pre, up_pre, silu_gate, sigma_gate, gate_w, up_w, down_w):
    dims = (((1,), (1,)), ((), ()))
    d_hidden = lax.dot_general(grad_block, down_w, dims, preferred_element_type=jnp.float32)
    d_gate = (d_hidden * up_pre * sigma_gate * (1.0 + gate_pre * (1.0 - sigma_gate))).astype(
        jnp.bfloat16
    )
    d_up = (d_hidden * silu_gate).astype(jnp.bfloat16)
    back_part = jnp.dot(d_gate, gate_w, preferred_element_type=jnp.float32) + jnp.dot(
        d_up, up_w, preferred_element_type=jnp.float32
    )
    return (d_gate, d_up, back_part)


def weight_grads(row_block, grad_block, hidden, d_gate, d_up):
    dims = (((0,), (0,)), ((), ()))
    grad_gate = lax.dot_general(d_gate, row_block, dims, preferred_element_type=jnp.float32).astype(
        jnp.bfloat16
    )
    grad_up = lax.dot_general(d_up, row_block, dims, preferred_element_type=jnp.float32).astype(
        jnp.bfloat16
    )
    grad_down = lax.dot_general(
        hidden, grad_block, dims, preferred_element_type=jnp.float32
    ).astype(jnp.bfloat16)
    return (grad_gate, grad_up, grad_down)


def per_device(tokens, cotangent, pick_lists, combine, w_gate, w_up, w_down):
    n_experts = lax.axis_size("expert")
    my_index = lax.axis_index("expert")
    tok_rows = tokens.shape[0]
    feat_width = tokens.shape[1]
    capacity = pick_lists.shape[2]
    slot_count = max(2, (2 * capacity + n_experts - 1) // n_experts)
    list_all = pick_lists[0]
    weight_all = combine[0]
    source_dev = list_all // tok_rows
    within_dev = list_all - source_dev * tok_rows
    is_mine = (source_dev == my_index).astype(jnp.int32)
    rank_mine = jnp.cumsum(is_mine, axis=1) - 1
    slot_ids = jnp.arange(slot_count, dtype=jnp.int32)
    select_mask = (is_mine[:, :, None] == 1) & (rank_mine[:, :, None] == slot_ids[None, None, :])
    select_int = select_mask.astype(jnp.int32)
    flat_row = jnp.sum(select_int * within_dev[:, :, None], axis=1).reshape(-1)
    flat_valid = (jnp.sum(select_int, axis=1) > 0).reshape(-1)
    flat_weight = jnp.sum(jnp.where(select_mask, weight_all[:, :, None], 0.0), axis=1).reshape(-1)
    slot_shape = (n_experts, slot_count, feat_width)
    row_send = jnp.where(
        flat_valid[:, None], jnp.take(tokens, flat_row, axis=0), jnp.zeros((), jnp.bfloat16)
    ).reshape(slot_shape)
    cot_rows = jnp.take(cotangent, flat_row, axis=0).astype(jnp.float32)
    grad_send = (
        jnp.where(flat_valid[:, None], flat_weight[:, None] * cot_rows, 0.0)
        .astype(jnp.bfloat16)
        .reshape(slot_shape)
    )
    own_source = lax.dynamic_index_in_dim(source_dev, my_index, 0, keepdims=False)
    order_ids = jnp.arange(capacity, dtype=jnp.int32)
    earlier = order_ids[:, None] > order_ids[None, :]
    same_source = own_source[:, None] == own_source[None, :]
    own_rank = jnp.sum((earlier & same_source).astype(jnp.int32), axis=1)
    position = own_source * slot_count + own_rank

    def compact(received):
        return jnp.take(received.reshape(n_experts * slot_count, feat_width), position, axis=0)

    def expand(result_rows):
        empty_slots = jnp.zeros((n_experts * slot_count, feat_width), jnp.bfloat16)
        return empty_slots.at[position].set(result_rows.astype(jnp.bfloat16)).reshape(slot_shape)

    gate_w = w_gate[0]
    up_w = w_up[0]
    down_w = w_down[0]
    recv_rows = lax.all_to_all(row_send, "expert", split_axis=0, concat_axis=0, tiled=True)
    row_block = lax.all_gather(compact(recv_rows), "dp", axis=0, tiled=True)
    gate_pre, up_pre, silu_gate, sigma_gate, hidden = project_hidden(row_block, gate_w, up_w)
    out_part = jnp.dot(hidden, down_w, preferred_element_type=jnp.float32)
    out_rows = lax.psum_scatter(
        out_part.astype(jnp.bfloat16), "dp", scatter_dimension=0, tiled=True
    ).astype(jnp.float32)
    out_slots = lax.all_to_all(expand(out_rows), "expert", split_axis=0, concat_axis=0, tiled=True)
    recv_grads = lax.all_to_all(grad_send, "expert", split_axis=0, concat_axis=0, tiled=True)
    grad_block = lax.all_gather(compact(recv_grads), "dp", axis=0, tiled=True)
    d_gate, d_up, back_part = backward_terms(
        grad_block, gate_pre, up_pre, silu_gate, sigma_gate, gate_w, up_w, down_w
    )
    back_rows = lax.psum_scatter(
        back_part.astype(jnp.bfloat16), "dp", scatter_dimension=0, tiled=True
    ).astype(jnp.float32)
    back_slots = lax.all_to_all(
        expand(back_rows), "expert", split_axis=0, concat_axis=0, tiled=True
    )
    grad_gate, grad_up, grad_down = weight_grads(row_block, grad_block, hidden, d_gate, d_up)
    out_flat = jnp.where(
        flat_valid[:, None],
        flat_weight[:, None] * out_slots.reshape(-1, feat_width).astype(jnp.float32),
        0.0,
    )
    layer_out = (
        jnp.zeros((tok_rows, feat_width), jnp.float32)
        .at[flat_row]
        .add(out_flat)
        .astype(jnp.bfloat16)
    )
    back_flat = jnp.where(
        flat_valid[:, None], back_slots.reshape(-1, feat_width).astype(jnp.float32), 0.0
    )
    tokens_grad = (
        jnp.zeros((tok_rows, feat_width), jnp.float32)
        .at[flat_row]
        .add(back_flat)
        .astype(jnp.bfloat16)
    )
    return (layer_out, tokens_grad, grad_gate[None], grad_up[None], grad_down[None])


def solution(mesh):
    placed = (
        P(("dp", "expert"), None),
        P(("dp", "expert"), None),
        P("dp", None, None),
        P("dp", None, None),
        P("expert", "dp", None),
        P("expert", "dp", None),
        P("expert", "dp", None),
    )
    return jax.shard_map(
        per_device,
        mesh=mesh,
        in_specs=placed,
        out_specs=(
            P(("dp", "expert"), None),
            P(("dp", "expert"), None),
            P("expert", "dp", None),
            P("expert", "dp", None),
            P("expert", "dp", None),
        ),
        check_vma=False,
    )
```

profile of v0, /device:TPU:1, one launch (start us, length us, event | category | flops | bytes accessed | tf_op | source)
XLA Modules:
  0.0 480.7 jit_solution(4581792306209189560)
XLA Ops:
  7.2 0.8 broadcast_compare_fusion
  8.0 0.3 reduce_window_sum.11
  8.3 0.8 add_select_fusion
  9.1 0.2 convert_reduce_fusion
  9.6 0.9 select_reduce_fusion
  10.6 0.1 gt.25
  10.9 1.2 gather_fusion.2
  12.1 0.3 select_convert_fusion
  12.4 1.0 reshape.203
  13.4 14.6 %all-to-all-start.2 = ((bf16[64,4,1024]{2,1,0:T(4,128)(2,1)}), bf16[64,4,1024]{2,1,0:T(4,128)(2,1)S(1)}, u32[]{:S(2)}, u32[]{:S(2)}) async-start(bf16[64,4,1024]{2,1,0:T(4,128)(2,1)} %reshape.203), calls=%async_computation.3 | async-start | bytes 1048576 | tf_op jit(solution)/shard_map/all_to_all | solution.py:102
  28.0 1.2 gather_fusion
  29.1 0.1 select_select_fusion
  29.3 1.0 reshape.200
  30.3 15.4 %all-to-all-done.2 = bf16[64,4,1024]{2,1,0:T(4,128)(2,1)S(1)} async-done(((bf16[64,4,1024]{2,1,0:T(4,128)(2,1)}), bf16[64,4,1024]{2,1,0:T(4,128)(2,1)S(1)}, u32[]{:S(2)}, u32[]{:S(2)}) %all-to-all-start.2) | async-done | bytes 524320 | tf_op jit(solution)/shard_map/all_to_all | solution.py:102
  45.6 5.6 %all-to-all-start = ((bf16[64,4,1024]{2,1,0:T(4,128)(2,1)}), bf16[64,4,1024]{2,1,0:T(4,128)(2,1)S(1)}, u32[]{:S(2)}, u32[]{:S(2)}) async-start(bf16[64,4,1024]{2,1,0:T(4,128)(2,1)} %reshape.200), calls=%async_computation | async-start | bytes 1048576 | tf_op jit(solution)/shard_map/all_to_all | solution.py:94
  51.3 0.2 convert_reduce_fusion.1
  51.5 0.1 reshape.204
  51.6 0.9 gather_fusion.3
  52.5 16.4 %all-to-all-done = bf16[64,4,1024]{2,1,0:T(4,128)(2,1)S(1)} async-done(((bf16[64,4,1024]{2,1,0:T(4,128)(2,1)}), bf16[64,4,1024]{2,1,0:T(4,128)(2,1)S(1)}, u32[]{:S(2)}, u32[]{:S(2)}) %all-to-all-start) | async-done | bytes 524320 | tf_op jit(solution)/shard_map/all_to_all | solution.py:94
  68.9 0.1 reshape.201
  69.1 0.9 gather_fusion.1
  69.9 0.9 broadcast_select_fusion
  70.9 0.7 all-gather.5.cloned.1.call-update
  71.7 78.6 %all-gather.3.cloned.1.call-done = bf16[1024,1024]{1,0:T(8,128)(2,1)} async-done(((bf16[128,1024]{1,0:T(8,128)(2,1)}), bf16[1024,1024]{1,0:T(8,128)(2,1)}) %all-gather.3.cloned.1.call-update) | async-done | bytes 2097168 | tf_op jit(solution)/shard_map/all_gather | solution.py:95
  150.3 3.3 fusion.18
  153.6 1.5 fusion.22
  155.1 76.9 %all-gather.5.cloned.1.call-done = bf16[1024,1024]{1,0:T(8,128)(2,1)} async-done(((bf16[128,1024]{1,0:T(8,128)(2,1)}), bf16[1024,1024]{1,0:T(8,128)(2,1)}) %all-gather.5.cloned.1.call-update) | async-done | bytes 2097168 | tf_op jit(solution)/shard_map/all_gather | solution.py:103
  232.0 2.6 multiply_convert_fusion
  234.7 0.7 copy-done.6
  235.3 2.0 convolution_convert_fusion
  237.4 0.7 fusion.20
  238.1 2.0 add_convert_fusion
  240.2 94.4 %reduce-scatter.3.cloned.1.call-done = bf16[128,1024]{1,0:T(8,128)(2,1)} async-done(((bf16[1024,1024]{1,0:T(8,128)(2,1)}), bf16[128,1024]{1,0:T(8,128)(2,1)}) %reduce-scatter.3.cloned.1.call-update) | async-done | bytes 262160 | tf_op jit(solution)/shard_map/reduce_scatter | solution.py:98
  334.6 1.7 scatter_custom_fusion
  336.3 1.0 reshape.202
  337.3 10.0 %all-to-all-start.1 = ((bf16[64,4,1024]{2,1,0:T(4,128)(2,1)}), bf16[64,4,1024]{2,1,0:T(4,128)(2,1)S(1)}, u32[]{:S(2)}, u32[]{:S(2)}) async-start(bf16[64,4,1024]{2,1,0:T(4,128)(2,1)} %reshape.202), calls=%async_computation.2 | async-start | bytes 1048576 | tf_op jit(solution)/shard_map/all_to_all | solution.py:101
  347.3 92.8 %reduce-scatter.5.cloned.1.call-done = bf16[128,1024]{1,0:T(8,128)(2,1)} async-done(((bf16[1024,1024]{1,0:T(8,128)(2,1)}), bf16[128,1024]{1,0:T(8,128)(2,1)}) %reduce-scatter.5.cloned.1.call-update) | async-done | bytes 262160 | tf_op jit(solution)/shard_map/reduce_scatter | solution.py:107
  440.1 1.7 scatter_custom_fusion.2
  441.8 1.0 reshape.205
  442.8 9.9 %all-to-all-start.3 = ((bf16[64,4,1024]{2,1,0:T(4,128)(2,1)}), bf16[64,4,1024]{2,1,0:T(4,128)(2,1)S(1)}, u32[]{:S(2)}, u32[]{:S(2)}) async-start(bf16[64,4,1024]{2,1,0:T(4,128)(2,1)} %reshape.205), calls=%async_computation.5 | async-start | bytes 1048576 | tf_op jit(solution)/shard_map/all_to_all | solution.py:110
  452.9 2.9 fusion.2
  455.8 1.2 fusion.1
  457.0 1.2 fusion
  458.2 2.9 scatter_custom_fusion.1
  461.2 0.7 convert_element_type.76
  461.9 8.5 %all-to-all-done.3 = bf16[64,4,1024]{2,1,0:T(4,128)(2,1)S(1)} async-done(((bf16[64,4,1024]{2,1,0:T(4,128)(2,1)}), bf16[64,4,1024]{2,1,0:T(4,128)(2,1)S(1)}, u32[]{:S(2)}, u32[]{:S(2)}) %all-to-all-start.3) | async-done | bytes 524320 | tf_op jit(solution)/shard_map/all_to_all | solution.py:110
  470.5 2.9 scatter_custom_fusion.3
  473.4 0.7 convert_element_type.84
  (46 shorter events, 1.1 us)
Async XLA Ops:
  7.2 224.8 %copy-start = (bf16[1,128,1024]{2,1,0:T(8,128)(2,1)S(1)}, bf16[1,128,1024]{2,1,0:T(8,128)(2,1)}, u32[]{:S(2)}) copy-start(bf16[1,128,1024]{2,1,0:T(8,128)(2,1)} %param.17) | copy-start | bytes 786436
  7.2 3.7 copy-start.1
  12.1 15.9 %copy-start.2 = (bf16[128,1024]{1,0:T(8,128)(2,1)S(1)}, bf16[128,1024]{1,0:T(8,128)(2,1)}, u32[]{:S(2)}) copy-start(bf16[128,1024]{1,0:T(8,128)(2,1)} %param.11) | copy-start | bytes 786436
  13.4 32.3 %all-to-all-start.2 = ((bf16[64,4,1024]{2,1,0:T(4,128)(2,1)}), bf16[64,4,1024]{2,1,0:T(4,128)(2,1)S(1)}, u32[]{:S(2)}, u32[]{:S(2)}) async-start(bf16[64,4,1024]{2,1,0:T(4,128)(2,1)} %reshape.203), calls=%async_computation.3 | async-start | bytes 1048576 | tf_op jit(solution)/shard_map/all_to_all | solution.py:102
  45.6 23.3 %all-to-all-start = ((bf16[64,4,1024]{2,1,0:T(4,128)(2,1)}), bf16[64,4,1024]{2,1,0:T(4,128)(2,1)S(1)}, u32[]{:S(2)}, u32[]{:S(2)}) async-start(bf16[64,4,1024]{2,1,0:T(4,128)(2,1)} %reshape.200), calls=%async_computation | async-start | bytes 1048576 | tf_op jit(solution)/shard_map/all_to_all | solution.py:94
  51.2 99.1 %all-gather.3.cloned.1.call-start = ((), (), s32[]{:S(2)}) async-start(), calls=%async_computation.6 | async-start | bytes 2359296 | tf_op jit(solution)/shard_map/all_gather | solution.py:95
  69.0 81.2 %copy-start.10 = (bf16[1,128,1024]{2,1,0:T(8,128)(2,1)S(1)}, bf16[1,128,1024]{2,1,0:T(8,128)(2,1)}, u32[]{:S(2)}) copy-start(bf16[1,128,1024]{2,1,0:T(8,128)(2,1)} %param.16) | copy-start | bytes 786436
  69.9 83.6 %copy-start.7 = (bf16[1,128,1024]{2,1,0:T(8,128)(2,1)S(1)}, bf16[1,128,1024]{2,1,0:T(8,128)(2,1)}, u32[]{:S(2)}) copy-start(bf16[1,128,1024]{2,1,0:T(8,128)(2,1)} %param.15) | copy-start | bytes 786436
  70.9 161.1 %all-gather.5.cloned.1.call-start = ((), (), s32[]{:S(2)}) async-start(), calls=%async_computation.8 | async-start | bytes 2359296 | tf_op jit(solution)/shard_map/all_gather | solution.py:103
  71.6 263.0 %reduce-scatter.3.cloned.1.call-start = ((), (), s32[]{:S(2)}) async-start(), calls=%async_computation.7 | async-start | bytes 2359296 | tf_op jit(solution)/shard_map/reduce_scatter | solution.py:98
  150.3 3.3 copy-start.3
  234.6 0.7 copy-start.6
  234.6 2.8 copy-start.4
  234.6 3.5 copy-start.8
  237.4 202.7 %reduce-scatter.5.cloned.1.call-start = ((), (), s32[]{:S(2)}) async-start(), calls=%async_computation.9 | async-start | bytes 2359296 | tf_op jit(solution)/shard_map/reduce_scatter | solution.py:107
  337.3 105.5 %all-to-all-start.1 = ((bf16[64,4,1024]{2,1,0:T(4,128)(2,1)}), bf16[64,4,1024]{2,1,0:T(4,128)(2,1)S(1)}, u32[]{:S(2)}, u32[]{:S(2)}) async-start(bf16[64,4,1024]{2,1,0:T(4,128)(2,1)} %reshape.202), calls=%async_computation.2 | async-start | bytes 1048576 | tf_op jit(solution)/shard_map/all_to_all | solution.py:101
  442.8 27.6 %all-to-all-start.3 = ((bf16[64,4,1024]{2,1,0:T(4,128)(2,1)}), bf16[64,4,1024]{2,1,0:T(4,128)(2,1)S(1)}, u32[]{:S(2)}, u32[]{:S(2)}) async-start(bf16[64,4,1024]{2,1,0:T(4,128)(2,1)} %reshape.205), calls=%async_computation.5 | async-start | bytes 1048576 | tf_op jit(solution)/shard_map/all_to_all | solution.py:110
  452.8 3.0 copy-start.9
  452.9 4.1 copy-start.5
Sparse Core Ops, SparseCore 0:
  71.0 79.2 all-gather.2
  154.1 77.8 all-gather.4
  237.5 97.0 reduce-scatter.2
  339.1 100.9 reduce-scatter.4
where the time goes:
time: 481 us
  waiting for transfers between devices  384 us (80%)
  starting transfers between devices  40.2 us (8%)
  matrix products  17.4 us (4%)
  between operations  14.1 us (3%)
  local copies, waits for them, and re-layouts  13.3 us (3%)
  other arithmetic  11.8 us (2%)
    reduce_scatter x1, waiting for transfers between devices, per_device(): lax.psum_scatter(out_part.astype(jnp.bfloat16), 'dp', scatter_dimension=0...  94.4 us
    reduce_scatter x1, waiting for transfers between devices, per_device(): lax.psum_scatter(back_part.astype(jnp.bfloat16), 'dp', scatter_dimension=...  92.8 us
    all_gather x1, waiting for transfers between devices, per_device(): row_block = lax.all_gather(compact(recv_rows), 'dp', axis=0, tiled=True)  78.6 us
    all_gather x1, waiting for transfers between devices, per_device(): grad_block = lax.all_gather(compact(recv_grads), 'dp', axis=0, tiled=True)  76.9 us
    all_to_all x1, waiting for transfers between devices, per_device(): lax.all_to_all(row_send, 'expert', split_axis=0, concat_axis=0, tiled=True)  16.4 us
    all_to_all x1, waiting for transfers between devices, per_device(): lax.all_to_all(grad_send, 'expert', split_axis=0, concat_axis=0, tiled=True)  15.4 us
    all_to_all x1, starting transfers between devices, per_device(): lax.all_to_all(grad_send, 'expert', split_axis=0, concat_axis=0, tiled=True)  14.6 us
    all_to_all x1, starting transfers between devices, per_device(): lax.all_to_all(expand(out_rows), 'expert', split_axis=0, concat_axis=0, t...  9.97 us
  transfers between devices with their start and end apart: 8, of which 7 were waited for; matrix products, arithmetic and copies ran while one was open for 5% of the time, Pallas kernels for 0%

commit v1 on v0

v1 whole, which is shorter than its diff:
```python
import jax
import jax.numpy as jnp
from jax import lax
from jax.experimental import pallas as pl
from jax.experimental.pallas import tpu as pltpu
from jax.sharding import PartitionSpec as P

N_X = 4
N_HALF = 2
SLOT = 4
BF16 = jnp.bfloat16
F32 = jnp.float32

HALF_PAIRS = [[i, i + N_X] for i in range(N_X)]


def x_shift(step):
    return [
        (h * N_X + i, h * N_X + (i + step) % N_X) for h in range(N_HALF) for i in range(N_X)
    ]


def mm(a, b, contract_a, contract_b):
    return lax.dot_general(
        a, b, (((contract_a,), (contract_b,)), ((), ())), preferred_element_type=F32
    )


def kernel_call(body, out_shapes, n_smem, n_vmem, flops, nbytes):
    return pl.pallas_call(
        body,
        out_shape=out_shapes,
        in_specs=[pl.BlockSpec(memory_space=pltpu.SMEM)] * n_smem
        + [pl.BlockSpec(memory_space=pltpu.VMEM)] * n_vmem,
        out_specs=jax.tree.map(lambda _: pl.BlockSpec(memory_space=pltpu.VMEM), out_shapes),
        cost_estimate=pl.CostEstimate(flops=flops, bytes_accessed=nbytes, transcendentals=0),
        compiler_params=pltpu.CompilerParams(vmem_limit_bytes=48 * 1024 * 1024),
    )


def strictly_before(n):
    rows = lax.broadcasted_iota(jnp.int32, (n, n), 0)
    cols = lax.broadcasted_iota(jnp.int32, (n, n), 1)
    return (rows < cols).astype(BF16)


def slot_tables(my, pick, weight, tok_rows):
    n_experts, cap = pick.shape
    low = my * tok_rows
    mine = (pick >= low) & (pick < low + tok_rows)
    rank = mm(mine.astype(F32).astype(BF16), strictly_before(cap), 1, 0)
    code = jnp.where(mine, rank, -1.0)
    place = jnp.where(mine, (pick - low + 1).astype(F32), 0.0)
    shape = (n_experts, 2 * SLOT, cap)
    slot = (lax.broadcasted_iota(jnp.int32, shape, 1) % SLOT).astype(F32)
    hit = jnp.broadcast_to(code[:, None, :], shape) == slot
    row = jnp.sum(
        jnp.where(hit, jnp.broadcast_to(place[:, None, :], shape), 0.0), axis=2, keepdims=True
    )
    share = jnp.sum(
        jnp.where(hit, jnp.broadcast_to(weight[:, None, :], shape), 0.0), axis=2, keepdims=True
    )
    return row - 1.0, share


def send_body(my_ref, pick_ref, weight_ref, tok_ref, cot_ref, out_ref):
    n_experts = pick_ref.shape[0]
    tok_rows = tok_ref.shape[0]
    row, share = slot_tables(my_ref[0], pick_ref[...], weight_ref[...], tok_rows)
    shape = (n_experts, 2 * SLOT, 2 * tok_rows)
    lane = lax.broadcasted_iota(jnp.int32, shape, 2).astype(F32)
    second = lax.broadcasted_iota(jnp.int32, (n_experts, 2 * SLOT, 1), 1) >= SLOT
    target = jnp.where(second & (row >= 0.0), row + float(tok_rows), row)
    scale = jnp.where(second, share, 1.0)
    n_slots = n_experts * 2 * SLOT
    select = (lane == target).astype(F32).reshape(n_slots, 2 * tok_rows).astype(BF16)
    both = jnp.concatenate([tok_ref[...], cot_ref[...]], axis=0)
    rows = mm(select, both, 1, 0)
    scale = jnp.broadcast_to(scale, (n_experts, 2 * SLOT, 128)).reshape(n_slots, 128)
    for c in range(rows.shape[1] // 128):
        part = rows[:, c * 128 : (c + 1) * 128] * scale
        out_ref[:, c * 128 : (c + 1) * 128] = part.astype(BF16)


def table_body(my_ref, pick_ref, weight_ref, place_ref, back_ref):
    n_experts, cap = pick_ref.shape
    my = my_ref[0]
    n_slots = n_experts * 2 * SLOT
    tok_rows = cap_rows = back_ref.shape[1] // 3
    own = pick_ref[pl.ds(my, 1), :]
    source = lax.shift_right_logical(own, 7)
    from_dev = (
        lax.broadcasted_iota(jnp.int32, (n_experts, cap), 0)
        == jnp.broadcast_to(source, (n_experts, cap))
    ).astype(F32)
    rank = jnp.sum(
        from_dev * mm(from_dev.astype(BF16), strictly_before(cap), 1, 0), axis=0, keepdims=True
    )
    position = source * (2 * SLOT) + rank.astype(jnp.int32)
    both = jnp.concatenate([position, position + SLOT], axis=1)
    sub = lax.broadcasted_iota(jnp.int32, (n_slots, 2 * cap), 0)
    place_ref[...] = (sub == jnp.broadcast_to(both, (n_slots, 2 * cap))).astype(F32).astype(BF16)
    row, share = slot_tables(my, pick_ref[...], weight_ref[...], tok_rows)
    shape = (n_experts, 2 * SLOT, tok_rows)
    lane = lax.broadcasted_iota(jnp.int32, shape, 2).astype(F32)
    second = lax.broadcasted_iota(jnp.int32, shape, 1) >= SLOT
    hit = lane == row
    high = share.astype(BF16).astype(F32)
    low = share - high
    zero = jnp.zeros(shape, F32)
    first_hit = hit & ~second
    pieces = (
        jnp.where(first_hit, high, zero),
        jnp.where(hit & second, 1.0, zero),
        jnp.where(first_hit, low, zero),
    )
    for i, piece in enumerate(pieces):
        back_ref[:, i * tok_rows : (i + 1) * tok_rows] = piece.reshape(n_slots, tok_rows).astype(
            BF16
        )


def compact_body(place_ref, recv_ref, chosen_ref, weighted_ref):
    rows = mm(place_ref[...], recv_ref[...], 0, 0).astype(BF16)
    cap = chosen_ref.shape[0]
    chosen_ref[...] = rows[:cap]
    weighted_ref[...] = rows[cap:]


def expert_body(
    half_ref,
    chosen_ref,
    weighted_ref,
    w0,
    w1,
    w2,
    w3,
    own_ref,
    send_out_ref,
    send_back_ref,
    g_own,
    g1,
    g2,
    g3,
):
    half = half_ref[0]
    _, cap, feat = chosen_ref.shape
    chosen = jnp.concatenate([chosen_ref[half], chosen_ref[1 - half]], axis=0)
    weighted = jnp.concatenate([weighted_ref[half], weighted_ref[1 - half]], axis=0)
    width = w0.shape[0] // 3
    out = jnp.zeros((2 * cap, feat), F32)
    back = jnp.zeros((2 * cap, feat), F32)
    for w_ref, g_ref in ((w0, g_own), (w1, g1), (w2, g2), (w3, g3)):
        pre = mm(chosen, w_ref[: 2 * width], 1, 1)
        d_hidden = mm(weighted, w_ref[2 * width :], 1, 1)
        gate, up = pre[:, :width], pre[:, width:]
        sigma = jax.nn.sigmoid(gate)
        silu = gate * sigma
        hidden = (silu * up).astype(BF16)
        d_gate = (d_hidden * up * sigma * (1.0 + gate * (1.0 - sigma))).astype(BF16)
        d_up = (d_hidden * silu).astype(BF16)
        d_both = jnp.concatenate([d_gate, d_up], axis=1)
        out = out + mm(hidden, w_ref[2 * width :], 1, 0)
        back = back + mm(d_both, w_ref[: 2 * width], 1, 0)
        g_ref[: 2 * width] = mm(d_both, chosen, 0, 0).astype(g_ref.dtype)
        g_ref[2 * width :] = mm(hidden, weighted, 0, 0).astype(g_ref.dtype)
    own_ref[:cap] = out[:cap]
    own_ref[cap:] = back[:cap]
    send_out_ref[...] = out[cap:].astype(BF16)
    send_back_ref[...] = back[cap:].astype(BF16)


def expand_body(half_ref, place_ref, own_ref, other_out_ref, other_back_ref, out_ref):
    there = 1 - half_ref[0]
    other = jnp.concatenate([other_out_ref[there], other_back_ref[there]], axis=0)
    total = (own_ref[...] + other.astype(F32)).astype(BF16)
    out_ref[...] = mm(place_ref[...], total, 1, 0).astype(BF16)


def combine_body(back_ref, slots_ref, layer_ref, grad_ref):
    n = layer_ref.shape[0]
    sums = mm(back_ref[...], slots_ref[...], 0, 0)
    layer_ref[...] = (sums[:n] + sums[2 * n :]).astype(BF16)
    grad_ref[...] = sums[n : 2 * n].astype(BF16)


def weight_sum_body(g_own, g1, g2, g3, gate_ref, up_ref, down_ref):
    width = gate_ref.shape[0]
    for i, ref in enumerate((gate_ref, up_ref, down_ref)):
        piece = pl.ds(i * width, width)
        ref[...] = (
            g_own[piece, :]
            + g1[piece, :].astype(F32)
            + g2[piece, :].astype(F32)
            + g3[piece, :].astype(F32)
        ).astype(BF16)


def per_device(tokens, cotangent, pick_lists, combine, w_gate, w_up, w_down):
    n_experts = lax.axis_size("expert")
    tok_rows, feat = tokens.shape
    cap = pick_lists.shape[2]
    width = w_gate.shape[1]
    n_slots = n_experts * 2 * SLOT
    my = lax.axis_index("expert").astype(jnp.int32).reshape(1)
    half = (lax.axis_index("dp") // N_X).astype(jnp.int32).reshape(1)
    sds = jax.ShapeDtypeStruct
    picks, shares = pick_lists[0], combine[0]

    def exchange(rows):
        parts = rows.reshape(n_experts, 2 * SLOT, feat)
        out = lax.all_to_all(parts, "expert", split_axis=0, concat_axis=0, tiled=True)
        return out.reshape(n_slots, feat)

    def pair_gather(rows):
        return lax.all_gather(rows, "dp", axis_index_groups=HALF_PAIRS)

    row_block = sds((cap, feat), BF16)
    send = kernel_call(send_body, sds((n_slots, feat), BF16), 1, 4, 3 * 10**8, 2 * 10**6)(
        my, picks, shares, tokens, cotangent
    )
    recv = exchange(send)
    place, back_table = kernel_call(
        table_body,
        (sds((n_slots, 2 * cap), BF16), sds((n_slots, 3 * tok_rows), BF16)),
        1,
        2,
        10**8,
        10**6,
    )(my, picks, shares)
    w_own = jnp.concatenate([w_gate[0], w_up[0], w_down[0]], axis=0)
    w_others = [lax.ppermute(w_own, "dp", x_shift(s)) for s in (1, -1, 2)]
    chosen, weighted = kernel_call(
        compact_body, (row_block, row_block), 0, 2, 3 * 10**8, 2 * 10**6
    )(place, recv)
    chosen, weighted = pair_gather(chosen), pair_gather(weighted)
    g_shape = (3 * width, feat)
    own_part, send_out, send_back, g_own, *g_others = kernel_call(
        expert_body,
        (sds((2 * cap, feat), F32), row_block, row_block, sds(g_shape, F32))
        + (sds(g_shape, BF16),) * 3,
        1,
        6,
        3 * 10**9,
        10**7,
    )(half, chosen, weighted, w_own, *w_others)
    g_home = [lax.ppermute(g, "dp", x_shift(-s)) for g, s in zip(g_others, (1, -1, 2))]
    other_out, other_back = pair_gather(send_out), pair_gather(send_back)
    slots = kernel_call(expand_body, sds((n_slots, feat), BF16), 1, 4, 3 * 10**8, 4 * 10**6)(
        half, place, own_part, other_out, other_back
    )
    returned = exchange(slots)
    layer_out, tokens_grad = kernel_call(
        combine_body, (sds((tok_rows, feat), BF16),) * 2, 0, 2, 4 * 10**8, 2 * 10**6
    )(back_table, returned)
    grads = kernel_call(
        weight_sum_body, (sds((width, feat), BF16),) * 3, 0, 4, 10**6, 5 * 10**6
    )(g_own, *g_home)
    return (layer_out, tokens_grad) + tuple(g[None] for g in grads)


def solution(mesh):
    rows = P(("dp", "expert"), None)
    lists = P("dp", None, None)
    weights = P("expert", "dp", None)
    return jax.shard_map(
        per_device,
        mesh=mesh,
        in_specs=(rows, rows, lists, lists, weights, weights, weights),
        out_specs=(rows, rows, weights, weights, weights),
        check_vma=False,
    )
```

time: 481 us -> 178 us (0.37)
  waiting for transfers between devices: 384 us -> 49.3 us
  blocking collectives: 0 us -> 53.7 us
  matrix products: 17.4 us -> 0 us
  starting transfers between devices: 40.2 us -> 54.1 us
  between operations: 14.1 us -> 0.83 us
  Pallas kernels: 0 us -> 12.8 us
  other arithmetic: 11.8 us -> 0.05 us
  local copies, waits for them, and re-layouts: 13.3 us -> 5.09 us
    reduce_scatter x2 -> x0, waiting for transfers between devices: 187 us -> none  [the longest x1 94.4 us: per_device(): lax.psum_scatter(out_part.astype(jnp.bfloat16), 'dp', scatter_dimension=0...]
    all_gather x2 -> x0, waiting for transfers between devices: 156 us -> none  [the longest x1 78.6 us: per_device(): row_block = lax.all_gather(compact(recv_rows), 'dp', axis=0, tiled=True)]
    all_gather x0 -> x4, blocking collectives: none -> 53.7 us  [pair_gather(): return lax.all_gather(rows, 'dp', axis_index_groups=HALF_PAIRS)]
    ppermute x0 -> x6, waiting for transfers between devices: none -> 32.1 us  [the longest x3 32.1 us: per_device(): lax.ppermute(g, 'dp', x_shift(-s))]
    all_to_all x4 -> x2, waiting for transfers between devices: 40.3 us -> 17.2 us  [exchange(): lax.all_to_all(parts, 'expert', split_axis=0, concat_axis=0, tiled=True)]
    ppermute x0 -> x6, starting transfers between devices: none -> 18.7 us  [the longest x3 9.94 us: per_device(): w_others = [lax.ppermute(w_own, 'dp', x_shift(s)) for s in (1, -1, 2)]]
    dot_general x9 -> x0, matrix products: 17.4 us -> none  [the longest x1 3.25 us: project_hidden(): lax.dot_general(row_block, up_w, dims, preferred_element_type=jnp.float32)]
    pallas_call x0 -> x7, Pallas kernels: none -> 12.8 us  [the longest x1 6.32 us: per_device(): kernel_call(expert_body, (sds((2 * cap, feat), F32), row_block, row_block...]
  transfers between devices with their start and end apart: 8 -> 8, of which waited for: 7 -> 4; matrix products, arithmetic and copies ran while one was open for 5% -> 0% of each run, Pallas kernels for 0% -> 1%
where the time goes in v1:
time: 178 us; the launch traced here: 176 us
  starting transfers between devices  54.1 us (30%)
  blocking collectives  53.7 us (30%)
  waiting for transfers between devices  49.3 us (28%)
  Pallas kernels  12.8 us (7%)
  local copies, waits for them, and re-layouts  5.09 us (3%)
    all_gather x4, blocking collectives, pair_gather(): return lax.all_gather(rows, 'dp', axis_index_groups=HALF_PAIRS)  53.7 us
    all_to_all x2, starting transfers between devices, exchange(): lax.all_to_all(parts, 'expert', split_axis=0, concat_axis=0, tiled=True)  35.4 us
    ppermute x3, waiting for transfers between devices, per_device(): lax.ppermute(g, 'dp', x_shift(-s))  32.1 us
    all_to_all x2, waiting for transfers between devices, exchange(): lax.all_to_all(parts, 'expert', split_axis=0, concat_axis=0, tiled=True)  17.2 us
    ppermute x3, starting transfers between devices, per_device(): w_others = [lax.ppermute(w_own, 'dp', x_shift(s)) for s in (1, -1, 2)]  9.94 us
    ppermute x3, starting transfers between devices, per_device(): lax.ppermute(g, 'dp', x_shift(-s))  8.74 us
    pallas_call x1, Pallas kernels, per_device(): kernel_call(expert_body, (sds((2 * cap, feat), F32), row_block, row_block...  6.32 us
    unnamed x34, local copies, waits for them, and re-layouts  5.09 us
  transfers between devices with their start and end apart: 8, of which 4 were waited for; matrix products, arithmetic and copies ran while one was open for 0% of the time, Pallas kernels for 1%

profile of v1, /device:TPU:1, one launch (start us, length us, event | category | flops | bytes accessed | tf_op | source)
XLA Modules:
  0.0 175.9 jit_solution(9395381542951824733)
XLA Ops:
  0.6 0.0 copy-start.2
  0.6 0.9 copy-done.2
  1.6 0.0 copy-start.3
  1.6 0.9 copy-done.3
  2.5 0.8 copy-done.4
  3.3 0.8 copy-done.6
  4.1 1.6 shard_map.111
  5.7 14.7 %all-to-all-start = ((bf16[64,8,1024]{2,1,0:T(8,128)(2,1)}), bf16[64,8,1024]{2,1,0:T(8,128)(2,1)S(1)}, u32[]{:S(2)}, u32[]{:S(2)}) async-start(bf16[64,8,1024]{2,1,0:T(8,128)(2,1)} %bitcast.4), calls=%async_computation | async-start | bytes 2097152 | tf_op jit(solution)/shard_map/all_to_all | solution.py:212
  20.4 0.0 copy-done.14
  20.4 0.0 copy-done.15
  20.5 0.0 copy-done.16
  20.5 0.1 pad_maximum_fusion.w0
  20.5 4.7 %collective-permute-start.2 = (bf16[384,1024]{1,0:T(8,128)(2,1)S(1)}, bf16[384,1024]{1,0:T(8,128)(2,1)}, u32[]{:S(2)}, u32[]{:S(2)}) collective-permute-start(bf16[384,1024]{1,0:T(8,128)(2,1)S(1)} %pad_maximum_fusion.w0), channel_id=1, source_target_pairs={{0,128},{64,192},{128,0},{192,64},{256,384},{320,448},{384,256},{4... | collective-permute-start | bytes 2359304 | tf_op jit(solution)/shard_map/ppermute | solution.py:232
  25.2 2.8 %collective-permute-start.1 = (bf16[384,1024]{1,0:T(8,128)(2,1)S(1)}, bf16[384,1024]{1,0:T(8,128)(2,1)}, u32[]{:S(2)}, u32[]{:S(2)}) collective-permute-start(bf16[384,1024]{1,0:T(8,128)(2,1)S(1)} %pad_maximum_fusion.w0), channel_id=1, source_target_pairs={{0,192},{64,0},{128,64},{192,128},{256,448},{320,256},{384,320},{4... | collective-permute-start | bytes 2359304 | tf_op jit(solution)/shard_map/ppermute | solution.py:232
  28.0 2.5 %collective-permute-start = (bf16[384,1024]{1,0:T(8,128)(2,1)S(1)}, bf16[384,1024]{1,0:T(8,128)(2,1)S(1)}, u32[]{:S(2)}, u32[]{:S(2)}) collective-permute-start(bf16[384,1024]{1,0:T(8,128)(2,1)S(1)} %pad_maximum_fusion.w0), channel_id=1, source_target_pairs={{0,64},{64,128},{128,192},{192,0},{256,320},{320,384},{384,448},{4... | collective-permute-start | bytes 2359304 | tf_op jit(solution)/shard_map/ppermute | solution.py:232
  30.5 0.0 copy-done.5
  30.5 0.0 copy-done.7
  30.5 0.4 shard_map.110
  31.0 0.0 copy-start.12
  31.0 0.8 copy-done.12
  31.7 17.2 %all-to-all-done = bf16[64,8,1024]{2,1,0:T(8,128)(2,1)S(1)} async-done(((bf16[64,8,1024]{2,1,0:T(8,128)(2,1)}), bf16[64,8,1024]{2,1,0:T(8,128)(2,1)S(1)}, u32[]{:S(2)}, u32[]{:S(2)}) %all-to-all-start) | async-done | bytes 1048608 | tf_op jit(solution)/shard_map/all_to_all | solution.py:212
  49.0 0.5 shard_map.112
  49.4 13.7 %all-gather = bf16[256,1024]{1,0:T(8,128)(2,1)S(1)} all-gather(bf16[128,1024]{1,0:T(8,128)(2,1)S(1)} %get-tuple-element.23), channel_id=2, replica_groups={{0,256},{64,320},{128,384},{192,448},{1,257},{65,321},{129,385},{193,44..., dimensions={0}, use_global_device_ids=true | all-gather | bytes 786432 | tf_op jit(solution)/shard_map/all_gather | solution.py:216
  63.2 12.1 %all-gather.1 = bf16[256,1024]{1,0:T(8,128)(2,1)S(1)} all-gather(bf16[128,1024]{1,0:T(8,128)(2,1)S(1)} %get-tuple-element.24), channel_id=3, replica_groups={{0,256},{64,320},{128,384},{192,448},{1,257},{65,321},{129,385},{193,44..., dimensions={0}, use_global_device_ids=true | all-gather | bytes 786432 | tf_op jit(solution)/shard_map/all_gather | solution.py:216
  75.2 0.0 collective-permute-done.2.w3
  75.3 0.0 collective-permute-done.1.w2
  75.3 0.0 collective-permute-done.w1
  75.3 6.3 %shard_map.113 = (f32[256,1024]{1,0:T(8,128)}, bf16[128,1024]{1,0:T(8,128)(2,1)S(1)}, bf16[128,1024]{1,0:T(8,128)(2,1)S(1)}, f32[384,1024]{1,0:T(8,128)}, bf16[3...) custom-call(s32[1]{0:T(128)} %bitcast.3.half_ref, ...), custom_call_target="tpu_custom_call" | custom-call | flops 3000000000 | bytes 10000000 | tf_op jit(solution)/shard_map/pallas_call | solution.py:238
  81.6 0.9 copy-done.8
  82.5 9.9 %all-gather.2 = bf16[256,1024]{1,0:T(8,128)(2,1)S(1)} all-gather(bf16[128,1024]{1,0:T(8,128)(2,1)S(1)} %get-tuple-element.26), channel_id=4, replica_groups={{0,256},{64,320},{128,384},{192,448},{1,257},{65,321},{129,385},{193,44..., dimensions={0}, use_global_device_ids=true | all-gather | bytes 786432 | tf_op jit(solution)/shard_map/all_gather | solution.py:216
  92.4 0.0 copy-done.10
  92.4 18.0 %all-gather.3 = bf16[256,1024]{1,0:T(8,128)(2,1)S(1)} all-gather(bf16[128,1024]{1,0:T(8,128)(2,1)S(1)} %get-tuple-element.27), channel_id=5, replica_groups={{0,256},{64,320},{128,384},{192,448},{1,257},{65,321},{129,385},{193,44..., dimensions={0}, use_global_device_ids=true | all-gather | bytes 786432 | tf_op jit(solution)/shard_map/all_gather | solution.py:216
  110.4 0.0 copy-done.11
  110.4 0.0 copy-done.1
  110.4 1.5 shard_map.114
  111.8 20.7 %all-to-all-start.1 = ((bf16[64,8,1024]{2,1,0:T(8,128)(2,1)}), bf16[64,8,1024]{2,1,0:T(8,128)(2,1)S(1)}, u32[]{:S(2)}, u32[]{:S(2)}) async-start(bf16[64,8,1024]{2,1,0:T(8,128)(2,1)} %bitcast.13), calls=%async_computation.1 | async-start | bytes 2097152 | tf_op jit(solution)/shard_map/all_to_all | solution.py:212
  132.5 3.2 %collective-permute-start.3 = (bf16[384,1024]{1,0:T(8,128)(2,1)}, bf16[384,1024]{1,0:T(8,128)(2,1)S(1)}, u32[]{:S(2)}, u32[]{:S(2)}) collective-permute-start(bf16[384,1024]{1,0:T(8,128)(2,1)} %copy-done.11), channel_id=1, source_target_pairs={{0,192},{64,0},{128,64},{192,128},{256,448},{320,256},{384,320},{4... | collective-permute-start | bytes 2359304 | tf_op jit(solution)/shard_map/ppermute | solution.py:247
  135.7 2.1 %collective-permute-start.4 = (bf16[384,1024]{1,0:T(8,128)(2,1)}, bf16[384,1024]{1,0:T(8,128)(2,1)S(1)}, u32[]{:S(2)}, u32[]{:S(2)}) collective-permute-start(bf16[384,1024]{1,0:T(8,128)(2,1)} %copy-done.10), channel_id=1, source_target_pairs={{0,64},{64,128},{128,192},{192,0},{256,320},{320,384},{384,448},{4... | collective-permute-start | bytes 2359304 | tf_op jit(solution)/shard_map/ppermute | solution.py:247
  137.8 0.0 copy-done.9
  137.8 3.5 %collective-permute-start.5 = (bf16[384,1024]{1,0:T(8,128)(2,1)S(1)}, bf16[384,1024]{1,0:T(8,128)(2,1)S(1)}, u32[]{:S(2)}, u32[]{:S(2)}) collective-permute-start(bf16[384,1024]{1,0:T(8,128)(2,1)S(1)} %copy-done.9), channel_id=1, source_target_pairs={{0,128},{64,192},{128,0},{192,64},{256,384},{320,448},{384,256},{4... | collective-permute-start | bytes 2359304 | tf_op jit(solution)/shard_map/ppermute | solution.py:247
  141.3 12.0 %collective-permute-done.3.g1 = bf16[384,1024]{1,0:T(8,128)(2,1)S(1)} collective-permute-done((bf16[384,1024]{1,0:T(8,128)(2,1)}, bf16[384,1024]{1,0:T(8,128)(2,1)S(1)}, u32[]{:S(2)}, u32[]{:S(2)}) %collective-permute-start.3) | collective-permute-done | bytes 786464 | tf_op jit(solution)/shard_map/ppermute | solution.py:247
  153.3 5.1 %collective-permute-done.4.g2 = bf16[384,1024]{1,0:T(8,128)(2,1)S(1)} collective-permute-done((bf16[384,1024]{1,0:T(8,128)(2,1)}, bf16[384,1024]{1,0:T(8,128)(2,1)S(1)}, u32[]{:S(2)}, u32[]{:S(2)}) %collective-permute-start.4) | collective-permute-done | bytes 786464 | tf_op jit(solution)/shard_map/ppermute | solution.py:247
  158.4 15.0 %collective-permute-done.5.g3 = bf16[384,1024]{1,0:T(8,128)(2,1)S(1)} collective-permute-done((bf16[384,1024]{1,0:T(8,128)(2,1)S(1)}, bf16[384,1024]{1,0:T(8,128)(2,1)S(1)}, u32[]{:S(2)}, u32[]{:S(2)}) %collective-permute-start.5) | collective-permute-done | bytes 786464 | tf_op jit(solution)/shard_map/ppermute | solution.py:247
  173.3 0.0 copy-done
  173.4 1.1 shard_map.116
  174.5 0.0 all-to-all-done.1
  174.5 0.0 copy-done.13
  174.5 1.4 shard_map.115
  (14 shorter events, 0.0 us)
Async XLA Ops:
  0.6 1.0 copy-start.2
  1.6 0.9 copy-start.3
  2.5 0.8 copy-start.4
  3.3 0.8 copy-start.6
  4.1 16.4 %copy-start.14 = (bf16[1,128,1024]{2,1,0:T(8,128)(2,1)S(1)}, bf16[1,128,1024]{2,1,0:T(8,128)(2,1)}, u32[]{:S(2)}) copy-start(bf16[1,128,1024]{2,1,0:T(8,128)(2,1)} %param.13) | copy-start | bytes 786436
  4.1 16.4 %copy-start.15 = (bf16[1,128,1024]{2,1,0:T(8,128)(2,1)S(1)}, bf16[1,128,1024]{2,1,0:T(8,128)(2,1)}, u32[]{:S(2)}) copy-start(bf16[1,128,1024]{2,1,0:T(8,128)(2,1)} %param.12) | copy-start | bytes 786436
  4.1 16.4 %copy-start.16 = (bf16[1,128,1024]{2,1,0:T(8,128)(2,1)S(1)}, bf16[1,128,1024]{2,1,0:T(8,128)(2,1)}, u32[]{:S(2)}) copy-start(bf16[1,128,1024]{2,1,0:T(8,128)(2,1)} %param.11) | copy-start | bytes 786436
  5.7 24.8 %copy-start.5 = (s32[1,64,128]{2,1,0:T(8,128)S(1)}, s32[1,64,128]{2,1,0:T(8,128)}, u32[]{:S(2)}) copy-start(s32[1,64,128]{2,1,0:T(8,128)} %param.9) | copy-start | bytes 98308
  5.7 24.8 %copy-start.7 = (f32[1,64,128]{2,1,0:T(8,128)S(1)}, f32[1,64,128]{2,1,0:T(8,128)}, u32[]{:S(2)}) copy-start(f32[1,64,128]{2,1,0:T(8,128)} %param.10) | copy-start | bytes 98308
  5.7 43.3 %all-to-all-start = ((bf16[64,8,1024]{2,1,0:T(8,128)(2,1)}), bf16[64,8,1024]{2,1,0:T(8,128)(2,1)S(1)}, u32[]{:S(2)}, u32[]{:S(2)}) async-start(bf16[64,8,1024]{2,1,0:T(8,128)(2,1)} %bitcast.4), calls=%async_computation | async-start | bytes 2097152 | tf_op jit(solution)/shard_map/all_to_all | solution.py:212
  20.5 54.7 %collective-permute-start.2 = (bf16[384,1024]{1,0:T(8,128)(2,1)S(1)}, bf16[384,1024]{1,0:T(8,128)(2,1)}, u32[]{:S(2)}, u32[]{:S(2)}) collective-permute-start(bf16[384,1024]{1,0:T(8,128)(2,1)S(1)} %pad_maximum_fusion.w0), channel_id=1, source_target_pairs={{0,128},{64,192},{128,0},{192,64},{256,384},{320,448},{384,256},{4... | collective-permute-start | bytes 2359304 | tf_op jit(solution)/shard_map/ppermute | solution.py:232
  25.2 50.1 %collective-permute-start.1 = (bf16[384,1024]{1,0:T(8,128)(2,1)S(1)}, bf16[384,1024]{1,0:T(8,128)(2,1)}, u32[]{:S(2)}, u32[]{:S(2)}) collective-permute-start(bf16[384,1024]{1,0:T(8,128)(2,1)S(1)} %pad_maximum_fusion.w0), channel_id=1, source_target_pairs={{0,192},{64,0},{128,64},{192,128},{256,448},{320,256},{384,320},{4... | collective-permute-start | bytes 2359304 | tf_op jit(solution)/shard_map/ppermute | solution.py:232
  28.0 47.3 %collective-permute-start = (bf16[384,1024]{1,0:T(8,128)(2,1)S(1)}, bf16[384,1024]{1,0:T(8,128)(2,1)S(1)}, u32[]{:S(2)}, u32[]{:S(2)}) collective-permute-start(bf16[384,1024]{1,0:T(8,128)(2,1)S(1)} %pad_maximum_fusion.w0), channel_id=1, source_target_pairs={{0,64},{64,128},{128,192},{192,0},{256,320},{320,384},{384,448},{4... | collective-permute-start | bytes 2359304 | tf_op jit(solution)/shard_map/ppermute | solution.py:232
  31.0 0.8 copy-start.12
  81.6 0.9 copy-start.8
  82.5 9.9 %copy-start.10 = (bf16[384,1024]{1,0:T(8,128)(2,1)}, bf16[384,1024]{1,0:T(8,128)(2,1)S(1)}, u32[]{:S(2)}) copy-start(bf16[384,1024]{1,0:T(8,128)(2,1)S(1)} %get-tuple-element.32) | copy-start | bytes 2359300
  82.5 27.9 %copy-start.11 = (bf16[384,1024]{1,0:T(8,128)(2,1)}, bf16[384,1024]{1,0:T(8,128)(2,1)S(1)}, u32[]{:S(2)}) copy-start(bf16[384,1024]{1,0:T(8,128)(2,1)S(1)} %get-tuple-element.31) | copy-start | bytes 2359300
  82.5 27.9 %copy-start.1 = (f32[256,1024]{1,0:T(8,128)S(1)}, f32[256,1024]{1,0:T(8,128)}, u32[]{:S(2)}) copy-start(f32[256,1024]{1,0:T(8,128)} %get-tuple-element.25.own_ref) | copy-start | bytes 3145732
  110.4 27.4 %copy-start.9 = (bf16[384,1024]{1,0:T(8,128)(2,1)S(1)}, bf16[384,1024]{1,0:T(8,128)(2,1)}, u32[]{:S(2)}) copy-start(bf16[384,1024]{1,0:T(8,128)(2,1)} %copy-done.8) | copy-start | bytes 2359300
  111.8 61.5 %copy-start = (f32[384,1024]{1,0:T(8,128)S(1)}, f32[384,1024]{1,0:T(8,128)}, u32[]{:S(2)}) copy-start(f32[384,1024]{1,0:T(8,128)} %get-tuple-element.30.g_own) | copy-start | bytes 4718596
  111.8 62.7 %all-to-all-start.1 = ((bf16[64,8,1024]{2,1,0:T(8,128)(2,1)}), bf16[64,8,1024]{2,1,0:T(8,128)(2,1)S(1)}, u32[]{:S(2)}, u32[]{:S(2)}) async-start(bf16[64,8,1024]{2,1,0:T(8,128)(2,1)} %bitcast.13), calls=%async_computation.1 | async-start | bytes 2097152 | tf_op jit(solution)/shard_map/all_to_all | solution.py:212
  132.5 20.7 %collective-permute-start.3 = (bf16[384,1024]{1,0:T(8,128)(2,1)}, bf16[384,1024]{1,0:T(8,128)(2,1)S(1)}, u32[]{:S(2)}, u32[]{:S(2)}) collective-permute-start(bf16[384,1024]{1,0:T(8,128)(2,1)} %copy-done.11), channel_id=1, source_target_pairs={{0,192},{64,0},{128,64},{192,128},{256,448},{320,256},{384,320},{4... | collective-permute-start | bytes 2359304 | tf_op jit(solution)/shard_map/ppermute | solution.py:247
  135.7 22.6 %collective-permute-start.4 = (bf16[384,1024]{1,0:T(8,128)(2,1)}, bf16[384,1024]{1,0:T(8,128)(2,1)S(1)}, u32[]{:S(2)}, u32[]{:S(2)}) collective-permute-start(bf16[384,1024]{1,0:T(8,128)(2,1)} %copy-done.10), channel_id=1, source_target_pairs={{0,64},{64,128},{128,192},{192,0},{256,320},{320,384},{384,448},{4... | collective-permute-start | bytes 2359304 | tf_op jit(solution)/shard_map/ppermute | solution.py:247
  137.8 35.5 %collective-permute-start.5 = (bf16[384,1024]{1,0:T(8,128)(2,1)S(1)}, bf16[384,1024]{1,0:T(8,128)(2,1)S(1)}, u32[]{:S(2)}, u32[]{:S(2)}) collective-permute-start(bf16[384,1024]{1,0:T(8,128)(2,1)S(1)} %copy-done.9), channel_id=1, source_target_pairs={{0,128},{64,192},{128,0},{192,64},{256,384},{320,448},{384,256},{4... | collective-permute-start | bytes 2359304 | tf_op jit(solution)/shard_map/ppermute | solution.py:247
  173.4 1.1 copy-start.13

commit v2 on v1

--- a/solution.py
+++ b/solution.py
@@ -11,7 +11,7 @@
 BF16 = jnp.bfloat16
 F32 = jnp.float32
 
-HALF_PAIRS = [[i, i + N_X] for i in range(N_X)]
+HALF_SWAP = [(i, (i + N_X) % (N_X * N_HALF)) for i in range(N_X * N_HALF)]
 
 
 def x_shift(step):
@@ -63,9 +63,21 @@
     return row - 1.0, share
 
 
-def send_body(my_ref, pick_ref, weight_ref, tok_ref, cot_ref, out_ref):
+def send_body(
+    my_ref, pick_hbm, weight_hbm, tok_hbm, cot_hbm, out_ref, pick_ref, weight_ref, both_ref, sems
+):
+    tok_rows = tok_hbm.shape[0]
+    copies = [
+        pltpu.make_async_copy(pick_hbm, pick_ref, sems.at[0]),
+        pltpu.make_async_copy(weight_hbm, weight_ref, sems.at[1]),
+        pltpu.make_async_copy(tok_hbm, both_ref.at[:tok_rows], sems.at[2]),
+        pltpu.make_async_copy(cot_hbm, both_ref.at[tok_rows:], sems.at[3]),
+    ]
+    for copy in copies:
+        copy.start()
+    copies[0].wait()
+    copies[1].wait()
     n_experts = pick_ref.shape[0]
-    tok_rows = tok_ref.shape[0]
     row, share = slot_tables(my_ref[0], pick_ref[...], weight_ref[...], tok_rows)
     shape = (n_experts, 2 * SLOT, 2 * tok_rows)
     lane = lax.broadcasted_iota(jnp.int32, shape, 2).astype(F32)
@@ -74,20 +86,19 @@
     scale = jnp.where(second, share, 1.0)
     n_slots = n_experts * 2 * SLOT
     select = (lane == target).astype(F32).reshape(n_slots, 2 * tok_rows).astype(BF16)
-    both = jnp.concatenate([tok_ref[...], cot_ref[...]], axis=0)
-    rows = mm(select, both, 1, 0)
     scale = jnp.broadcast_to(scale, (n_experts, 2 * SLOT, 128)).reshape(n_slots, 128)
+    copies[2].wait()
+    copies[3].wait()
+    rows = mm(select, both_ref[...], 1, 0)
     for c in range(rows.shape[1] // 128):
         part = rows[:, c * 128 : (c + 1) * 128] * scale
         out_ref[:, c * 128 : (c + 1) * 128] = part.astype(BF16)
 
 
-def table_body(my_ref, pick_ref, weight_ref, place_ref, back_ref):
+def place_body(my_ref, pick_ref, place_ref):
     n_experts, cap = pick_ref.shape
-    my = my_ref[0]
-    n_slots = n_experts * 2 * SLOT
-    tok_rows = cap_rows = back_ref.shape[1] // 3
-    own = pick_ref[pl.ds(my, 1), :]
+    n_slots = n_experts * 2 * SLOT
+    own = pick_ref[pl.ds(my_ref[0], 1), :]
     source = lax.shift_right_logical(own, 7)
     from_dev = (
         lax.broadcasted_iota(jnp.int32, (n_experts, cap), 0)
@@ -100,7 +111,13 @@
     both = jnp.concatenate([position, position + SLOT], axis=1)
     sub = lax.broadcasted_iota(jnp.int32, (n_slots, 2 * cap), 0)
     place_ref[...] = (sub == jnp.broadcast_to(both, (n_slots, 2 * cap))).astype(F32).astype(BF16)
-    row, share = slot_tables(my, pick_ref[...], weight_ref[...], tok_rows)
+
+
+def back_body(my_ref, pick_ref, weight_ref, back_ref):
+    n_experts = pick_ref.shape[0]
+    n_slots = n_experts * 2 * SLOT
+    tok_rows = back_ref.shape[1] // 3
+    row, share = slot_tables(my_ref[0], pick_ref[...], weight_ref[...], tok_rows)
     shape = (n_experts, 2 * SLOT, tok_rows)
     lane = lax.broadcasted_iota(jnp.int32, shape, 2).astype(F32)
     second = lax.broadcasted_iota(jnp.int32, shape, 1) >= SLOT
@@ -120,37 +137,17 @@
         )
 
 
-def compact_body(place_ref, recv_ref, chosen_ref, weighted_ref):
-    rows = mm(place_ref[...], recv_ref[...], 0, 0).astype(BF16)
-    cap = chosen_ref.shape[0]
-    chosen_ref[...] = rows[:cap]
-    weighted_ref[...] = rows[cap:]
-
-
-def expert_body(
-    half_ref,
-    chosen_ref,
-    weighted_ref,
-    w0,
-    w1,
-    w2,
-    w3,
-    own_ref,
-    send_out_ref,
-    send_back_ref,
-    g_own,
-    g1,
-    g2,
-    g3,
-):
-    half = half_ref[0]
-    _, cap, feat = chosen_ref.shape
-    chosen = jnp.concatenate([chosen_ref[half], chosen_ref[1 - half]], axis=0)
-    weighted = jnp.concatenate([weighted_ref[half], weighted_ref[1 - half]], axis=0)
+def compact_body(place_ref, recv_ref, out_ref):
+    out_ref[...] = mm(place_ref[...], recv_ref[...], 0, 0).astype(BF16)
+
+
+def expert_body(rows_ref, w0, w1, w2, w3, part_ref, act_ref):
+    cap = rows_ref.shape[0] // 2
+    chosen, weighted = rows_ref[:cap], rows_ref[cap:]
     width = w0.shape[0] // 3
-    out = jnp.zeros((2 * cap, feat), F32)
-    back = jnp.zeros((2 * cap, feat), F32)
-    for w_ref, g_ref in ((w0, g_own), (w1, g1), (w2, g2), (w3, g3)):
+    out = jnp.zeros((cap, rows_ref.shape[1]), F32)
+    back = jnp.zeros((cap, rows_ref.shape[1]), F32)
+    for i, w_ref in enumerate((w0, w1, w2, w3)):
         pre = mm(chosen, w_ref[: 2 * width], 1, 1)
         d_hidden = mm(weighted, w_ref[2 * width :], 1, 1)
         gate, up = pre[:, :width], pre[:, width:]
@@ -162,18 +159,25 @@
         d_both = jnp.concatenate([d_gate, d_up], axis=1)
         out = out + mm(hidden, w_ref[2 * width :], 1, 0)
         back = back + mm(d_both, w_ref[: 2 * width], 1, 0)
-        g_ref[: 2 * width] = mm(d_both, chosen, 0, 0).astype(g_ref.dtype)
-        g_ref[2 * width :] = mm(hidden, weighted, 0, 0).astype(g_ref.dtype)
-    own_ref[:cap] = out[:cap]
-    own_ref[cap:] = back[:cap]
-    send_out_ref[...] = out[cap:].astype(BF16)
-    send_back_ref[...] = back[cap:].astype(BF16)
-
-
-def expand_body(half_ref, place_ref, own_ref, other_out_ref, other_back_ref, out_ref):
-    there = 1 - half_ref[0]
-    other = jnp.concatenate([other_out_ref[there], other_back_ref[there]], axis=0)
-    total = (own_ref[...] + other.astype(F32)).astype(BF16)
+        act_ref[i, :, : 2 * width] = d_both
+        act_ref[i, :, 2 * width :] = hidden
+    part_ref[:cap] = out.astype(part_ref.dtype)
+    part_ref[cap:] = back.astype(part_ref.dtype)
+
+
+def grads_body(rows_here, rows_there, act_here, act_there, g_own, g1, g2, g3):
+    cap = rows_here.shape[0] // 2
+    width = g_own.shape[0] // 3
+    chosen = jnp.concatenate([rows_here[:cap], rows_there[:cap]], axis=0)
+    weighted = jnp.concatenate([rows_here[cap:], rows_there[cap:]], axis=0)
+    for i, g_ref in ((3, g3), (1, g1), (2, g2), (0, g_own)):
+        act = jnp.concatenate([act_here[i], act_there[i]], axis=0)
+        g_ref[: 2 * width] = mm(act[:, : 2 * width], chosen, 0, 0).astype(g_ref.dtype)
+        g_ref[2 * width :] = mm(act[:, 2 * width :], weighted, 0, 0).astype(g_ref.dtype)
+
+
+def expand_body(place_ref, own_ref, other_ref, out_ref):
+    total = (own_ref[...] + other_ref[...].astype(F32)).astype(BF16)
     out_ref[...] = mm(place_ref[...], total, 1, 0).astype(BF16)
 
 
@@ -203,53 +207,56 @@
     width = w_gate.shape[1]
     n_slots = n_experts * 2 * SLOT
     my = lax.axis_index("expert").astype(jnp.int32).reshape(1)
-    half = (lax.axis_index("dp") // N_X).astype(jnp.int32).reshape(1)
     sds = jax.ShapeDtypeStruct
     picks, shares = pick_lists[0], combine[0]
+    row_pair = sds((2 * cap, feat), BF16)
+    slot_rows = sds((n_slots, feat), BF16)
 
     def exchange(rows):
         parts = rows.reshape(n_experts, 2 * SLOT, feat)
         out = lax.all_to_all(parts, "expert", split_axis=0, concat_axis=0, tiled=True)
         return out.reshape(n_slots, feat)
 
-    def pair_gather(rows):
-        return lax.all_gather(rows, "dp", axis_index_groups=HALF_PAIRS)
-
-    row_block = sds((cap, feat), BF16)
-    send = kernel_call(send_body, sds((n_slots, feat), BF16), 1, 4, 3 * 10**8, 2 * 10**6)(
-        my, picks, shares, tokens, cotangent
-    )
+    hbm = pl.BlockSpec(memory_space=pl.ANY)
+    send = pl.pallas_call(
+        send_body,
+        out_shape=slot_rows,
+        in_specs=[pl.BlockSpec(memory_space=pltpu.SMEM)] + [hbm] * 4,
+        out_specs=pl.BlockSpec(memory_space=pltpu.VMEM),
+        scratch_shapes=[
+            pltpu.VMEM(picks.shape, picks.dtype),
+            pltpu.VMEM(shares.shape, shares.dtype),
+            pltpu.VMEM((2 * tok_rows, feat), BF16),
+            pltpu.SemaphoreType.DMA((4,)),
+        ],
+        cost_estimate=pl.CostEstimate(flops=3 * 10**8, bytes_accessed=2 * 10**6, transcendentals=0),
+    )(my, picks, shares, tokens, cotangent)
     recv = exchange(send)
-    place, back_table = kernel_call(
-        table_body,
-        (sds((n_slots, 2 * cap), BF16), sds((n_slots, 3 * tok_rows), BF16)),
-        1,
-        2,
-        10**8,
-        10**6,
+    place = kernel_call(place_body, sds((n_slots, 2 * cap), BF16), 1, 1, 10**7, 10**6)(my, picks)
+    w_own = jnp.concatenate([w_gate[0], w_up[0], w_down[0]], axis=0)
+    w_all = [w_own] + [lax.ppermute(w_own, "dp", x_shift(s)) for s in (1, -1, 2)]
+    rows = kernel_call(compact_body, row_pair, 0, 2, 3 * 10**8, 2 * 10**6)(place, recv)
+    rows_there = lax.ppermute(rows, "dp", HALF_SWAP)
+    act = sds((len(w_all), cap, 3 * width), BF16)
+
+    def expert(rows_of_one, part):
+        return kernel_call(expert_body, (part, act), 0, 5, 10**9, 7 * 10**6)(rows_of_one, *w_all)
+
+    part_here, act_here = expert(rows, sds(row_pair.shape, F32))
+    part_there, act_there = expert(rows_there, row_pair)
+    part_back = lax.ppermute(part_there, "dp", HALF_SWAP)
+    g_shape = (3 * width, feat)
+    g_own, *g_others = kernel_call(
+        grads_body, (sds(g_shape, F32),) + (sds(g_shape, BF16),) * 3, 0, 4, 10**9, 6 * 10**6
+    )(rows, rows_there, act_here, act_there)
+    g_home = [lax.ppermute(g, "dp", x_shift(-s)) for g, s in zip(g_others, (1, -1, 2))]
+    slots = kernel_call(expand_body, slot_rows, 0, 3, 3 * 10**8, 4 * 10**6)(
+        place, part_here, part_back
+    )
+    returned = exchange(slots)
+    back_table = kernel_call(
+        back_body, sds((n_slots, 3 * tok_rows), BF16), 1, 2, 10**7, 10**6
     )(my, picks, shares)
-    w_own = jnp.concatenate([w_gate[0], w_up[0], w_down[0]], axis=0)
-    w_others = [lax.ppermute(w_own, "dp", x_shift(s)) for s in (1, -1, 2)]
-    chosen, weighted = kernel_call(
-        compact_body, (row_block, row_block), 0, 2, 3 * 10**8, 2 * 10**6
-    )(place, recv)
-    chosen, weighted = pair_gather(chosen), pair_gather(weighted)
-    g_shape = (3 * width, feat)
-    own_part, send_out, send_back, g_own, *g_others = kernel_call(
-        expert_body,
-        (sds((2 * cap, feat), F32), row_block, row_block, sds(g_shape, F32))
-        + (sds(g_shape, BF16),) * 3,
-        1,
-        6,
-        3 * 10**9,
-        10**7,
-    )(half, chosen, weighted, w_own, *w_others)
-    g_home = [lax.ppermute(g, "dp", x_shift(-s)) for g, s in zip(g_others, (1, -1, 2))]
-    other_out, other_back = pair_gather(send_out), pair_gather(send_back)
-    slots = kernel_call(expand_body, sds((n_slots, feat), BF16), 1, 4, 3 * 10**8, 4 * 10**6)(
-        half, place, own_part, other_out, other_back
-    )
-    returned = exchange(slots)
     layer_out, tokens_grad = kernel_call(
         combine_body, (sds((tok_rows, feat), BF16),) * 2, 0, 2, 4 * 10**8, 2 * 10**6
     )(back_table, returned)

time: 178 us -> 167 us (0.938)
  blocking collectives: 53.7 us -> 0 us
  starting transfers between devices: 54.1 us -> 79.5 us
  waiting for transfers between devices: 49.3 us -> 67.8 us
  local copies, waits for them, and re-layouts: 5.09 us -> 0.78 us
  Pallas kernels: 12.8 us -> 15.8 us
    all_gather x4 -> x0, blocking collectives: 53.7 us -> none  [pair_gather(): return lax.all_gather(rows, 'dp', axis_index_groups=HALF_PAIRS)]
    ppermute x3 -> x5, waiting for transfers between devices: 0.01 us -> 18.1 us  [the longest x1 10.9 us: per_device(): rows_there = lax.ppermute(rows, 'dp', HALF_SWAP)]
    ppermute x3 -> x5, starting transfers between devices: 9.94 us -> 24.9 us  [the longest x3 9.94 us: per_device(): lax.ppermute(w_own, 'dp', x_shift(s))]
    all_to_all x2, starting transfers between devices: 35.4 us -> 44.7 us  [exchange(): lax.all_to_all(parts, 'expert', split_axis=0, concat_axis=0, tiled=True)]
    unnamed x34 -> x22, local copies, waits for them, and re-layouts: 5.09 us -> 0.78 us
    pallas_call x5 -> x8, Pallas kernels: 10.3 us -> 13.3 us  [the longest x2 7.08 us: expert(): kernel_call(expert_body, (part, act), 0, 5, 10 ** 9, 7 * 10 ** 6)]
  transfers between devices with their start and end apart: 8 -> 10, of which waited for: 4 -> 8; matrix products, arithmetic and copies ran while one was open for 0% -> 0% of each run, Pallas kernels for 1% -> 4%
where the time goes in v2:
time: 167 us; the launch traced here: 165 us
  starting transfers between devices  79.5 us (48%)
  waiting for transfers between devices  67.8 us (41%)
  Pallas kernels  15.8 us (9%)
    all_to_all x2, starting transfers between devices, exchange(): lax.all_to_all(parts, 'expert', split_axis=0, concat_axis=0, tiled=True)  44.7 us
    ppermute x3, waiting for transfers between devices, per_device(): lax.ppermute(g, 'dp', x_shift(-s))  31.5 us
    all_to_all x2, waiting for transfers between devices, exchange(): lax.all_to_all(parts, 'expert', split_axis=0, concat_axis=0, tiled=True)  18.2 us
    ppermute x1, waiting for transfers between devices, per_device(): rows_there = lax.ppermute(rows, 'dp', HALF_SWAP)  10.9 us
    ppermute x3, starting transfers between devices, per_device(): lax.ppermute(g, 'dp', x_shift(-s))  9.94 us
    ppermute x3, starting transfers between devices, per_device(): lax.ppermute(w_own, 'dp', x_shift(s))  9.94 us
    ppermute x1, starting transfers between devices, per_device(): rows_there = lax.ppermute(rows, 'dp', HALF_SWAP)  7.94 us
    pallas_call x2, Pallas kernels, expert(): kernel_call(expert_body, (part, act), 0, 5, 10 ** 9, 7 * 10 ** 6)  7.08 us
  transfers between devices with their start and end apart: 10, of which 8 were waited for; matrix products, arithmetic and copies ran while one was open for 0% of the time, Pallas kernels for 4%

profile of v2, /device:TPU:1, one launch (start us, length us, event | category | flops | bytes accessed | tf_op | source)
XLA Modules:
  0.0 164.9 jit_solution(8386984212707571781)
XLA Ops:
  0.6 0.0 copy-start.8
  0.6 0.0 copy-start.9
  0.7 0.0 copy-start.10
  0.7 2.7 %shard_map.112 = bf16[512,1024]{1,0:T(8,128)(2,1)} custom-call(s32[1]{0:T(128)} %bitcast.my_ref, s32[64,128]{1,0:T(8,128)} %bitcast.15, f32[64,128]{1,0:T(8,128)} %bitcast.18, bf16[128,1024]{1,0:T(8,128)(2,1)} %tok_hbm.1, bf16[128,1024]{1,0:T(8,128)(2,1)} %cot_hbm.1), custom_call_target="tpu_custom_call" | custom-call | flops 300000000 | bytes 2000000 | tf_op jit(solution)/shard_map/pallas_call | solution.py:221
  3.4 0.0 copy-start
  3.4 14.6 %all-to-all-start = ((bf16[64,8,1024]{2,1,0:T(8,128)(2,1)}), bf16[64,8,1024]{2,1,0:T(8,128)(2,1)S(1)}, u32[]{:S(2)}, u32[]{:S(2)}) async-start(bf16[64,8,1024]{2,1,0:T(8,128)(2,1)} %bitcast.20), calls=%async_computation | async-start | bytes 2097152 | tf_op jit(solution)/shard_map/all_to_all | solution.py:217
  18.0 0.0 copy-done.8
  18.0 0.0 copy-done.9
  18.0 0.0 copy-done.10
  18.0 0.1 pad_maximum_fusion.w0
  18.1 4.7 %collective-permute-start.2 = (bf16[384,1024]{1,0:T(8,128)(2,1)S(1)}, bf16[384,1024]{1,0:T(8,128)(2,1)S(1)}, u32[]{:S(2)}, u32[]{:S(2)}) collective-permute-start(bf16[384,1024]{1,0:T(8,128)(2,1)S(1)} %pad_maximum_fusion.w0), channel_id=1, source_target_pairs={{0,128},{64,192},{128,0},{192,64},{256,384},{320,448},{384,256},{4... | collective-permute-start | bytes 2359304 | tf_op jit(solution)/shard_map/ppermute | solution.py:237
  22.7 2.8 %collective-permute-start.1 = (bf16[384,1024]{1,0:T(8,128)(2,1)S(1)}, bf16[384,1024]{1,0:T(8,128)(2,1)}, u32[]{:S(2)}, u32[]{:S(2)}) collective-permute-start(bf16[384,1024]{1,0:T(8,128)(2,1)S(1)} %pad_maximum_fusion.w0), channel_id=1, source_target_pairs={{0,192},{64,0},{128,64},{192,128},{256,448},{320,256},{384,320},{4... | collective-permute-start | bytes 2359304 | tf_op jit(solution)/shard_map/ppermute | solution.py:237
  25.5 2.5 %collective-permute-start = (bf16[384,1024]{1,0:T(8,128)(2,1)S(1)}, bf16[384,1024]{1,0:T(8,128)(2,1)}, u32[]{:S(2)}, u32[]{:S(2)}) collective-permute-start(bf16[384,1024]{1,0:T(8,128)(2,1)S(1)} %pad_maximum_fusion.w0), channel_id=1, source_target_pairs={{0,64},{64,128},{128,192},{192,0},{256,320},{320,384},{384,448},{4... | collective-permute-start | bytes 2359304 | tf_op jit(solution)/shard_map/ppermute | solution.py:237
  28.0 0.0 copy-done
  28.0 0.3 shard_map.111.place_ref
  28.3 18.2 %all-to-all-done = bf16[64,8,1024]{2,1,0:T(8,128)(2,1)S(1)} async-done(((bf16[64,8,1024]{2,1,0:T(8,128)(2,1)}), bf16[64,8,1024]{2,1,0:T(8,128)(2,1)S(1)}, u32[]{:S(2)}, u32[]{:S(2)}) %all-to-all-start) | async-done | bytes 1048608 | tf_op jit(solution)/shard_map/all_to_all | solution.py:217
  46.5 0.5 shard_map.113.rows_ref.rows_here
  47.0 7.9 %collective-permute-start.3 = (bf16[256,1024]{1,0:T(8,128)(2,1)S(1)}, bf16[256,1024]{1,0:T(8,128)(2,1)S(1)}, u32[]{:S(2)}, u32[]{:S(2)}) collective-permute-start(bf16[256,1024]{1,0:T(8,128)(2,1)S(1)} %shard_map.113.rows_ref.rows_here), channel_id=1, source_target_pairs={{0,256},{64,320},{128,384},{192,448},{256,0},{320,64},{384,128},{4... | collective-permute-start | bytes 1572872 | tf_op jit(solution)/shard_map/ppermute | solution.py:239
  54.9 0.0 collective-permute-done.2.w3
  54.9 2.3 %collective-permute-done.1.w2 = bf16[384,1024]{1,0:T(8,128)(2,1)} collective-permute-done((bf16[384,1024]{1,0:T(8,128)(2,1)S(1)}, bf16[384,1024]{1,0:T(8,128)(2,1)}, u32[]{:S(2)}, u32[]{:S(2)}) %collective-permute-start.1) | collective-permute-done | bytes 786464 | tf_op jit(solution)/shard_map/ppermute | solution.py:237
  57.2 0.7 collective-permute-done.w1
  57.9 10.9 %collective-permute-done.3.rows_ref.rows_there = bf16[256,1024]{1,0:T(8,128)(2,1)S(1)} collective-permute-done((bf16[256,1024]{1,0:T(8,128)(2,1)S(1)}, bf16[256,1024]{1,0:T(8,128)(2,1)S(1)}, u32[]{:S(2)}, u32[]{:S(2)}) %collective-permute-start.3) | collective-permute-done | bytes 524320 | tf_op jit(solution)/shard_map/ppermute | solution.py:239
  68.8 3.6 %shard_map.115 = (bf16[256,1024]{1,0:T(8,128)(2,1)S(1)}, bf16[4,128,384]{2,1,0:T(8,128)(2,1)S(1)}) custom-call(bf16[256,1024]{1,0:T(8,128)(2,1)S(1)} %collective-permute-done.3.rows_ref.rows_there, bf16[384,1024]{1,0:T(8,128)(2,1)S(1)} %pad_maximum_fusion.w0, bf16[384,1024]{1,0:T(8,128)(2,1)} %collective-permute-done.w1, ...), custom_call_target="tpu_custom_call" | custom-call | flops 1000000000 | bytes 7000000 | tf_op jit(solution)/shard_map/pallas_call | solution.py:243
  72.5 0.0 copy-done.2
  72.5 0.0 copy-start.4
  72.5 0.7 copy-done.4
  73.2 7.0 %collective-permute-start.4 = (bf16[256,1024]{1,0:T(8,128)(2,1)S(1)}, bf16[256,1024]{1,0:T(8,128)(2,1)S(1)}, u32[]{:S(2)}, u32[]{:S(2)}) collective-permute-start(bf16[256,1024]{1,0:T(8,128)(2,1)S(1)} %get-tuple-element.19), channel_id=1, source_target_pairs={{0,256},{64,320},{128,384},{192,448},{256,0},{320,64},{384,128},{4... | collective-permute-start | bytes 1572872 | tf_op jit(solution)/shard_map/ppermute | solution.py:247
  80.2 3.4 %shard_map.114 = (f32[256,1024]{1,0:T(8,128)S(1)}, bf16[4,128,384]{2,1,0:T(8,128)(2,1)S(1)}) custom-call(bf16[256,1024]{1,0:T(8,128)(2,1)S(1)} %shard_map.113.rows_ref.rows_here, bf16[384,1024]{1,0:T(8,128)(2,1)S(1)} %pad_maximum_fusion.w0, bf16[384,1024]{1,0:T(8,128)(2,1)} %collective-permute-done.w1, bf16[384,1024]{1,0:T(8,128)(2,1)} %collective-permute-done.1.w2, ...), custom_call_target="tpu_custom_call" | custom-call | flops 1000000000 | bytes 7000000 | tf_op jit(solution)/shard_map/pallas_call | solution.py:243
  83.7 0.0 copy-start.6
  83.7 4.2 %collective-permute-done.4.other_ref = bf16[256,1024]{1,0:T(8,128)(2,1)S(1)} collective-permute-done((bf16[256,1024]{1,0:T(8,128)(2,1)S(1)}, bf16[256,1024]{1,0:T(8,128)(2,1)S(1)}, u32[]{:S(2)}, u32[]{:S(2)}) %collective-permute-start.4) | collective-permute-done | bytes 524320 | tf_op jit(solution)/shard_map/ppermute | solution.py:247
  87.9 1.5 shard_map.116
  89.4 0.0 copy-done.6
  89.4 30.1 %all-to-all-start.1 = ((bf16[64,8,1024]{2,1,0:T(8,128)(2,1)}), bf16[64,8,1024]{2,1,0:T(8,128)(2,1)S(1)}, u32[]{:S(2)}, u32[]{:S(2)}) async-start(bf16[64,8,1024]{2,1,0:T(8,128)(2,1)} %bitcast.8), calls=%async_computation.1 | async-start | bytes 2097152 | tf_op jit(solution)/shard_map/all_to_all | solution.py:217
  119.5 0.0 copy-done.3
  119.5 0.0 copy-done.5
  119.5 0.0 copy-done.7
  119.5 0.0 copy-start.1
  119.5 1.0 shard_map.118
  120.5 4.4 %collective-permute-start.5 = (bf16[384,1024]{1,0:T(8,128)(2,1)S(1)}, bf16[384,1024]{1,0:T(8,128)(2,1)S(1)}, u32[]{:S(2)}, u32[]{:S(2)}) collective-permute-start(bf16[384,1024]{1,0:T(8,128)(2,1)S(1)} %get-tuple-element.25), channel_id=1, source_target_pairs={{0,192},{64,0},{128,64},{192,128},{256,448},{320,256},{384,320},{4... | collective-permute-start | bytes 2359304 | tf_op jit(solution)/shard_map/ppermute | solution.py:252
  124.9 1.9 %collective-permute-start.6 = (bf16[384,1024]{1,0:T(8,128)(2,1)S(1)}, bf16[384,1024]{1,0:T(8,128)(2,1)S(1)}, u32[]{:S(2)}, u32[]{:S(2)}) collective-permute-start(bf16[384,1024]{1,0:T(8,128)(2,1)S(1)} %get-tuple-element.26), channel_id=1, source_target_pairs={{0,64},{64,128},{128,192},{192,0},{256,320},{320,384},{384,448},{4... | collective-permute-start | bytes 2359304 | tf_op jit(solution)/shard_map/ppermute | solution.py:252
  126.8 3.6 %collective-permute-start.7 = (bf16[384,1024]{1,0:T(8,128)(2,1)S(1)}, bf16[384,1024]{1,0:T(8,128)(2,1)S(1)}, u32[]{:S(2)}, u32[]{:S(2)}) collective-permute-start(bf16[384,1024]{1,0:T(8,128)(2,1)S(1)} %get-tuple-element.27), channel_id=1, source_target_pairs={{0,128},{64,192},{128,0},{192,64},{256,384},{320,448},{384,256},{4... | collective-permute-start | bytes 2359304 | tf_op jit(solution)/shard_map/ppermute | solution.py:252
  130.5 0.4 shard_map.110.back_ref
  130.9 11.2 %collective-permute-done.5.g1 = bf16[384,1024]{1,0:T(8,128)(2,1)S(1)} collective-permute-done((bf16[384,1024]{1,0:T(8,128)(2,1)S(1)}, bf16[384,1024]{1,0:T(8,128)(2,1)S(1)}, u32[]{:S(2)}, u32[]{:S(2)}) %collective-permute-start.5) | collective-permute-done | bytes 786464 | tf_op jit(solution)/shard_map/ppermute | solution.py:252
  142.1 5.2 %collective-permute-done.6.g2 = bf16[384,1024]{1,0:T(8,128)(2,1)S(1)} collective-permute-done((bf16[384,1024]{1,0:T(8,128)(2,1)S(1)}, bf16[384,1024]{1,0:T(8,128)(2,1)S(1)}, u32[]{:S(2)}, u32[]{:S(2)}) %collective-permute-start.6) | collective-permute-done | bytes 786464 | tf_op jit(solution)/shard_map/ppermute | solution.py:252
  147.3 15.0 %collective-permute-done.7.g3 = bf16[384,1024]{1,0:T(8,128)(2,1)S(1)} collective-permute-done((bf16[384,1024]{1,0:T(8,128)(2,1)S(1)}, bf16[384,1024]{1,0:T(8,128)(2,1)S(1)}, u32[]{:S(2)}, u32[]{:S(2)}) %collective-permute-start.7) | collective-permute-done | bytes 786464 | tf_op jit(solution)/shard_map/ppermute | solution.py:252
  162.4 1.1 shard_map.119
  163.5 0.0 all-to-all-done.1
  163.5 1.4 shard_map.117
  (5 shorter events, 0.0 us)
Async XLA Ops:
  0.6 17.3 %copy-start.8 = (bf16[1,128,1024]{2,1,0:T(8,128)(2,1)S(1)}, bf16[1,128,1024]{2,1,0:T(8,128)(2,1)}, u32[]{:S(2)}) copy-start(bf16[1,128,1024]{2,1,0:T(8,128)(2,1)} %param.13) | copy-start | bytes 786436
  0.6 17.3 %copy-start.9 = (bf16[1,128,1024]{2,1,0:T(8,128)(2,1)S(1)}, bf16[1,128,1024]{2,1,0:T(8,128)(2,1)}, u32[]{:S(2)}) copy-start(bf16[1,128,1024]{2,1,0:T(8,128)(2,1)} %param.12) | copy-start | bytes 786436
  0.7 17.3 %copy-start.10 = (bf16[1,128,1024]{2,1,0:T(8,128)(2,1)S(1)}, bf16[1,128,1024]{2,1,0:T(8,128)(2,1)}, u32[]{:S(2)}) copy-start(bf16[1,128,1024]{2,1,0:T(8,128)(2,1)} %param.11) | copy-start | bytes 786436
  3.4 24.7 %copy-start = (s32[1,64,128]{2,1,0:T(8,128)S(1)}, s32[1,64,128]{2,1,0:T(8,128)}, u32[]{:S(2)}) copy-start(s32[1,64,128]{2,1,0:T(8,128)} %param.9) | copy-start | bytes 98308
  3.4 43.1 %all-to-all-start = ((bf16[64,8,1024]{2,1,0:T(8,128)(2,1)}), bf16[64,8,1024]{2,1,0:T(8,128)(2,1)S(1)}, u32[]{:S(2)}, u32[]{:S(2)}) async-start(bf16[64,8,1024]{2,1,0:T(8,128)(2,1)} %bitcast.20), calls=%async_computation | async-start | bytes 2097152 | tf_op jit(solution)/shard_map/all_to_all | solution.py:217
  18.1 36.9 %collective-permute-start.2 = (bf16[384,1024]{1,0:T(8,128)(2,1)S(1)}, bf16[384,1024]{1,0:T(8,128)(2,1)S(1)}, u32[]{:S(2)}, u32[]{:S(2)}) collective-permute-start(bf16[384,1024]{1,0:T(8,128)(2,1)S(1)} %pad_maximum_fusion.w0), channel_id=1, source_target_pairs={{0,128},{64,192},{128,0},{192,64},{256,384},{320,448},{384,256},{4... | collective-permute-start | bytes 2359304 | tf_op jit(solution)/shard_map/ppermute | solution.py:237
  22.7 34.5 %collective-permute-start.1 = (bf16[384,1024]{1,0:T(8,128)(2,1)S(1)}, bf16[384,1024]{1,0:T(8,128)(2,1)}, u32[]{:S(2)}, u32[]{:S(2)}) collective-permute-start(bf16[384,1024]{1,0:T(8,128)(2,1)S(1)} %pad_maximum_fusion.w0), channel_id=1, source_target_pairs={{0,192},{64,0},{128,64},{192,128},{256,448},{320,256},{384,320},{4... | collective-permute-start | bytes 2359304 | tf_op jit(solution)/shard_map/ppermute | solution.py:237
  25.5 32.4 %collective-permute-start = (bf16[384,1024]{1,0:T(8,128)(2,1)S(1)}, bf16[384,1024]{1,0:T(8,128)(2,1)}, u32[]{:S(2)}, u32[]{:S(2)}) collective-permute-start(bf16[384,1024]{1,0:T(8,128)(2,1)S(1)} %pad_maximum_fusion.w0), channel_id=1, source_target_pairs={{0,64},{64,128},{128,192},{192,0},{256,320},{320,384},{384,448},{4... | collective-permute-start | bytes 2359304 | tf_op jit(solution)/shard_map/ppermute | solution.py:237
  47.0 21.8 %collective-permute-start.3 = (bf16[256,1024]{1,0:T(8,128)(2,1)S(1)}, bf16[256,1024]{1,0:T(8,128)(2,1)S(1)}, u32[]{:S(2)}, u32[]{:S(2)}) collective-permute-start(bf16[256,1024]{1,0:T(8,128)(2,1)S(1)} %shard_map.113.rows_ref.rows_here), channel_id=1, source_target_pairs={{0,256},{64,320},{128,384},{192,448},{256,0},{320,64},{384,128},{4... | collective-permute-start | bytes 1572872 | tf_op jit(solution)/shard_map/ppermute | solution.py:239
  68.8 3.6 %copy-start.2 = (bf16[256,1024]{1,0:T(8,128)(2,1)}, bf16[256,1024]{1,0:T(8,128)(2,1)S(1)}, u32[]{:S(2)}) copy-start(bf16[256,1024]{1,0:T(8,128)(2,1)S(1)} %collective-permute-done.3.rows_ref.rows_there) | copy-start | bytes 1572868
  72.5 0.7 copy-start.4
  73.2 14.7 %collective-permute-start.4 = (bf16[256,1024]{1,0:T(8,128)(2,1)S(1)}, bf16[256,1024]{1,0:T(8,128)(2,1)S(1)}, u32[]{:S(2)}, u32[]{:S(2)}) collective-permute-start(bf16[256,1024]{1,0:T(8,128)(2,1)S(1)} %get-tuple-element.19), channel_id=1, source_target_pairs={{0,256},{64,320},{128,384},{192,448},{256,0},{320,64},{384,128},{4... | collective-permute-start | bytes 1572872 | tf_op jit(solution)/shard_map/ppermute | solution.py:247
  83.7 5.7 %copy-start.6 = (bf16[4,128,384]{2,1,0:T(8,128)(2,1)}, bf16[4,128,384]{2,1,0:T(8,128)(2,1)S(1)}, u32[]{:S(2)}) copy-start(bf16[4,128,384]{2,1,0:T(8,128)(2,1)S(1)} %get-tuple-element.22.act_here) | copy-start | bytes 1179652
  89.4 30.1 %copy-start.3 = (bf16[256,1024]{1,0:T(8,128)(2,1)S(1)}, bf16[256,1024]{1,0:T(8,128)(2,1)}, u32[]{:S(2)}) copy-start(bf16[256,1024]{1,0:T(8,128)(2,1)} %copy-done.2) | copy-start | bytes 1572868
  89.4 30.1 %copy-start.5 = (bf16[4,128,384]{2,1,0:T(8,128)(2,1)S(1)}, bf16[4,128,384]{2,1,0:T(8,128)(2,1)}, u32[]{:S(2)}) copy-start(bf16[4,128,384]{2,1,0:T(8,128)(2,1)} %copy-done.4) | copy-start | bytes 1179652
  89.4 30.1 %copy-start.7 = (bf16[4,128,384]{2,1,0:T(8,128)(2,1)S(1)}, bf16[4,128,384]{2,1,0:T(8,128)(2,1)}, u32[]{:S(2)}) copy-start(bf16[4,128,384]{2,1,0:T(8,128)(2,1)} %copy-done.6) | copy-start | bytes 1179652
  89.4 74.1 %all-to-all-start.1 = ((bf16[64,8,1024]{2,1,0:T(8,128)(2,1)}), bf16[64,8,1024]{2,1,0:T(8,128)(2,1)S(1)}, u32[]{:S(2)}, u32[]{:S(2)}) async-start(bf16[64,8,1024]{2,1,0:T(8,128)(2,1)} %bitcast.8), calls=%async_computation.1 | async-start | bytes 2097152 | tf_op jit(solution)/shard_map/all_to_all | solution.py:217
  119.5 11.0 %copy-start.1 = (f32[1,64,128]{2,1,0:T(8,128)S(1)}, f32[1,64,128]{2,1,0:T(8,128)}, u32[]{:S(2)}) copy-start(f32[1,64,128]{2,1,0:T(8,128)} %param.10) | copy-start | bytes 98308
  120.5 21.6 %collective-permute-start.5 = (bf16[384,1024]{1,0:T(8,128)(2,1)S(1)}, bf16[384,1024]{1,0:T(8,128)(2,1)S(1)}, u32[]{:S(2)}, u32[]{:S(2)}) collective-permute-start(bf16[384,1024]{1,0:T(8,128)(2,1)S(1)} %get-tuple-element.25), channel_id=1, source_target_pairs={{0,192},{64,0},{128,64},{192,128},{256,448},{320,256},{384,320},{4... | collective-permute-start | bytes 2359304 | tf_op jit(solution)/shard_map/ppermute | solution.py:252
  124.9 22.4 %collective-permute-start.6 = (bf16[384,1024]{1,0:T(8,128)(2,1)S(1)}, bf16[384,1024]{1,0:T(8,128)(2,1)S(1)}, u32[]{:S(2)}, u32[]{:S(2)}) collective-permute-start(bf16[384,1024]{1,0:T(8,128)(2,1)S(1)} %get-tuple-element.26), channel_id=1, source_target_pairs={{0,64},{64,128},{128,192},{192,0},{256,320},{320,384},{384,448},{4... | collective-permute-start | bytes 2359304 | tf_op jit(solution)/shard_map/ppermute | solution.py:252
  126.8 35.5 %collective-permute-start.7 = (bf16[384,1024]{1,0:T(8,128)(2,1)S(1)}, bf16[384,1024]{1,0:T(8,128)(2,1)S(1)}, u32[]{:S(2)}, u32[]{:S(2)}) collective-permute-start(bf16[384,1024]{1,0:T(8,128)(2,1)S(1)} %get-tuple-element.27), channel_id=1, source_target_pairs={{0,128},{64,192},{128,0},{192,64},{256,384},{320,448},{384,256},{4... | collective-permute-start | bytes 2359304 | tf_op jit(solution)/shard_map/ppermute | solution.py:252

commit v3 on v2

--- a/solution.py
+++ b/solution.py
@@ -1,3 +1,5 @@
+import functools
+
 import jax
 import jax.numpy as jnp
 from jax import lax
@@ -7,6 +9,7 @@
 
 N_X = 4
 N_HALF = 2
+CHUNKS = 2
 SLOT = 4
 BF16 = jnp.bfloat16
 F32 = jnp.float32
@@ -34,7 +37,7 @@
         + [pl.BlockSpec(memory_space=pltpu.VMEM)] * n_vmem,
         out_specs=jax.tree.map(lambda _: pl.BlockSpec(memory_space=pltpu.VMEM), out_shapes),
         cost_estimate=pl.CostEstimate(flops=flops, bytes_accessed=nbytes, transcendentals=0),
-        compiler_params=pltpu.CompilerParams(vmem_limit_bytes=48 * 1024 * 1024),
+        compiler_params=pltpu.CompilerParams(vmem_limit_bytes=24 * 1024 * 1024),
     )
 
 
@@ -137,17 +140,30 @@
         )
 
 
-def compact_body(place_ref, recv_ref, out_ref):
-    out_ref[...] = mm(place_ref[...], recv_ref[...], 0, 0).astype(BF16)
-
-
-def expert_body(rows_ref, w0, w1, w2, w3, part_ref, act_ref):
-    cap = rows_ref.shape[0] // 2
-    chosen, weighted = rows_ref[:cap], rows_ref[cap:]
-    width = w0.shape[0] // 3
-    out = jnp.zeros((cap, rows_ref.shape[1]), F32)
-    back = jnp.zeros((cap, rows_ref.shape[1]), F32)
-    for i, w_ref in enumerate((w0, w1, w2, w3)):
+def chunk_rows(refs):
+    n = refs[0].shape[0] // 2
+    return (
+        jnp.concatenate([ref[:n] for ref in refs], axis=0),
+        jnp.concatenate([ref[n:] for ref in refs], axis=0),
+    )
+
+
+def compact_body(place_ref, recv_ref, *chunk_refs):
+    rows = mm(place_ref[...], recv_ref[...], 0, 0).astype(BF16)
+    n = chunk_refs[0].shape[0] // 2
+    for c, ref in enumerate(chunk_refs):
+        ref[:n] = rows[c * n : (c + 1) * n]
+        ref[n:] = rows[(c + len(chunk_refs)) * n : (c + len(chunk_refs) + 1) * n]
+
+
+def expert_body(n_chunks, *refs):
+    chunks, w_refs, (part_ref, act_ref) = refs[:n_chunks], refs[n_chunks:-2], refs[-2:]
+    chosen, weighted = chunk_rows(chunks)
+    n = chosen.shape[0]
+    width = w_refs[0].shape[0] // 3
+    out = jnp.zeros(chosen.shape, F32)
+    back = jnp.zeros(chosen.shape, F32)
+    for i, w_ref in enumerate(w_refs):
         pre = mm(chosen, w_ref[: 2 * width], 1, 1)
         d_hidden = mm(weighted, w_ref[2 * width :], 1, 1)
         gate, up = pre[:, :width], pre[:, width:]
@@ -161,24 +177,26 @@
         back = back + mm(d_both, w_ref[: 2 * width], 1, 0)
         act_ref[i, :, : 2 * width] = d_both
         act_ref[i, :, 2 * width :] = hidden
-    part_ref[:cap] = out.astype(part_ref.dtype)
-    part_ref[cap:] = back.astype(part_ref.dtype)
-
-
-def grads_body(rows_here, rows_there, act_here, act_there, g_own, g1, g2, g3):
-    cap = rows_here.shape[0] // 2
+    part_ref[:n] = out.astype(part_ref.dtype)
+    part_ref[n:] = back.astype(part_ref.dtype)
+
+
+def grads_body(n_chunks, *refs):
+    chunks = refs[: 2 * n_chunks]
+    acts = refs[2 * n_chunks : 3 * n_chunks + 1]
+    g_own, g1, g2, g3 = refs[3 * n_chunks + 1 :]
     width = g_own.shape[0] // 3
-    chosen = jnp.concatenate([rows_here[:cap], rows_there[:cap]], axis=0)
-    weighted = jnp.concatenate([rows_here[cap:], rows_there[cap:]], axis=0)
+    chosen, weighted = chunk_rows(chunks)
     for i, g_ref in ((3, g3), (1, g1), (2, g2), (0, g_own)):
-        act = jnp.concatenate([act_here[i], act_there[i]], axis=0)
+        act = jnp.concatenate([ref[i] for ref in acts], axis=0)
         g_ref[: 2 * width] = mm(act[:, : 2 * width], chosen, 0, 0).astype(g_ref.dtype)
         g_ref[2 * width :] = mm(act[:, 2 * width :], weighted, 0, 0).astype(g_ref.dtype)
 
 
-def expand_body(place_ref, own_ref, other_ref, out_ref):
-    total = (own_ref[...] + other_ref[...].astype(F32)).astype(BF16)
-    out_ref[...] = mm(place_ref[...], total, 1, 0).astype(BF16)
+def expand_body(place_ref, own_ref, *refs):
+    other = jnp.concatenate(chunk_rows(refs[:-1]), axis=0)
+    total = (own_ref[...] + other.astype(F32)).astype(BF16)
+    refs[-1][...] = mm(place_ref[...], total, 1, 0).astype(BF16)
 
 
 def combine_body(back_ref, slots_ref, layer_ref, grad_ref):
@@ -209,7 +227,6 @@
     my = lax.axis_index("expert").astype(jnp.int32).reshape(1)
     sds = jax.ShapeDtypeStruct
     picks, shares = pick_lists[0], combine[0]
-    row_pair = sds((2 * cap, feat), BF16)
     slot_rows = sds((n_slots, feat), BF16)
 
     def exchange(rows):
@@ -235,23 +252,38 @@
     place = kernel_call(place_body, sds((n_slots, 2 * cap), BF16), 1, 1, 10**7, 10**6)(my, picks)
     w_own = jnp.concatenate([w_gate[0], w_up[0], w_down[0]], axis=0)
     w_all = [w_own] + [lax.ppermute(w_own, "dp", x_shift(s)) for s in (1, -1, 2)]
-    rows = kernel_call(compact_body, row_pair, 0, 2, 3 * 10**8, 2 * 10**6)(place, recv)
-    rows_there = lax.ppermute(rows, "dp", HALF_SWAP)
-    act = sds((len(w_all), cap, 3 * width), BF16)
-
-    def expert(rows_of_one, part):
-        return kernel_call(expert_body, (part, act), 0, 5, 10**9, 7 * 10**6)(rows_of_one, *w_all)
-
-    part_here, act_here = expert(rows, sds(row_pair.shape, F32))
-    part_there, act_there = expert(rows_there, row_pair)
-    part_back = lax.ppermute(part_there, "dp", HALF_SWAP)
+    chunk = sds((2 * cap // CHUNKS, feat), BF16)
+    rows = kernel_call(compact_body, (chunk,) * CHUNKS, 0, 2, 3 * 10**8, 2 * 10**6)(
+        place, recv
+    )
+
+    def expert(chunks, dtype):
+        n_rows = sum(c.shape[0] for c in chunks)
+        outs = (sds((n_rows, feat), dtype), sds((len(w_all), n_rows // 2, 3 * width), BF16))
+        body = functools.partial(expert_body, len(chunks))
+        n_in = len(chunks) + len(w_all)
+        return kernel_call(body, outs, 0, n_in, 10**9, 6 * 10**6)(*chunks, *w_all)
+
+    rows_there, acts_there, parts_back = [], [], []
+    for c in range(CHUNKS):
+        rows_there.append(lax.ppermute(rows[c], "dp", HALF_SWAP))
+    part_here, act_here = expert(rows, F32)
+    for c in range(CHUNKS):
+        part_there, act_there = expert(rows_there[c : c + 1], BF16)
+        acts_there.append(act_there)
+        parts_back.append(lax.ppermute(part_there, "dp", HALF_SWAP))
     g_shape = (3 * width, feat)
     g_own, *g_others = kernel_call(
-        grads_body, (sds(g_shape, F32),) + (sds(g_shape, BF16),) * 3, 0, 4, 10**9, 6 * 10**6
-    )(rows, rows_there, act_here, act_there)
+        functools.partial(grads_body, CHUNKS),
+        (sds(g_shape, F32),) + (sds(g_shape, BF16),) * 3,
+        0,
+        3 * CHUNKS + 1,
+        10**9,
+        6 * 10**6,
+    )(*rows, *rows_there, act_here, *acts_there)
     g_home = [lax.ppermute(g, "dp", x_shift(-s)) for g, s in zip(g_others, (1, -1, 2))]
-    slots = kernel_call(expand_body, slot_rows, 0, 3, 3 * 10**8, 4 * 10**6)(
-        place, part_here, part_back
+    slots = kernel_call(expand_body, slot_rows, 0, 2 + CHUNKS, 3 * 10**8, 4 * 10**6)(
+        place, part_here, *parts_back
     )
     returned = exchange(slots)
     back_table = kernel_call(

time: 167 us -> 160 us (0.958)
  waiting for transfers between devices: 67.8 us -> 60.8 us
  starting transfers between devices: 79.5 us -> 75.5 us
  Pallas kernels: 15.8 us -> 19.1 us
    all_to_all x2, starting transfers between devices: 44.7 us -> 35.6 us  [exchange(): lax.all_to_all(parts, 'expert', split_axis=0, concat_axis=0, tiled=True)]
    ppermute x2 -> x4, starting transfers between devices: 15 us -> 20.3 us  [the longest x2 10.5 us: per_device(): parts_back.append(lax.ppermute(part_there, 'dp', HALF_SWAP))]
    ppermute x2 -> x4, waiting for transfers between devices: 15.1 us -> 10.1 us  [the longest x2 6.01 us: per_device(): parts_back.append(lax.ppermute(part_there, 'dp', HALF_SWAP))]
    pallas_call x5 -> x6, Pallas kernels: 10 us -> 13.4 us  [the longest x3 10.4 us: expert(): kernel_call(body, outs, 0, n_in, 10 ** 9, 6 * 10 ** 6)(*chunks, *w_all)]
    ppermute x3, waiting for transfers between devices: 2.94 us -> 1.01 us  [per_device(): lax.ppermute(w_own, 'dp', x_shift(s))]
  transfers between devices with their start and end apart: 10 -> 12, of which waited for: 8 -> 9; matrix products, arithmetic and copies ran while one was open for 0% -> 0% of each run, Pallas kernels for 4% -> 9%
where the time goes in v3:
time: 160 us; the launch traced here: 158 us
  starting transfers between devices  75.5 us (47%)
  waiting for transfers between devices  60.8 us (38%)
  Pallas kernels  19.1 us (12%)
    all_to_all x2, starting transfers between devices, exchange(): lax.all_to_all(parts, 'expert', split_axis=0, concat_axis=0, tiled=True)  35.6 us
    ppermute x3, waiting for transfers between devices, per_device(): lax.ppermute(g, 'dp', x_shift(-s))  31.5 us
    all_to_all x2, waiting for transfers between devices, exchange(): lax.all_to_all(parts, 'expert', split_axis=0, concat_axis=0, tiled=True)  18.2 us
    ppermute x2, starting transfers between devices, per_device(): parts_back.append(lax.ppermute(part_there, 'dp', HALF_SWAP))  10.5 us
    pallas_call x3, Pallas kernels, expert(): kernel_call(body, outs, 0, n_in, 10 ** 9, 6 * 10 ** 6)(*chunks, *w_all)  10.4 us
    ppermute x3, starting transfers between devices, per_device(): lax.ppermute(w_own, 'dp', x_shift(s))  9.94 us
    ppermute x2, starting transfers between devices, per_device(): rows_there.append(lax.ppermute(rows[c], 'dp', HALF_SWAP))  9.86 us
    ppermute x3, starting transfers between devices, per_device(): lax.ppermute(g, 'dp', x_shift(-s))  9.72 us
  transfers between devices with their start and end apart: 12, of which 9 were waited for; matrix products, arithmetic and copies ran while one was open for 0% of the time, Pallas kernels for 9%

profile of v3, /device:TPU:1, one launch (start us, length us, event | category | flops | bytes accessed | tf_op | source)
XLA Modules:
  0.0 157.9 jit_solution(7001343852049936743)
XLA Ops:
  0.6 0.0 copy-start.12
  0.6 0.0 copy-start.13
  0.7 0.0 copy-start.14
  0.7 2.7 %shard_map.112 = bf16[512,1024]{1,0:T(8,128)(2,1)} custom-call(s32[1]{0:T(128)} %bitcast.my_ref, s32[64,128]{1,0:T(8,128)} %bitcast.15, f32[64,128]{1,0:T(8,128)} %bitcast.18, bf16[128,1024]{1,0:T(8,128)(2,1)} %tok_hbm.1, bf16[128,1024]{1,0:T(8,128)(2,1)} %cot_hbm.1), custom_call_target="tpu_custom_call" | custom-call | flops 300000000 | bytes 2000000 | tf_op jit(solution)/shard_map/pallas_call | solution.py:238
  3.3 0.0 copy-start
  3.3 14.6 %all-to-all-start = ((bf16[64,8,1024]{2,1,0:T(8,128)(2,1)}), bf16[64,8,1024]{2,1,0:T(8,128)(2,1)S(1)}, u32[]{:S(2)}, u32[]{:S(2)}) async-start(bf16[64,8,1024]{2,1,0:T(8,128)(2,1)} %bitcast.20), calls=%async_computation | async-start | bytes 2097152 | tf_op jit(solution)/shard_map/all_to_all | solution.py:234
  18.0 0.1 pad_maximum_fusion.refs_2_.refs_1_
  18.0 4.7 %collective-permute-start.2 = (bf16[384,1024]{1,0:T(8,128)(2,1)S(1)}, bf16[384,1024]{1,0:T(8,128)(2,1)S(1)}, u32[]{:S(2)}, u32[]{:S(2)}) collective-permute-start(bf16[384,1024]{1,0:T(8,128)(2,1)S(1)} %pad_maximum_fusion.refs_2_.refs_1_), channel_id=1, source_target_pairs={{0,128},{64,192},{128,0},{192,64},{256,384},{320,448},{384,256},{4... | collective-permute-start | bytes 2359304 | tf_op jit(solution)/shard_map/ppermute | solution.py:254
  22.7 2.8 %collective-permute-start.1 = (bf16[384,1024]{1,0:T(8,128)(2,1)S(1)}, bf16[384,1024]{1,0:T(8,128)(2,1)}, u32[]{:S(2)}, u32[]{:S(2)}) collective-permute-start(bf16[384,1024]{1,0:T(8,128)(2,1)S(1)} %pad_maximum_fusion.refs_2_.refs_1_), channel_id=1, source_target_pairs={{0,192},{64,0},{128,64},{192,128},{256,448},{320,256},{384,320},{4... | collective-permute-start | bytes 2359304 | tf_op jit(solution)/shard_map/ppermute | solution.py:254
  25.5 2.5 %collective-permute-start = (bf16[384,1024]{1,0:T(8,128)(2,1)S(1)}, bf16[384,1024]{1,0:T(8,128)(2,1)}, u32[]{:S(2)}, u32[]{:S(2)}) collective-permute-start(bf16[384,1024]{1,0:T(8,128)(2,1)S(1)} %pad_maximum_fusion.refs_2_.refs_1_), channel_id=1, source_target_pairs={{0,64},{64,128},{128,192},{192,0},{256,320},{320,384},{384,448},{4... | collective-permute-start | bytes 2359304 | tf_op jit(solution)/shard_map/ppermute | solution.py:254
  28.0 0.0 copy-done
  28.0 0.3 shard_map.111.place_ref
  28.3 18.2 %all-to-all-done = bf16[64,8,1024]{2,1,0:T(8,128)(2,1)S(1)} async-done(((bf16[64,8,1024]{2,1,0:T(8,128)(2,1)}), bf16[64,8,1024]{2,1,0:T(8,128)(2,1)S(1)}, u32[]{:S(2)}, u32[]{:S(2)}) %all-to-all-start) | async-done | bytes 1048608 | tf_op jit(solution)/shard_map/all_to_all | solution.py:234
  46.5 0.5 shard_map.113
  47.0 7.9 %collective-permute-start.5 = (bf16[128,1024]{1,0:T(8,128)(2,1)S(1)}, bf16[128,1024]{1,0:T(8,128)(2,1)S(1)}, u32[]{:S(2)}, u32[]{:S(2)}) collective-permute-start(bf16[128,1024]{1,0:T(8,128)(2,1)S(1)} %get-tuple-element.23.refs_1_), channel_id=1, source_target_pairs={{0,256},{64,320},{128,384},{192,448},{256,0},{320,64},{384,128},{4... | collective-permute-start | bytes 786440 | tf_op jit(solution)/shard_map/ppermute | solution.py:269
  54.9 1.9 %collective-permute-start.3 = (bf16[128,1024]{1,0:T(8,128)(2,1)S(1)}, bf16[128,1024]{1,0:T(8,128)(2,1)S(1)}, u32[]{:S(2)}, u32[]{:S(2)}) collective-permute-start(bf16[128,1024]{1,0:T(8,128)(2,1)S(1)} %get-tuple-element.22.refs_0_), channel_id=1, source_target_pairs={{0,256},{64,320},{128,384},{192,448},{256,0},{320,64},{384,128},{4... | collective-permute-start | bytes 786440 | tf_op jit(solution)/shard_map/ppermute | solution.py:269
  56.8 0.0 collective-permute-done.2.refs_5_.refs_4_
  56.8 0.3 collective-permute-done.1.refs_4_.refs_3_
  57.2 0.7 collective-permute-done.refs_3_.refs_2_
  57.9 4.0 %collective-permute-done.5.refs_0_.refs_3_ = bf16[128,1024]{1,0:T(8,128)(2,1)S(1)} collective-permute-done((bf16[128,1024]{1,0:T(8,128)(2,1)S(1)}, bf16[128,1024]{1,0:T(8,128)(2,1)S(1)}, u32[]{:S(2)}, u32[]{:S(2)}) %collective-permute-start.5) | collective-permute-done | bytes 262176 | tf_op jit(solution)/shard_map/ppermute | solution.py:269
  61.9 3.5 %shard_map.116 = (bf16[128,1024]{1,0:T(8,128)(2,1)S(1)}, bf16[4,64,384]{2,1,0:T(8,128)(2,1)S(1)}) custom-call(bf16[128,1024]{1,0:T(8,128)(2,1)S(1)} %collective-permute-done.5.refs_0_.refs_3_, bf16[384,1024]{1,0:T(8,128)(2,1)S(1)} %pad_maximum_fusion.refs_2_.refs_1_, bf16[384,1024]{1,0:T(8,128)(2,1)} %collective-permute-done.refs_3_.refs_2_, ...), custom_call_target="tpu_custom_call" | custom-call | flops 1000000000 | bytes 6000000 | tf_op jit(solution)/shard_map/pallas_call | solution.py:265
  65.4 0.0 copy-start.8
  65.4 0.7 copy-done.8
  66.1 7.0 %collective-permute-start.6 = (bf16[128,1024]{1,0:T(8,128)(2,1)S(1)}, bf16[128,1024]{1,0:T(8,128)(2,1)S(1)}, u32[]{:S(2)}, u32[]{:S(2)}) collective-permute-start(bf16[128,1024]{1,0:T(8,128)(2,1)S(1)} %get-tuple-element.26), channel_id=1, source_target_pairs={{0,256},{64,320},{128,384},{192,448},{256,0},{320,64},{384,128},{4... | collective-permute-start | bytes 786440 | tf_op jit(solution)/shard_map/ppermute | solution.py:274
  73.1 0.0 collective-permute-done.3.refs_0_.refs_2_
  73.2 0.0 copy-start.4
  73.2 3.5 %shard_map.115 = (bf16[128,1024]{1,0:T(8,128)(2,1)S(1)}, bf16[4,64,384]{2,1,0:T(8,128)(2,1)S(1)}) custom-call(bf16[128,1024]{1,0:T(8,128)(2,1)S(1)} %collective-permute-done.3.refs_0_.refs_2_, bf16[384,1024]{1,0:T(8,128)(2,1)S(1)} %pad_maximum_fusion.refs_2_.refs_1_, bf16[384,1024]{1,0:T(8,128)(2,1)} %collective-permute-done.refs_3_.refs_2_, ...), custom_call_target="tpu_custom_call" | custom-call | flops 1000000000 | bytes 6000000 | tf_op jit(solution)/shard_map/pallas_call | solution.py:265
  76.7 0.0 copy-start.10
  76.7 0.7 copy-done.10
  77.4 3.4 %collective-permute-start.4 = (bf16[128,1024]{1,0:T(8,128)(2,1)S(1)}, bf16[128,1024]{1,0:T(8,128)(2,1)S(1)}, u32[]{:S(2)}, u32[]{:S(2)}) collective-permute-start(bf16[128,1024]{1,0:T(8,128)(2,1)S(1)} %get-tuple-element.25), channel_id=1, source_target_pairs={{0,256},{64,320},{128,384},{192,448},{256,0},{320,64},{384,128},{4... | collective-permute-start | bytes 786440 | tf_op jit(solution)/shard_map/ppermute | solution.py:274
  80.8 3.4 %shard_map.114 = (f32[256,1024]{1,0:T(8,128)S(1)}, bf16[4,128,384]{2,1,0:T(8,128)(2,1)S(1)}) custom-call(bf16[128,1024]{1,0:T(8,128)(2,1)S(1)} %get-tuple-element.22.refs_0_, bf16[128,1024]{1,0:T(8,128)(2,1)S(1)} %get-tuple-element.23.refs_1_, bf16[384,1024]{1,0:T(8,128)(2,1)S(1)} %pad_maximum_fusion.refs_2_.refs_1_, ...), custom_call_target="tpu_custom_call" | custom-call | flops 1000000000 | bytes 6000000 | tf_op jit(solution)/shard_map/pallas_call | solution.py:265
  84.3 2.1 %collective-permute-done.6.refs_1_ = bf16[128,1024]{1,0:T(8,128)(2,1)S(1)} collective-permute-done((bf16[128,1024]{1,0:T(8,128)(2,1)S(1)}, bf16[128,1024]{1,0:T(8,128)(2,1)S(1)}, u32[]{:S(2)}, u32[]{:S(2)}) %collective-permute-start.6) | collective-permute-done | bytes 262176 | tf_op jit(solution)/shard_map/ppermute | solution.py:274
  86.3 3.9 %collective-permute-done.4.refs_0_ = bf16[128,1024]{1,0:T(8,128)(2,1)S(1)} collective-permute-done((bf16[128,1024]{1,0:T(8,128)(2,1)S(1)}, bf16[128,1024]{1,0:T(8,128)(2,1)S(1)}, u32[]{:S(2)}, u32[]{:S(2)}) %collective-permute-start.4) | collective-permute-done | bytes 262176 | tf_op jit(solution)/shard_map/ppermute | solution.py:274
  90.3 1.4 shard_map.117
  91.7 0.0 copy-start.11
  91.8 21.0 %all-to-all-start.1 = ((bf16[64,8,1024]{2,1,0:T(8,128)(2,1)}), bf16[64,8,1024]{2,1,0:T(8,128)(2,1)S(1)}, u32[]{:S(2)}, u32[]{:S(2)}) async-start(bf16[64,8,1024]{2,1,0:T(8,128)(2,1)} %bitcast.8), calls=%async_computation.1 | async-start | bytes 2097152 | tf_op jit(solution)/shard_map/all_to_all | solution.py:234
  112.8 0.0 copy-start.1
  112.8 1.0 shard_map.119
  113.8 4.4 %collective-permute-start.7 = (bf16[384,1024]{1,0:T(8,128)(2,1)S(1)}, bf16[384,1024]{1,0:T(8,128)(2,1)S(1)}, u32[]{:S(2)}, u32[]{:S(2)}) collective-permute-start(bf16[384,1024]{1,0:T(8,128)(2,1)S(1)} %get-tuple-element.33), channel_id=1, source_target_pairs={{0,192},{64,0},{128,64},{192,128},{256,448},{320,256},{384,320},{4... | collective-permute-start | bytes 2359304 | tf_op jit(solution)/shard_map/ppermute | solution.py:284
  118.2 1.9 %collective-permute-start.8 = (bf16[384,1024]{1,0:T(8,128)(2,1)S(1)}, bf16[384,1024]{1,0:T(8,128)(2,1)S(1)}, u32[]{:S(2)}, u32[]{:S(2)}) collective-permute-start(bf16[384,1024]{1,0:T(8,128)(2,1)S(1)} %get-tuple-element.34), channel_id=1, source_target_pairs={{0,64},{64,128},{128,192},{192,0},{256,320},{320,384},{384,448},{4... | collective-permute-start | bytes 2359304 | tf_op jit(solution)/shard_map/ppermute | solution.py:284
  120.1 3.4 %collective-permute-start.9 = (bf16[384,1024]{1,0:T(8,128)(2,1)S(1)}, bf16[384,1024]{1,0:T(8,128)(2,1)S(1)}, u32[]{:S(2)}, u32[]{:S(2)}) collective-permute-start(bf16[384,1024]{1,0:T(8,128)(2,1)S(1)} %get-tuple-element.35), channel_id=1, source_target_pairs={{0,128},{64,192},{128,0},{192,64},{256,384},{320,448},{384,256},{4... | collective-permute-start | bytes 2359304 | tf_op jit(solution)/shard_map/ppermute | solution.py:284
  123.6 0.4 shard_map.110.back_ref
  123.9 11.5 %collective-permute-done.7.g1 = bf16[384,1024]{1,0:T(8,128)(2,1)S(1)} collective-permute-done((bf16[384,1024]{1,0:T(8,128)(2,1)S(1)}, bf16[384,1024]{1,0:T(8,128)(2,1)S(1)}, u32[]{:S(2)}, u32[]{:S(2)}) %collective-permute-start.7) | collective-permute-done | bytes 786464 | tf_op jit(solution)/shard_map/ppermute | solution.py:284
  135.4 5.4 %collective-permute-done.8.g2 = bf16[384,1024]{1,0:T(8,128)(2,1)S(1)} collective-permute-done((bf16[384,1024]{1,0:T(8,128)(2,1)S(1)}, bf16[384,1024]{1,0:T(8,128)(2,1)S(1)}, u32[]{:S(2)}, u32[]{:S(2)}) %collective-permute-start.8) | collective-permute-done | bytes 786464 | tf_op jit(solution)/shard_map/ppermute | solution.py:284
  140.8 14.6 %collective-permute-done.9.g3 = bf16[384,1024]{1,0:T(8,128)(2,1)S(1)} collective-permute-done((bf16[384,1024]{1,0:T(8,128)(2,1)S(1)}, bf16[384,1024]{1,0:T(8,128)(2,1)S(1)}, u32[]{:S(2)}, u32[]{:S(2)}) %collective-permute-start.9) | collective-permute-done | bytes 786464 | tf_op jit(solution)/shard_map/ppermute | solution.py:284
  155.4 1.1 shard_map.120
  156.6 0.0 all-to-all-done.1
  156.6 1.4 shard_map.118
  (18 shorter events, 0.0 us)
Async XLA Ops:
  0.6 17.3 %copy-start.12 = (bf16[1,128,1024]{2,1,0:T(8,128)(2,1)S(1)}, bf16[1,128,1024]{2,1,0:T(8,128)(2,1)}, u32[]{:S(2)}) copy-start(bf16[1,128,1024]{2,1,0:T(8,128)(2,1)} %param.13) | copy-start | bytes 786436
  0.6 17.3 %copy-start.13 = (bf16[1,128,1024]{2,1,0:T(8,128)(2,1)S(1)}, bf16[1,128,1024]{2,1,0:T(8,128)(2,1)}, u32[]{:S(2)}) copy-start(bf16[1,128,1024]{2,1,0:T(8,128)(2,1)} %param.12) | copy-start | bytes 786436
  0.7 17.3 %copy-start.14 = (bf16[1,128,1024]{2,1,0:T(8,128)(2,1)S(1)}, bf16[1,128,1024]{2,1,0:T(8,128)(2,1)}, u32[]{:S(2)}) copy-start(bf16[1,128,1024]{2,1,0:T(8,128)(2,1)} %param.11) | copy-start | bytes 786436
  3.3 24.7 %copy-start = (s32[1,64,128]{2,1,0:T(8,128)S(1)}, s32[1,64,128]{2,1,0:T(8,128)}, u32[]{:S(2)}) copy-start(s32[1,64,128]{2,1,0:T(8,128)} %param.9) | copy-start | bytes 98308
  3.3 43.1 %all-to-all-start = ((bf16[64,8,1024]{2,1,0:T(8,128)(2,1)}), bf16[64,8,1024]{2,1,0:T(8,128)(2,1)S(1)}, u32[]{:S(2)}, u32[]{:S(2)}) async-start(bf16[64,8,1024]{2,1,0:T(8,128)(2,1)} %bitcast.20), calls=%async_computation | async-start | bytes 2097152 | tf_op jit(solution)/shard_map/all_to_all | solution.py:234
  18.0 38.8 %collective-permute-start.2 = (bf16[384,1024]{1,0:T(8,128)(2,1)S(1)}, bf16[384,1024]{1,0:T(8,128)(2,1)S(1)}, u32[]{:S(2)}, u32[]{:S(2)}) collective-permute-start(bf16[384,1024]{1,0:T(8,128)(2,1)S(1)} %pad_maximum_fusion.refs_2_.refs_1_), channel_id=1, source_target_pairs={{0,128},{64,192},{128,0},{192,64},{256,384},{320,448},{384,256},{4... | collective-permute-start | bytes 2359304 | tf_op jit(solution)/shard_map/ppermute | solution.py:254
  22.7 34.5 %collective-permute-start.1 = (bf16[384,1024]{1,0:T(8,128)(2,1)S(1)}, bf16[384,1024]{1,0:T(8,128)(2,1)}, u32[]{:S(2)}, u32[]{:S(2)}) collective-permute-start(bf16[384,1024]{1,0:T(8,128)(2,1)S(1)} %pad_maximum_fusion.refs_2_.refs_1_), channel_id=1, source_target_pairs={{0,192},{64,0},{128,64},{192,128},{256,448},{320,256},{384,320},{4... | collective-permute-start | bytes 2359304 | tf_op jit(solution)/shard_map/ppermute | solution.py:254
  25.5 32.4 %collective-permute-start = (bf16[384,1024]{1,0:T(8,128)(2,1)S(1)}, bf16[384,1024]{1,0:T(8,128)(2,1)}, u32[]{:S(2)}, u32[]{:S(2)}) collective-permute-start(bf16[384,1024]{1,0:T(8,128)(2,1)S(1)} %pad_maximum_fusion.refs_2_.refs_1_), channel_id=1, source_target_pairs={{0,64},{64,128},{128,192},{192,0},{256,320},{320,384},{384,448},{4... | collective-permute-start | bytes 2359304 | tf_op jit(solution)/shard_map/ppermute | solution.py:254
  47.0 14.9 %collective-permute-start.5 = (bf16[128,1024]{1,0:T(8,128)(2,1)S(1)}, bf16[128,1024]{1,0:T(8,128)(2,1)S(1)}, u32[]{:S(2)}, u32[]{:S(2)}) collective-permute-start(bf16[128,1024]{1,0:T(8,128)(2,1)S(1)} %get-tuple-element.23.refs_1_), channel_id=1, source_target_pairs={{0,256},{64,320},{128,384},{192,448},{256,0},{320,64},{384,128},{4... | collective-permute-start | bytes 786440 | tf_op jit(solution)/shard_map/ppermute | solution.py:269
  54.9 18.2 %collective-permute-start.3 = (bf16[128,1024]{1,0:T(8,128)(2,1)S(1)}, bf16[128,1024]{1,0:T(8,128)(2,1)S(1)}, u32[]{:S(2)}, u32[]{:S(2)}) collective-permute-start(bf16[128,1024]{1,0:T(8,128)(2,1)S(1)} %get-tuple-element.22.refs_0_), channel_id=1, source_target_pairs={{0,256},{64,320},{128,384},{192,448},{256,0},{320,64},{384,128},{4... | collective-permute-start | bytes 786440 | tf_op jit(solution)/shard_map/ppermute | solution.py:269
  61.9 3.5 %copy-start.2 = (bf16[128,1024]{1,0:T(8,128)(2,1)}, bf16[128,1024]{1,0:T(8,128)(2,1)S(1)}, u32[]{:S(2)}) copy-start(bf16[128,1024]{1,0:T(8,128)(2,1)S(1)} %collective-permute-done.5.refs_0_.refs_3_) | copy-start | bytes 786436
  65.4 0.7 copy-start.8
  66.1 20.2 %collective-permute-start.6 = (bf16[128,1024]{1,0:T(8,128)(2,1)S(1)}, bf16[128,1024]{1,0:T(8,128)(2,1)S(1)}, u32[]{:S(2)}, u32[]{:S(2)}) collective-permute-start(bf16[128,1024]{1,0:T(8,128)(2,1)S(1)} %get-tuple-element.26), channel_id=1, source_target_pairs={{0,256},{64,320},{128,384},{192,448},{256,0},{320,64},{384,128},{4... | collective-permute-start | bytes 786440 | tf_op jit(solution)/shard_map/ppermute | solution.py:274
  73.2 3.5 %copy-start.4 = (bf16[128,1024]{1,0:T(8,128)(2,1)}, bf16[128,1024]{1,0:T(8,128)(2,1)S(1)}, u32[]{:S(2)}) copy-start(bf16[128,1024]{1,0:T(8,128)(2,1)S(1)} %collective-permute-done.3.refs_0_.refs_2_) | copy-start | bytes 786436
  76.7 0.7 copy-start.10
  77.4 12.9 %collective-permute-start.4 = (bf16[128,1024]{1,0:T(8,128)(2,1)S(1)}, bf16[128,1024]{1,0:T(8,128)(2,1)S(1)}, u32[]{:S(2)}, u32[]{:S(2)}) collective-permute-start(bf16[128,1024]{1,0:T(8,128)(2,1)S(1)} %get-tuple-element.25), channel_id=1, source_target_pairs={{0,256},{64,320},{128,384},{192,448},{256,0},{320,64},{384,128},{4... | collective-permute-start | bytes 786440 | tf_op jit(solution)/shard_map/ppermute | solution.py:274
  84.3 7.5 %copy-start.6 = (bf16[4,128,384]{2,1,0:T(8,128)(2,1)}, bf16[4,128,384]{2,1,0:T(8,128)(2,1)S(1)}, u32[]{:S(2)}) copy-start(bf16[4,128,384]{2,1,0:T(8,128)(2,1)S(1)} %get-tuple-element.29.refs_4_) | copy-start | bytes 1179652
  91.7 21.0 %copy-start.3 = (bf16[128,1024]{1,0:T(8,128)(2,1)S(1)}, bf16[128,1024]{1,0:T(8,128)(2,1)}, u32[]{:S(2)}) copy-start(bf16[128,1024]{1,0:T(8,128)(2,1)} %copy-done.2) | copy-start | bytes 786436
  91.7 21.0 %copy-start.5 = (bf16[128,1024]{1,0:T(8,128)(2,1)S(1)}, bf16[128,1024]{1,0:T(8,128)(2,1)}, u32[]{:S(2)}) copy-start(bf16[128,1024]{1,0:T(8,128)(2,1)} %copy-done.4) | copy-start | bytes 786436
  91.7 21.0 %copy-start.9 = (bf16[4,64,384]{2,1,0:T(8,128)(2,1)S(1)}, bf16[4,64,384]{2,1,0:T(8,128)(2,1)}, u32[]{:S(2)}) copy-start(bf16[4,64,384]{2,1,0:T(8,128)(2,1)} %copy-done.8) | copy-start | bytes 589828
  91.7 21.0 %copy-start.11 = (bf16[4,64,384]{2,1,0:T(8,128)(2,1)S(1)}, bf16[4,64,384]{2,1,0:T(8,128)(2,1)}, u32[]{:S(2)}) copy-start(bf16[4,64,384]{2,1,0:T(8,128)(2,1)} %copy-done.10) | copy-start | bytes 589828
  91.8 21.0 %copy-start.7 = (bf16[4,128,384]{2,1,0:T(8,128)(2,1)S(1)}, bf16[4,128,384]{2,1,0:T(8,128)(2,1)}, u32[]{:S(2)}) copy-start(bf16[4,128,384]{2,1,0:T(8,128)(2,1)} %copy-done.6) | copy-start | bytes 1179652
  91.8 64.8 %all-to-all-start.1 = ((bf16[64,8,1024]{2,1,0:T(8,128)(2,1)}), bf16[64,8,1024]{2,1,0:T(8,128)(2,1)S(1)}, u32[]{:S(2)}, u32[]{:S(2)}) async-start(bf16[64,8,1024]{2,1,0:T(8,128)(2,1)} %bitcast.8), calls=%async_computation.1 | async-start | bytes 2097152 | tf_op jit(solution)/shard_map/all_to_all | solution.py:234
  112.8 10.8 %copy-start.1 = (f32[1,64,128]{2,1,0:T(8,128)S(1)}, f32[1,64,128]{2,1,0:T(8,128)}, u32[]{:S(2)}) copy-start(f32[1,64,128]{2,1,0:T(8,128)} %param.10) | copy-start | bytes 98308
  113.8 21.6 %collective-permute-start.7 = (bf16[384,1024]{1,0:T(8,128)(2,1)S(1)}, bf16[384,1024]{1,0:T(8,128)(2,1)S(1)}, u32[]{:S(2)}, u32[]{:S(2)}) collective-permute-start(bf16[384,1024]{1,0:T(8,128)(2,1)S(1)} %get-tuple-element.33), channel_id=1, source_target_pairs={{0,192},{64,0},{128,64},{192,128},{256,448},{320,256},{384,320},{4... | collective-permute-start | bytes 2359304 | tf_op jit(solution)/shard_map/ppermute | solution.py:284
  118.2 22.6 %collective-permute-start.8 = (bf16[384,1024]{1,0:T(8,128)(2,1)S(1)}, bf16[384,1024]{1,0:T(8,128)(2,1)S(1)}, u32[]{:S(2)}, u32[]{:S(2)}) collective-permute-start(bf16[384,1024]{1,0:T(8,128)(2,1)S(1)} %get-tuple-element.34), channel_id=1, source_target_pairs={{0,64},{64,128},{128,192},{192,0},{256,320},{320,384},{384,448},{4... | collective-permute-start | bytes 2359304 | tf_op jit(solution)/shard_map/ppermute | solution.py:284
  120.1 35.3 %collective-permute-start.9 = (bf16[384,1024]{1,0:T(8,128)(2,1)S(1)}, bf16[384,1024]{1,0:T(8,128)(2,1)S(1)}, u32[]{:S(2)}, u32[]{:S(2)}) collective-permute-start(bf16[384,1024]{1,0:T(8,128)(2,1)S(1)} %get-tuple-element.35), channel_id=1, source_target_pairs={{0,128},{64,192},{128,0},{192,64},{256,384},{320,448},{384,256},{4... | collective-permute-start | bytes 2359304 | tf_op jit(solution)/shard_map/ppermute | solution.py:284

commit v4 on v2

--- a/solution.py
+++ b/solution.py
@@ -34,7 +34,7 @@
         + [pl.BlockSpec(memory_space=pltpu.VMEM)] * n_vmem,
         out_specs=jax.tree.map(lambda _: pl.BlockSpec(memory_space=pltpu.VMEM), out_shapes),
         cost_estimate=pl.CostEstimate(flops=flops, bytes_accessed=nbytes, transcendentals=0),
-        compiler_params=pltpu.CompilerParams(vmem_limit_bytes=48 * 1024 * 1024),
+        compiler_params=pltpu.CompilerParams(vmem_limit_bytes=24 * 1024 * 1024),
     )
 
 
@@ -95,10 +95,10 @@
         out_ref[:, c * 128 : (c + 1) * 128] = part.astype(BF16)
 
 
-def place_body(my_ref, pick_ref, place_ref):
+def place_table(my, pick_ref):
     n_experts, cap = pick_ref.shape
     n_slots = n_experts * 2 * SLOT
-    own = pick_ref[pl.ds(my_ref[0], 1), :]
+    own = pick_ref[pl.ds(my, 1), :]
     source = lax.shift_right_logical(own, 7)
     from_dev = (
         lax.broadcasted_iota(jnp.int32, (n_experts, cap), 0)
@@ -110,13 +110,13 @@
     position = source * (2 * SLOT) + rank.astype(jnp.int32)
     both = jnp.concatenate([position, position + SLOT], axis=1)
     sub = lax.broadcasted_iota(jnp.int32, (n_slots, 2 * cap), 0)
-    place_ref[...] = (sub == jnp.broadcast_to(both, (n_slots, 2 * cap))).astype(F32).astype(BF16)
-
-
-def back_body(my_ref, pick_ref, weight_ref, back_ref):
+    return (sub == jnp.broadcast_to(both, (n_slots, 2 * cap))).astype(F32).astype(BF16)
+
+
+def combine_body(my_ref, pick_ref, weight_ref, slots_ref, layer_ref, grad_ref):
     n_experts = pick_ref.shape[0]
+    tok_rows = layer_ref.shape[0]
     n_slots = n_experts * 2 * SLOT
-    tok_rows = back_ref.shape[1] // 3
     row, share = slot_tables(my_ref[0], pick_ref[...], weight_ref[...], tok_rows)
     shape = (n_experts, 2 * SLOT, tok_rows)
     lane = lax.broadcasted_iota(jnp.int32, shape, 2).astype(F32)
@@ -131,61 +131,90 @@
         jnp.where(hit & second, 1.0, zero),
         jnp.where(first_hit, low, zero),
     )
-    for i, piece in enumerate(pieces):
-        back_ref[:, i * tok_rows : (i + 1) * tok_rows] = piece.reshape(n_slots, tok_rows).astype(
-            BF16
-        )
-
-
-def compact_body(place_ref, recv_ref, out_ref):
-    out_ref[...] = mm(place_ref[...], recv_ref[...], 0, 0).astype(BF16)
-
-
-def expert_body(rows_ref, w0, w1, w2, w3, part_ref, act_ref):
-    cap = rows_ref.shape[0] // 2
-    chosen, weighted = rows_ref[:cap], rows_ref[cap:]
+    table = jnp.concatenate([p.reshape(n_slots, tok_rows).astype(BF16) for p in pieces], axis=1)
+    sums = mm(table, slots_ref[...], 0, 0)
+    layer_ref[...] = (sums[:tok_rows] + sums[2 * tok_rows :]).astype(BF16)
+    grad_ref[...] = sums[tok_rows : 2 * tok_rows].astype(BF16)
+
+
+def compact_body(my_ref, pick_ref, recv_ref, chosen_ref, weighted_ref):
+    rows = mm(place_table(my_ref[0], pick_ref), recv_ref[...], 0, 0).astype(BF16)
+    cap = chosen_ref.shape[0]
+    chosen_ref[...] = rows[:cap]
+    weighted_ref[...] = rows[cap:]
+
+
+def forward(chosen, w_ref):
+    width = w_ref.shape[0] // 3
+    pre = mm(chosen, w_ref[: 2 * width], 1, 1)
+    gate, up = pre[:, :width], pre[:, width:]
+    sigma = jax.nn.sigmoid(gate)
+    silu = gate * sigma
+    slope = up * sigma * (1.0 + gate * (1.0 - sigma))
+    return (silu * up).astype(BF16), slope, silu
+
+
+def backward(weighted, slope, silu, w_ref):
+    d_hidden = mm(weighted, w_ref[2 * (w_ref.shape[0] // 3) :], 1, 1)
+    return jnp.concatenate([(d_hidden * slope).astype(BF16), (d_hidden * silu).astype(BF16)], axis=1)
+
+
+def forward_body(chosen_ref, w0, w1, w2, w3, out_ref, hidden_ref, factor_ref):
     width = w0.shape[0] // 3
-    out = jnp.zeros((cap, rows_ref.shape[1]), F32)
-    back = jnp.zeros((cap, rows_ref.shape[1]), F32)
+    chosen = chosen_ref[...]
+    out = jnp.zeros(chosen.shape, F32)
     for i, w_ref in enumerate((w0, w1, w2, w3)):
-        pre = mm(chosen, w_ref[: 2 * width], 1, 1)
-        d_hidden = mm(weighted, w_ref[2 * width :], 1, 1)
-        gate, up = pre[:, :width], pre[:, width:]
-        sigma = jax.nn.sigmoid(gate)
-        silu = gate * sigma
-        hidden = (silu * up).astype(BF16)
-        d_gate = (d_hidden * up * sigma * (1.0 + gate * (1.0 - sigma))).astype(BF16)
-        d_up = (d_hidden * silu).astype(BF16)
-        d_both = jnp.concatenate([d_gate, d_up], axis=1)
+        hidden, slope, silu = forward(chosen, w_ref)
+        out = out + mm(hidden, w_ref[2 * width :], 1, 0)
+        hidden_ref[i] = hidden
+        factor_ref[i, :, :width] = slope
+        factor_ref[i, :, width:] = silu
+    out_ref[...] = out.astype(BF16)
+
+
+def backward_body(weighted_ref, factor_ref, w0, w1, w2, w3, back_ref, d_ref):
+    width = w0.shape[0] // 3
+    weighted = weighted_ref[...]
+    back = jnp.zeros(weighted.shape, F32)
+    for i, w_ref in enumerate((w0, w1, w2, w3)):
+        d_both = backward(weighted, factor_ref[i, :, :width], factor_ref[i, :, width:], w_ref)
+        back = back + mm(d_both, w_ref[: 2 * width], 1, 0)
+        d_ref[i] = d_both
+    back_ref[...] = back.astype(BF16)
+
+
+def here_body(chosen_ref, weighted_ref, w0, w1, w2, w3, part_ref, hidden_ref, d_ref):
+    width = w0.shape[0] // 3
+    chosen, weighted = chosen_ref[...], weighted_ref[...]
+    cap = chosen.shape[0]
+    out = jnp.zeros(chosen.shape, F32)
+    back = jnp.zeros(chosen.shape, F32)
+    for i, w_ref in enumerate((w0, w1, w2, w3)):
+        hidden, slope, silu = forward(chosen, w_ref)
+        d_both = backward(weighted, slope, silu, w_ref)
         out = out + mm(hidden, w_ref[2 * width :], 1, 0)
         back = back + mm(d_both, w_ref[: 2 * width], 1, 0)
-        act_ref[i, :, : 2 * width] = d_both
-        act_ref[i, :, 2 * width :] = hidden
-    part_ref[:cap] = out.astype(part_ref.dtype)
-    part_ref[cap:] = back.astype(part_ref.dtype)
-
-
-def grads_body(rows_here, rows_there, act_here, act_there, g_own, g1, g2, g3):
-    cap = rows_here.shape[0] // 2
-    width = g_own.shape[0] // 3
-    chosen = jnp.concatenate([rows_here[:cap], rows_there[:cap]], axis=0)
-    weighted = jnp.concatenate([rows_here[cap:], rows_there[cap:]], axis=0)
-    for i, g_ref in ((3, g3), (1, g1), (2, g2), (0, g_own)):
-        act = jnp.concatenate([act_here[i], act_there[i]], axis=0)
-        g_ref[: 2 * width] = mm(act[:, : 2 * width], chosen, 0, 0).astype(g_ref.dtype)
-        g_ref[2 * width :] = mm(act[:, 2 * width :], weighted, 0, 0).astype(g_ref.dtype)
-
-
-def expand_body(place_ref, own_ref, other_ref, out_ref):
-    total = (own_ref[...] + other_ref[...].astype(F32)).astype(BF16)
-    out_ref[...] = mm(place_ref[...], total, 1, 0).astype(BF16)
-
-
-def combine_body(back_ref, slots_ref, layer_ref, grad_ref):
-    n = layer_ref.shape[0]
-    sums = mm(back_ref[...], slots_ref[...], 0, 0)
-    layer_ref[...] = (sums[:n] + sums[2 * n :]).astype(BF16)
-    grad_ref[...] = sums[n : 2 * n].astype(BF16)
+        hidden_ref[i] = hidden
+        d_ref[i] = d_both
+    part_ref[:cap] = out
+    part_ref[cap:] = back
+
+
+def grads_body(blocks, chosen2, weighted2, hidden2, d2, *g_refs):
+    chosen = jnp.concatenate([ref[...] for ref in chosen2], axis=0)
+    weighted = jnp.concatenate([ref[...] for ref in weighted2], axis=0)
+    for i, g_ref in zip(blocks, g_refs):
+        hidden = jnp.concatenate([ref[i] for ref in hidden2], axis=0)
+        d_both = jnp.concatenate([ref[i] for ref in d2], axis=0)
+        n = d_both.shape[1]
+        g_ref[:n] = mm(d_both, chosen, 0, 0).astype(g_ref.dtype)
+        g_ref[n:] = mm(hidden, weighted, 0, 0).astype(g_ref.dtype)
+
+
+def expand_body(my_ref, pick_ref, own_ref, out_ref, back_ref, slots_ref):
+    other = jnp.concatenate([out_ref[...], back_ref[...]], axis=0)
+    total = (own_ref[...] + other.astype(F32)).astype(BF16)
+    slots_ref[...] = mm(place_table(my_ref[0], pick_ref), total, 1, 0).astype(BF16)
 
 
 def weight_sum_body(g_own, g1, g2, g3, gate_ref, up_ref, down_ref):
@@ -193,7 +222,7 @@
     for i, ref in enumerate((gate_ref, up_ref, down_ref)):
         piece = pl.ds(i * width, width)
         ref[...] = (
-            g_own[piece, :]
+            g_own[piece, :].astype(F32)
             + g1[piece, :].astype(F32)
             + g2[piece, :].astype(F32)
             + g3[piece, :].astype(F32)
@@ -209,7 +238,6 @@
     my = lax.axis_index("expert").astype(jnp.int32).reshape(1)
     sds = jax.ShapeDtypeStruct
     picks, shares = pick_lists[0], combine[0]
-    row_pair = sds((2 * cap, feat), BF16)
     slot_rows = sds((n_slots, feat), BF16)
 
     def exchange(rows):
@@ -232,38 +260,65 @@
         cost_estimate=pl.CostEstimate(flops=3 * 10**8, bytes_accessed=2 * 10**6, transcendentals=0),
     )(my, picks, shares, tokens, cotangent)
     recv = exchange(send)
-    place = kernel_call(place_body, sds((n_slots, 2 * cap), BF16), 1, 1, 10**7, 10**6)(my, picks)
     w_own = jnp.concatenate([w_gate[0], w_up[0], w_down[0]], axis=0)
     w_all = [w_own] + [lax.ppermute(w_own, "dp", x_shift(s)) for s in (1, -1, 2)]
-    rows = kernel_call(compact_body, row_pair, 0, 2, 3 * 10**8, 2 * 10**6)(place, recv)
-    rows_there = lax.ppermute(rows, "dp", HALF_SWAP)
-    act = sds((len(w_all), cap, 3 * width), BF16)
-
-    def expert(rows_of_one, part):
-        return kernel_call(expert_body, (part, act), 0, 5, 10**9, 7 * 10**6)(rows_of_one, *w_all)
-
-    part_here, act_here = expert(rows, sds(row_pair.shape, F32))
-    part_there, act_there = expert(rows_there, row_pair)
-    part_back = lax.ppermute(part_there, "dp", HALF_SWAP)
+    block = sds((cap, feat), BF16)
+    n_blocks = len(w_all)
+    hidden_shape = sds((n_blocks, cap, width), BF16)
+    d_shape = sds((n_blocks, cap, 2 * width), BF16)
+
+    def swap(rows):
+        return lax.ppermute(rows, "dp", HALF_SWAP)
+
+    chosen, weighted = kernel_call(compact_body, (block,) * 2, 1, 2, 3 * 10**8, 2 * 10**6)(
+        my, picks, recv
+    )
+    chosen_there = swap(chosen)
+    weighted_there = swap(weighted)
+    out_there, hidden_there, factors = kernel_call(
+        forward_body,
+        (block, hidden_shape, sds(d_shape.shape, F32)),
+        0,
+        1 + n_blocks,
+        5 * 10**8,
+        5 * 10**6,
+    )(chosen_there, *w_all)
+    out_back = swap(out_there)
+    back_there, d_there = kernel_call(
+        backward_body, (block, d_shape), 0, 2 + n_blocks, 5 * 10**8, 5 * 10**6
+    )(weighted_there, factors, *w_all)
+    back_back = swap(back_there)
+    part_here, hidden_here, d_here = kernel_call(
+        here_body,
+        (sds((2 * cap, feat), F32), hidden_shape, d_shape),
+        0,
+        2 + n_blocks,
+        10**9,
+        6 * 10**6,
+    )(chosen, weighted, *w_all)
     g_shape = (3 * width, feat)
-    g_own, *g_others = kernel_call(
-        grads_body, (sds(g_shape, F32),) + (sds(g_shape, BF16),) * 3, 0, 4, 10**9, 6 * 10**6
-    )(rows, rows_there, act_here, act_there)
-    g_home = [lax.ppermute(g, "dp", x_shift(-s)) for g, s in zip(g_others, (1, -1, 2))]
-    slots = kernel_call(expand_body, slot_rows, 0, 3, 3 * 10**8, 4 * 10**6)(
-        place, part_here, part_back
+
+    def grads(*refs):
+        pairs = [refs[2 * i : 2 * i + 2] for i in range(4)]
+        grads_body((3, 1, 2, 0), *pairs, *refs[8:])
+
+    g_far, g_right, g_left, g_own = kernel_call(
+        grads, (sds(g_shape, BF16),) * 4, 0, 8, 10**9, 6 * 10**6
+    )(chosen, chosen_there, weighted, weighted_there, hidden_here, hidden_there, d_here, d_there)
+    g3 = lax.ppermute(g_far, "dp", x_shift(-2))
+    slots = kernel_call(expand_body, slot_rows, 1, 4, 3 * 10**8, 4 * 10**6)(
+        my, picks, part_here, out_back, back_back
     )
     returned = exchange(slots)
-    back_table = kernel_call(
-        back_body, sds((n_slots, 3 * tok_rows), BF16), 1, 2, 10**7, 10**6
-    )(my, picks, shares)
+    g1 = lax.ppermute(g_right, "dp", x_shift(-1))
+    g2 = lax.ppermute(g_left, "dp", x_shift(1))
     layer_out, tokens_grad = kernel_call(
-        combine_body, (sds((tok_rows, feat), BF16),) * 2, 0, 2, 4 * 10**8, 2 * 10**6
-    )(back_table, returned)
-    grads = kernel_call(
+        combine_body, (sds((tok_rows, feat), BF16),) * 2, 1, 3, 4 * 10**8, 2 * 10**6
+    )(my, picks, shares, returned)
+    w_grads = kernel_call(
         weight_sum_body, (sds((width, feat), BF16),) * 3, 0, 4, 10**6, 5 * 10**6
-    )(g_own, *g_home)
-    return (layer_out, tokens_grad) + tuple(g[None] for g in grads)
+    )(g_own, g1, g2, g3)
+    return (layer_out, tokens_grad) + tuple(g[None] for g in w_grads)
 
 
 def solution(mesh):

time: 167 us -> 159 us (0.952)
  starting transfers between devices: 79.5 us -> 74.5 us
  waiting for transfers between devices: 67.8 us -> 64.4 us
    all_to_all x2, starting transfers between devices: 44.7 us -> 32.4 us  [exchange(): lax.all_to_all(parts, 'expert', split_axis=0, concat_axis=0, tiled=True)]
    ppermute x5 -> x7, starting transfers between devices: 24.9 us -> 32.2 us  [the longest x4 22.2 us: swap(): return lax.ppermute(rows, 'dp', HALF_SWAP)]
    ppermute x3, waiting for transfers between devices: 2.94 us -> 0.01 us  [per_device(): lax.ppermute(w_own, 'dp', x_shift(s))]
    pallas_call x8 -> x7, Pallas kernels: 12 us -> 11 us  [the longest x1 2.1 us: per_device(): kernel_call(here_body, (sds((2 * cap, feat), F32), hidden_shape, d_shape)...]
    ppermute x5 -> x7, waiting for transfers between devices: 46.6 us -> 46 us  [the longest x1 15.1 us: per_device(): g3 = lax.ppermute(g_far, 'dp', x_shift(-2))]
  transfers between devices with their start and end apart: 10 -> 12, of which waited for: 8 -> 6; matrix products, arithmetic and copies ran while one was open for 0% -> 0% of each run, Pallas kernels for 4% -> 6%
where the time goes in v4:
time: 159 us; the launch traced here: 157 us
  starting transfers between devices  74.5 us (47%)
  waiting for transfers between devices  64.4 us (41%)
  Pallas kernels  14.8 us (9%)
  local copies, waits for them, and re-layouts  2.36 us (1%)
    all_to_all x2, starting transfers between devices, exchange(): lax.all_to_all(parts, 'expert', split_axis=0, concat_axis=0, tiled=True)  32.4 us
    ppermute x4, starting transfers between devices, swap(): return lax.ppermute(rows, 'dp', HALF_SWAP)  22.2 us
    all_to_all x2, waiting for transfers between devices, exchange(): lax.all_to_all(parts, 'expert', split_axis=0, concat_axis=0, tiled=True)  18.4 us
    ppermute x1, waiting for transfers between devices, per_device(): g3 = lax.ppermute(g_far, 'dp', x_shift(-2))  15.1 us
    ppermute x4, waiting for transfers between devices, swap(): return lax.ppermute(rows, 'dp', HALF_SWAP)  14.2 us
    ppermute x1, waiting for transfers between devices, per_device(): g1 = lax.ppermute(g_right, 'dp', x_shift(-1))  11.6 us
    ppermute x3, starting transfers between devices, per_device(): lax.ppermute(w_own, 'dp', x_shift(s))  9.94 us
    ppermute x1, waiting for transfers between devices, per_device(): g2 = lax.ppermute(g_left, 'dp', x_shift(1))  5.17 us
  transfers between devices with their start and end apart: 12, of which 6 were waited for; matrix products, arithmetic and copies ran while one was open for 0% of the time, Pallas kernels for 6%

profile of v4, /device:TPU:1, one launch (start us, length us, event | category | flops | bytes accessed | tf_op | source)
XLA Modules:
  0.0 157.2 jit_solution(3482633298342926127)
XLA Ops:
  0.6 2.6 %shard_map.110 = bf16[512,1024]{1,0:T(8,128)(2,1)} custom-call(s32[1]{0:T(128)} %bitcast.my_ref, s32[64,128]{1,0:T(8,128)} %bitcast.14, f32[64,128]{1,0:T(8,128)} %bitcast.18, bf16[128,1024]{1,0:T(8,128)(2,1)} %tok_hbm.1, bf16[128,1024]{1,0:T(8,128)(2,1)} %cot_hbm.1), custom_call_target="tpu_custom_call" | custom-call | flops 300000000 | bytes 2000000 | tf_op jit(solution)/shard_map/pallas_call | solution.py:249
  3.2 0.0 copy-start.16
  3.3 0.0 copy-start.17
  3.3 0.0 copy-start.18
  3.3 14.9 %all-to-all-start = ((bf16[64,8,1024]{2,1,0:T(8,128)(2,1)}), bf16[64,8,1024]{2,1,0:T(8,128)(2,1)}, u32[]{:S(2)}, u32[]{:S(2)}) async-start(bf16[64,8,1024]{2,1,0:T(8,128)(2,1)} %bitcast.20), calls=%async_computation | async-start | bytes 2097152 | tf_op jit(solution)/shard_map/all_to_all | solution.py:245
  18.2 0.0 copy-start.2
  18.2 0.1 pad_maximum_fusion.w0
  18.3 4.7 %collective-permute-start.2 = (bf16[384,1024]{1,0:T(8,128)(2,1)S(1)}, bf16[384,1024]{1,0:T(8,128)(2,1)S(1)}, u32[]{:S(2)}, u32[]{:S(2)}) collective-permute-start(bf16[384,1024]{1,0:T(8,128)(2,1)S(1)} %pad_maximum_fusion.w0), channel_id=1, source_target_pairs={{0,128},{64,192},{128,0},{192,64},{256,384},{320,448},{384,256},{4... | collective-permute-start | bytes 2359304 | tf_op jit(solution)/shard_map/ppermute | solution.py:264
  23.0 2.8 %collective-permute-start.1 = (bf16[384,1024]{1,0:T(8,128)(2,1)S(1)}, bf16[384,1024]{1,0:T(8,128)(2,1)S(1)}, u32[]{:S(2)}, u32[]{:S(2)}) collective-permute-start(bf16[384,1024]{1,0:T(8,128)(2,1)S(1)} %pad_maximum_fusion.w0), channel_id=1, source_target_pairs={{0,192},{64,0},{128,64},{192,128},{256,448},{320,256},{384,320},{4... | collective-permute-start | bytes 2359304 | tf_op jit(solution)/shard_map/ppermute | solution.py:264
  25.7 2.5 %collective-permute-start = (bf16[384,1024]{1,0:T(8,128)(2,1)S(1)}, bf16[384,1024]{1,0:T(8,128)(2,1)S(1)}, u32[]{:S(2)}, u32[]{:S(2)}) collective-permute-start(bf16[384,1024]{1,0:T(8,128)(2,1)S(1)} %pad_maximum_fusion.w0), channel_id=1, source_target_pairs={{0,64},{64,128},{128,192},{192,0},{256,320},{320,384},{384,448},{4... | collective-permute-start | bytes 2359304 | tf_op jit(solution)/shard_map/ppermute | solution.py:264
  28.3 18.4 %all-to-all-done = bf16[64,8,1024]{2,1,0:T(8,128)(2,1)} async-done(((bf16[64,8,1024]{2,1,0:T(8,128)(2,1)}), bf16[64,8,1024]{2,1,0:T(8,128)(2,1)}, u32[]{:S(2)}, u32[]{:S(2)}) %all-to-all-start) | async-done | bytes 1048608 | tf_op jit(solution)/shard_map/all_to_all | solution.py:245
  46.7 1.8 %shard_map.111 = (bf16[128,1024]{1,0:T(8,128)(2,1)S(1)}, bf16[128,1024]{1,0:T(8,128)(2,1)S(1)}) custom-call(s32[1]{0:T(128)} %bitcast.my_ref, s32[64,128]{1,0:T(8,128)S(1)} %bitcast.15, bf16[512,1024]{1,0:T(8,128)(2,1)} %bitcast.4.recv_ref), custom_call_target="tpu_custom_call" | custom-call | flops 300000000 | bytes 2000000 | tf_op jit(solution)/shard_map/pallas_call | solution.py:273
  48.5 0.0 copy-start.4
  48.5 0.0 copy-start.6
  48.5 7.9 %collective-permute-start.3 = (bf16[128,1024]{1,0:T(8,128)(2,1)S(1)}, bf16[128,1024]{1,0:T(8,128)(2,1)S(1)}, u32[]{:S(2)}, u32[]{:S(2)}) collective-permute-start(bf16[128,1024]{1,0:T(8,128)(2,1)S(1)} %get-tuple-element.24.chosen_ref.refs_0_), channel_id=1, source_target_pairs={{0,256},{64,320},{128,384},{192,448},{256,0},{320,64},{384,128},{4... | collective-permute-start | bytes 786440 | tf_op jit(solution)/shard_map/ppermute | solution.py:271
  56.5 1.9 %collective-permute-start.5 = (bf16[128,1024]{1,0:T(8,128)(2,1)S(1)}, bf16[128,1024]{1,0:T(8,128)(2,1)S(1)}, u32[]{:S(2)}, u32[]{:S(2)}) collective-permute-start(bf16[128,1024]{1,0:T(8,128)(2,1)S(1)} %get-tuple-element.25.weighted_ref.refs_2_), channel_id=1, source_target_pairs={{0,256},{64,320},{128,384},{192,448},{256,0},{320,64},{384,128},{4... | collective-permute-start | bytes 786440 | tf_op jit(solution)/shard_map/ppermute | solution.py:271
  58.4 0.0 collective-permute-done.2.w3
  58.4 0.0 collective-permute-done.1.w2
  58.4 0.0 collective-permute-done.w1
  58.4 5.0 %collective-permute-done.3.chosen_ref.refs_1_ = bf16[128,1024]{1,0:T(8,128)(2,1)S(1)} collective-permute-done((bf16[128,1024]{1,0:T(8,128)(2,1)S(1)}, bf16[128,1024]{1,0:T(8,128)(2,1)S(1)}, u32[]{:S(2)}, u32[]{:S(2)}) %collective-permute-start.3) | collective-permute-done | bytes 262176 | tf_op jit(solution)/shard_map/ppermute | solution.py:271
  63.5 1.7 %shard_map.113 = (bf16[128,1024]{1,0:T(8,128)(2,1)S(1)}, bf16[4,128,128]{2,1,0:T(8,128)(2,1)S(1)}, f32[4,128,256]{2,1,0:T(8,128)S(1)}) custom-call(bf16[128,1024]{1,0:T(8,128)(2,1)S(1)} %collective-permute-done.3.chosen_ref.refs_1_, bf16[384,1024]{1,0:T(8,128)(2,1)S(1)} %pad_maximum_fusion.w0, bf16[384,1024]{1,0:T(8,128)(2,1)S(1)} %collective-permute-done.w1, ...), custom_call_target="tpu_custom_call" | custom-call | flops 500000000 | bytes 5000000 | tf_op jit(solution)/shard_map/pallas_call | solution.py:278
  65.1 0.6 copy-done.10
  65.8 7.0 %collective-permute-start.4 = (bf16[128,1024]{1,0:T(8,128)(2,1)S(1)}, bf16[128,1024]{1,0:T(8,128)(2,1)S(1)}, u32[]{:S(2)}, u32[]{:S(2)}) collective-permute-start(bf16[128,1024]{1,0:T(8,128)(2,1)S(1)} %get-tuple-element.27), channel_id=1, source_target_pairs={{0,256},{64,320},{128,384},{192,448},{256,0},{320,64},{384,128},{4... | collective-permute-start | bytes 786440 | tf_op jit(solution)/shard_map/ppermute | solution.py:271
  72.8 0.0 collective-permute-done.5.weighted_ref.refs_3_
  72.8 0.0 copy-start
  72.8 1.2 shard_map.114
  74.0 0.0 copy-start.8
  74.0 5.3 %collective-permute-start.6 = (bf16[128,1024]{1,0:T(8,128)(2,1)S(1)}, bf16[128,1024]{1,0:T(8,128)(2,1)S(1)}, u32[]{:S(2)}, u32[]{:S(2)}) collective-permute-start(bf16[128,1024]{1,0:T(8,128)(2,1)S(1)} %get-tuple-element.29), channel_id=1, source_target_pairs={{0,256},{64,320},{128,384},{192,448},{256,0},{320,64},{384,128},{4... | collective-permute-start | bytes 786440 | tf_op jit(solution)/shard_map/ppermute | solution.py:271
  79.4 2.1 %shard_map.112 = (f32[256,1024]{1,0:T(8,128)S(1)}, bf16[4,128,128]{2,1,0:T(8,128)(2,1)S(1)}, bf16[4,128,256]{2,1,0:T(8,128)(2,1)S(1)}) custom-call(bf16[128,1024]{1,0:T(8,128)(2,1)S(1)} %get-tuple-element.24.chosen_ref.refs_0_, bf16[128,1024]{1,0:T(8,128)(2,1)S(1)} %get-tuple-element.25.weighted_ref.refs_2_, bf16[384,1024]{1,0:T(8,128)(2,1)S(1)} %pad_maximum_fusion.w0, ...), custom_call_target="tpu_custom_call" | custom-call | flops 1000000000 | bytes 6000000 | tf_op jit(solution)/shard_map/pallas_call | solution.py:291
  81.5 0.0 copy-start.12
  81.5 0.7 copy-done.12
  82.2 0.0 collective-permute-done.4.out_ref
  82.2 9.1 %collective-permute-done.6.back_ref = bf16[128,1024]{1,0:T(8,128)(2,1)S(1)} collective-permute-done((bf16[128,1024]{1,0:T(8,128)(2,1)S(1)}, bf16[128,1024]{1,0:T(8,128)(2,1)S(1)}, u32[]{:S(2)}, u32[]{:S(2)}) %collective-permute-start.6) | collective-permute-done | bytes 262176 | tf_op jit(solution)/shard_map/ppermute | solution.py:271
  91.3 1.6 shard_map.115
  92.9 0.0 copy-start.9
  92.9 17.5 %all-to-all-start.1 = ((bf16[64,8,1024]{2,1,0:T(8,128)(2,1)}), bf16[64,8,1024]{2,1,0:T(8,128)(2,1)S(1)}, u32[]{:S(2)}, u32[]{:S(2)}) async-start(bf16[64,8,1024]{2,1,0:T(8,128)(2,1)} %bitcast.8), calls=%async_computation.1 | async-start | bytes 2097152 | tf_op jit(solution)/shard_map/all_to_all | solution.py:245
  110.5 0.0 copy-start.13
  110.5 0.9 copy-done.13
  111.5 1.0 shard_map.117
  112.5 4.4 %collective-permute-start.7 = (bf16[384,1024]{1,0:T(8,128)(2,1)S(1)}, bf16[384,1024]{1,0:T(8,128)(2,1)S(1)}, u32[]{:S(2)}, u32[]{:S(2)}) collective-permute-start(bf16[384,1024]{1,0:T(8,128)(2,1)S(1)} %get-tuple-element.37), channel_id=1, source_target_pairs={{0,192},{64,0},{128,64},{192,128},{256,448},{320,256},{384,320},{4... | collective-permute-start | bytes 2359304 | tf_op jit(solution)/shard_map/ppermute | solution.py:313
  116.9 1.9 %collective-permute-start.8 = (bf16[384,1024]{1,0:T(8,128)(2,1)S(1)}, bf16[384,1024]{1,0:T(8,128)(2,1)S(1)}, u32[]{:S(2)}, u32[]{:S(2)}) collective-permute-start(bf16[384,1024]{1,0:T(8,128)(2,1)S(1)} %get-tuple-element.38), channel_id=1, source_target_pairs={{0,64},{64,128},{128,192},{192,0},{256,320},{320,384},{384,448},{4... | collective-permute-start | bytes 2359304 | tf_op jit(solution)/shard_map/ppermute | solution.py:314
  118.8 3.7 %collective-permute-start.9 = (bf16[384,1024]{1,0:T(8,128)(2,1)S(1)}, bf16[384,1024]{1,0:T(8,128)(2,1)S(1)}, u32[]{:S(2)}, u32[]{:S(2)}) collective-permute-start(bf16[384,1024]{1,0:T(8,128)(2,1)S(1)} %get-tuple-element.39), channel_id=1, source_target_pairs={{0,128},{64,192},{128,0},{192,64},{256,384},{320,448},{384,256},{4... | collective-permute-start | bytes 2359304 | tf_op jit(solution)/shard_map/ppermute | solution.py:308
  122.5 11.6 %collective-permute-done.7.g1 = bf16[384,1024]{1,0:T(8,128)(2,1)S(1)} collective-permute-done((bf16[384,1024]{1,0:T(8,128)(2,1)S(1)}, bf16[384,1024]{1,0:T(8,128)(2,1)S(1)}, u32[]{:S(2)}, u32[]{:S(2)}) %collective-permute-start.7) | collective-permute-done | bytes 786464 | tf_op jit(solution)/shard_map/ppermute | solution.py:313
  134.1 5.2 %collective-permute-done.8.g2 = bf16[384,1024]{1,0:T(8,128)(2,1)S(1)} collective-permute-done((bf16[384,1024]{1,0:T(8,128)(2,1)S(1)}, bf16[384,1024]{1,0:T(8,128)(2,1)S(1)}, u32[]{:S(2)}, u32[]{:S(2)}) %collective-permute-start.8) | collective-permute-done | bytes 786464 | tf_op jit(solution)/shard_map/ppermute | solution.py:314
  139.2 15.1 %collective-permute-done.9.g3 = bf16[384,1024]{1,0:T(8,128)(2,1)S(1)} collective-permute-done((bf16[384,1024]{1,0:T(8,128)(2,1)S(1)}, bf16[384,1024]{1,0:T(8,128)(2,1)S(1)}, u32[]{:S(2)}, u32[]{:S(2)}) %collective-permute-start.9) | collective-permute-done | bytes 786464 | tf_op jit(solution)/shard_map/ppermute | solution.py:308
  154.3 1.2 shard_map.118
  155.5 0.0 all-to-all-done.1
  155.5 1.7 %shard_map.116 = (bf16[128,1024]{1,0:T(8,128)(2,1)}, bf16[128,1024]{1,0:T(8,128)(2,1)}) custom-call(s32[1]{0:T(128)} %bitcast.my_ref, s32[64,128]{1,0:T(8,128)S(1)} %bitcast.17, f32[64,128]{1,0:T(8,128)S(1)} %bitcast.19, bf16[512,1024]{1,0:T(8,128)(2,1)S(1)} %bitcast.13), custom_call_target="tpu_custom_call" | custom-call | flops 400000000 | bytes 2000000 | tf_op jit(solution)/shard_map/pallas_call | solution.py:315
  (24 shorter events, 0.0 us)
Async XLA Ops:
  3.2 15.0 %copy-start.16 = (bf16[1,128,1024]{2,1,0:T(8,128)(2,1)S(1)}, bf16[1,128,1024]{2,1,0:T(8,128)(2,1)}, u32[]{:S(2)}) copy-start(bf16[1,128,1024]{2,1,0:T(8,128)(2,1)} %param.13) | copy-start | bytes 786436
  3.3 15.0 %copy-start.17 = (bf16[1,128,1024]{2,1,0:T(8,128)(2,1)S(1)}, bf16[1,128,1024]{2,1,0:T(8,128)(2,1)}, u32[]{:S(2)}) copy-start(bf16[1,128,1024]{2,1,0:T(8,128)(2,1)} %param.12) | copy-start | bytes 786436
  3.3 15.0 %copy-start.18 = (bf16[1,128,1024]{2,1,0:T(8,128)(2,1)S(1)}, bf16[1,128,1024]{2,1,0:T(8,128)(2,1)}, u32[]{:S(2)}) copy-start(bf16[1,128,1024]{2,1,0:T(8,128)(2,1)} %param.11) | copy-start | bytes 786436
  3.3 43.4 %all-to-all-start = ((bf16[64,8,1024]{2,1,0:T(8,128)(2,1)}), bf16[64,8,1024]{2,1,0:T(8,128)(2,1)}, u32[]{:S(2)}, u32[]{:S(2)}) async-start(bf16[64,8,1024]{2,1,0:T(8,128)(2,1)} %bitcast.20), calls=%async_computation | async-start | bytes 2097152 | tf_op jit(solution)/shard_map/all_to_all | solution.py:245
  18.2 28.5 %copy-start.2 = (s32[1,64,128]{2,1,0:T(8,128)S(1)}, s32[1,64,128]{2,1,0:T(8,128)}, u32[]{:S(2)}) copy-start(s32[1,64,128]{2,1,0:T(8,128)} %param.9) | copy-start | bytes 98308
  18.3 40.1 %collective-permute-start.2 = (bf16[384,1024]{1,0:T(8,128)(2,1)S(1)}, bf16[384,1024]{1,0:T(8,128)(2,1)S(1)}, u32[]{:S(2)}, u32[]{:S(2)}) collective-permute-start(bf16[384,1024]{1,0:T(8,128)(2,1)S(1)} %pad_maximum_fusion.w0), channel_id=1, source_target_pairs={{0,128},{64,192},{128,0},{192,64},{256,384},{320,448},{384,256},{4... | collective-permute-start | bytes 2359304 | tf_op jit(solution)/shard_map/ppermute | solution.py:264
  23.0 35.5 %collective-permute-start.1 = (bf16[384,1024]{1,0:T(8,128)(2,1)S(1)}, bf16[384,1024]{1,0:T(8,128)(2,1)S(1)}, u32[]{:S(2)}, u32[]{:S(2)}) collective-permute-start(bf16[384,1024]{1,0:T(8,128)(2,1)S(1)} %pad_maximum_fusion.w0), channel_id=1, source_target_pairs={{0,192},{64,0},{128,64},{192,128},{256,448},{320,256},{384,320},{4... | collective-permute-start | bytes 2359304 | tf_op jit(solution)/shard_map/ppermute | solution.py:264
  25.7 32.7 %collective-permute-start = (bf16[384,1024]{1,0:T(8,128)(2,1)S(1)}, bf16[384,1024]{1,0:T(8,128)(2,1)S(1)}, u32[]{:S(2)}, u32[]{:S(2)}) collective-permute-start(bf16[384,1024]{1,0:T(8,128)(2,1)S(1)} %pad_maximum_fusion.w0), channel_id=1, source_target_pairs={{0,64},{64,128},{128,192},{192,0},{256,320},{320,384},{384,448},{4... | collective-permute-start | bytes 2359304 | tf_op jit(solution)/shard_map/ppermute | solution.py:264
  48.5 30.9 %copy-start.4 = (bf16[128,1024]{1,0:T(8,128)(2,1)}, bf16[128,1024]{1,0:T(8,128)(2,1)S(1)}, u32[]{:S(2)}) copy-start(bf16[128,1024]{1,0:T(8,128)(2,1)S(1)} %get-tuple-element.24.chosen_ref.refs_0_) | copy-start | bytes 786436
  48.5 30.9 %copy-start.6 = (bf16[128,1024]{1,0:T(8,128)(2,1)}, bf16[128,1024]{1,0:T(8,128)(2,1)S(1)}, u32[]{:S(2)}) copy-start(bf16[128,1024]{1,0:T(8,128)(2,1)S(1)} %get-tuple-element.25.weighted_ref.refs_2_) | copy-start | bytes 786436
  48.5 14.9 %collective-permute-start.3 = (bf16[128,1024]{1,0:T(8,128)(2,1)S(1)}, bf16[128,1024]{1,0:T(8,128)(2,1)S(1)}, u32[]{:S(2)}, u32[]{:S(2)}) collective-permute-start(bf16[128,1024]{1,0:T(8,128)(2,1)S(1)} %get-tuple-element.24.chosen_ref.refs_0_), channel_id=1, source_target_pairs={{0,256},{64,320},{128,384},{192,448},{256,0},{320,64},{384,128},{4... | collective-permute-start | bytes 786440 | tf_op jit(solution)/shard_map/ppermute | solution.py:271
  56.5 16.3 %collective-permute-start.5 = (bf16[128,1024]{1,0:T(8,128)(2,1)S(1)}, bf16[128,1024]{1,0:T(8,128)(2,1)S(1)}, u32[]{:S(2)}, u32[]{:S(2)}) collective-permute-start(bf16[128,1024]{1,0:T(8,128)(2,1)S(1)} %get-tuple-element.25.weighted_ref.refs_2_), channel_id=1, source_target_pairs={{0,256},{64,320},{128,384},{192,448},{256,0},{320,64},{384,128},{4... | collective-permute-start | bytes 786440 | tf_op jit(solution)/shard_map/ppermute | solution.py:271
  65.1 0.6 copy-start.10
  65.8 16.4 %collective-permute-start.4 = (bf16[128,1024]{1,0:T(8,128)(2,1)S(1)}, bf16[128,1024]{1,0:T(8,128)(2,1)S(1)}, u32[]{:S(2)}, u32[]{:S(2)}) collective-permute-start(bf16[128,1024]{1,0:T(8,128)(2,1)S(1)} %get-tuple-element.27), channel_id=1, source_target_pairs={{0,256},{64,320},{128,384},{192,448},{256,0},{320,64},{384,128},{4... | collective-permute-start | bytes 786440 | tf_op jit(solution)/shard_map/ppermute | solution.py:271
  72.8 1.2 copy-start
  74.0 7.5 %copy-start.8 = (bf16[4,128,256]{2,1,0:T(8,128)(2,1)}, bf16[4,128,256]{2,1,0:T(8,128)(2,1)S(1)}, u32[]{:S(2)}) copy-start(bf16[4,128,256]{2,1,0:T(8,128)(2,1)S(1)} %get-tuple-element.35.refs_7_) | copy-start | bytes 786436
  74.0 17.3 %collective-permute-start.6 = (bf16[128,1024]{1,0:T(8,128)(2,1)S(1)}, bf16[128,1024]{1,0:T(8,128)(2,1)S(1)}, u32[]{:S(2)}, u32[]{:S(2)}) collective-permute-start(bf16[128,1024]{1,0:T(8,128)(2,1)S(1)} %get-tuple-element.29), channel_id=1, source_target_pairs={{0,256},{64,320},{128,384},{192,448},{256,0},{320,64},{384,128},{4... | collective-permute-start | bytes 786440 | tf_op jit(solution)/shard_map/ppermute | solution.py:271
  81.5 0.7 copy-start.12
  82.2 10.7 %copy-start.14 = (bf16[4,128,128]{2,1,0:T(8,128)(2,1)}, bf16[4,128,128]{2,1,0:T(8,128)(2,1)S(1)}, u32[]{:S(2)}) copy-start(bf16[4,128,128]{2,1,0:T(8,128)(2,1)S(1)} %get-tuple-element.32.refs_4_) | copy-start | bytes 393220
  92.9 17.6 %copy-start.1 = (bf16[128,1024]{1,0:T(8,128)(2,1)S(1)}, bf16[128,1024]{1,0:T(8,128)(2,1)}, u32[]{:S(2)}) copy-start(bf16[128,1024]{1,0:T(8,128)(2,1)} %copy-done) | copy-start | bytes 786436
  92.9 17.6 %copy-start.5 = (bf16[128,1024]{1,0:T(8,128)(2,1)S(1)}, bf16[128,1024]{1,0:T(8,128)(2,1)}, u32[]{:S(2)}) copy-start(bf16[128,1024]{1,0:T(8,128)(2,1)} %copy-done.4) | copy-start | bytes 786436
  92.9 17.6 %copy-start.7 = (bf16[128,1024]{1,0:T(8,128)(2,1)S(1)}, bf16[128,1024]{1,0:T(8,128)(2,1)}, u32[]{:S(2)}) copy-start(bf16[128,1024]{1,0:T(8,128)(2,1)} %copy-done.6) | copy-start | bytes 786436
  92.9 17.6 %copy-start.9 = (bf16[4,128,256]{2,1,0:T(8,128)(2,1)S(1)}, bf16[4,128,256]{2,1,0:T(8,128)(2,1)}, u32[]{:S(2)}) copy-start(bf16[4,128,256]{2,1,0:T(8,128)(2,1)} %copy-done.8) | copy-start | bytes 786436
  92.9 17.6 %copy-start.11 = (bf16[4,128,128]{2,1,0:T(8,128)(2,1)S(1)}, bf16[4,128,128]{2,1,0:T(8,128)(2,1)}, u32[]{:S(2)}) copy-start(bf16[4,128,128]{2,1,0:T(8,128)(2,1)} %copy-done.10) | copy-start | bytes 393220
  92.9 17.6 %copy-start.15 = (bf16[4,128,128]{2,1,0:T(8,128)(2,1)S(1)}, bf16[4,128,128]{2,1,0:T(8,128)(2,1)}, u32[]{:S(2)}) copy-start(bf16[4,128,128]{2,1,0:T(8,128)(2,1)} %copy-done.14) | copy-start | bytes 393220
  92.9 62.6 %all-to-all-start.1 = ((bf16[64,8,1024]{2,1,0:T(8,128)(2,1)}), bf16[64,8,1024]{2,1,0:T(8,128)(2,1)S(1)}, u32[]{:S(2)}, u32[]{:S(2)}) async-start(bf16[64,8,1024]{2,1,0:T(8,128)(2,1)} %bitcast.8), calls=%async_computation.1 | async-start | bytes 2097152 | tf_op jit(solution)/shard_map/all_to_all | solution.py:245
  110.5 1.0 copy-start.13
  112.5 21.6 %collective-permute-start.7 = (bf16[384,1024]{1,0:T(8,128)(2,1)S(1)}, bf16[384,1024]{1,0:T(8,128)(2,1)S(1)}, u32[]{:S(2)}, u32[]{:S(2)}) collective-permute-start(bf16[384,1024]{1,0:T(8,128)(2,1)S(1)} %get-tuple-element.37), channel_id=1, source_target_pairs={{0,192},{64,0},{128,64},{192,128},{256,448},{320,256},{384,320},{4... | collective-permute-start | bytes 2359304 | tf_op jit(solution)/shard_map/ppermute | solution.py:313
  116.9 22.4 %collective-permute-start.8 = (bf16[384,1024]{1,0:T(8,128)(2,1)S(1)}, bf16[384,1024]{1,0:T(8,128)(2,1)S(1)}, u32[]{:S(2)}, u32[]{:S(2)}) collective-permute-start(bf16[384,1024]{1,0:T(8,128)(2,1)S(1)} %get-tuple-element.38), channel_id=1, source_target_pairs={{0,64},{64,128},{128,192},{192,0},{256,320},{320,384},{384,448},{4... | collective-permute-start | bytes 2359304 | tf_op jit(solution)/shard_map/ppermute | solution.py:314
  118.8 35.5 %collective-permute-start.9 = (bf16[384,1024]{1,0:T(8,128)(2,1)S(1)}, bf16[384,1024]{1,0:T(8,128)(2,1)S(1)}, u32[]{:S(2)}, u32[]{:S(2)}) collective-permute-start(bf16[384,1024]{1,0:T(8,128)(2,1)S(1)} %get-tuple-element.39), channel_id=1, source_target_pairs={{0,128},{64,192},{128,0},{192,64},{256,384},{320,448},{384,256},{4... | collective-permute-start | bytes 2359304 | tf_op jit(solution)/shard_map/ppermute | solution.py:308
  154.3 1.2 copy-start.3

commit v5 on v2

v5 whole, which is shorter than its diff:
```python
import jax
import jax.numpy as jnp
from jax import lax
from jax.experimental import pallas as pl
from jax.experimental.pallas import tpu as pltpu
from jax.sharding import PartitionSpec as P

N_X = 4
N_HALF = 2
SLOT = 4
BF16 = jnp.bfloat16
F32 = jnp.float32

HALF_SWAP = [(i, (i + N_X) % (N_X * N_HALF)) for i in range(N_X * N_HALF)]


def x_shift(step):
    return [
        (h * N_X + i, h * N_X + (i + step) % N_X) for h in range(N_HALF) for i in range(N_X)
    ]


def mm(a, b, contract_a, contract_b):
    return lax.dot_general(
        a, b, (((contract_a,), (contract_b,)), ((), ())), preferred_element_type=F32
    )


def kernel_call(body, out_shapes, n_smem, n_vmem, flops, nbytes):
    return pl.pallas_call(
        body,
        out_shape=out_shapes,
        in_specs=[pl.BlockSpec(memory_space=pltpu.SMEM)] * n_smem
        + [pl.BlockSpec(memory_space=pltpu.VMEM)] * n_vmem,
        out_specs=jax.tree.map(lambda _: pl.BlockSpec(memory_space=pltpu.VMEM), out_shapes),
        cost_estimate=pl.CostEstimate(flops=flops, bytes_accessed=nbytes, transcendentals=0),
        compiler_params=pltpu.CompilerParams(vmem_limit_bytes=24 * 1024 * 1024),
    )


def strictly_before(n):
    rows = lax.broadcasted_iota(jnp.int32, (n, n), 0)
    cols = lax.broadcasted_iota(jnp.int32, (n, n), 1)
    return (rows < cols).astype(BF16)


def slot_tables(my, pick, weight, tok_rows):
    n_experts, cap = pick.shape
    low = my * tok_rows
    mine = (pick >= low) & (pick < low + tok_rows)
    rank = mm(mine.astype(F32).astype(BF16), strictly_before(cap), 1, 0)
    code = jnp.where(mine, rank, -1.0)
    place = jnp.where(mine, (pick - low + 1).astype(F32), 0.0)
    shape = (n_experts, 2 * SLOT, cap)
    slot = (lax.broadcasted_iota(jnp.int32, shape, 1) % SLOT).astype(F32)
    hit = jnp.broadcast_to(code[:, None, :], shape) == slot
    row = jnp.sum(
        jnp.where(hit, jnp.broadcast_to(place[:, None, :], shape), 0.0), axis=2, keepdims=True
    )
    share = jnp.sum(
        jnp.where(hit, jnp.broadcast_to(weight[:, None, :], shape), 0.0), axis=2, keepdims=True
    )
    return row - 1.0, share


def send_body(
    my_ref, pick_hbm, weight_hbm, tok_hbm, cot_hbm, out_ref, pick_ref, weight_ref, both_ref, sems
):
    tok_rows = tok_hbm.shape[0]
    copies = [
        pltpu.make_async_copy(pick_hbm, pick_ref, sems.at[0]),
        pltpu.make_async_copy(weight_hbm, weight_ref, sems.at[1]),
        pltpu.make_async_copy(tok_hbm, both_ref.at[:tok_rows], sems.at[2]),
        pltpu.make_async_copy(cot_hbm, both_ref.at[tok_rows:], sems.at[3]),
    ]
    for copy in copies:
        copy.start()
    copies[0].wait()
    copies[1].wait()
    n_experts = pick_ref.shape[0]
    row, share = slot_tables(my_ref[0], pick_ref[...], weight_ref[...], tok_rows)
    shape = (n_experts, 2 * SLOT, 2 * tok_rows)
    lane = lax.broadcasted_iota(jnp.int32, shape, 2).astype(F32)
    second = lax.broadcasted_iota(jnp.int32, (n_experts, 2 * SLOT, 1), 1) >= SLOT
    target = jnp.where(second & (row >= 0.0), row + float(tok_rows), row)
    scale = jnp.where(second, share, 1.0)
    n_slots = n_experts * 2 * SLOT
    select = (lane == target).astype(F32).reshape(n_slots, 2 * tok_rows).astype(BF16)
    scale = jnp.broadcast_to(scale, (n_experts, 2 * SLOT, 128)).reshape(n_slots, 128)
    copies[2].wait()
    copies[3].wait()
    rows = mm(select, both_ref[...], 1, 0)
    for c in range(rows.shape[1] // 128):
        part = (rows[:, c * 128 : (c + 1) * 128] * scale).astype(BF16)
        for h in range(N_HALF):
            out_ref[h * n_slots : (h + 1) * n_slots, c * 128 : (c + 1) * 128] = part


def place_table(own, n_experts):
    cap = own.shape[1]
    n_slots = n_experts * 2 * SLOT
    source = lax.shift_right_logical(own, 7)
    from_dev = (
        lax.broadcasted_iota(jnp.int32, (n_experts, cap), 0)
        == jnp.broadcast_to(source, (n_experts, cap))
    ).astype(F32)
    rank = jnp.sum(
        from_dev * mm(from_dev.astype(BF16), strictly_before(cap), 1, 0), axis=0, keepdims=True
    )
    position = source * (2 * SLOT) + rank.astype(jnp.int32)
    both = jnp.concatenate([position, position + SLOT], axis=1)
    sub = lax.broadcasted_iota(jnp.int32, (n_slots, 2 * cap), 0)
    return (sub == jnp.broadcast_to(both, (n_slots, 2 * cap))).astype(F32).astype(BF16)


def combine_body(my_ref, pick_ref, weight_ref, slots_ref, layer_ref, grad_ref):
    n_experts = pick_ref.shape[0]
    tok_rows = layer_ref.shape[0]
    n_slots = n_experts * 2 * SLOT
    row, share = slot_tables(my_ref[0], pick_ref[...], weight_ref[...], tok_rows)
    shape = (n_experts, 2 * SLOT, tok_rows)
    lane = lax.broadcasted_iota(jnp.int32, shape, 2).astype(F32)
    second = lax.broadcasted_iota(jnp.int32, shape, 1) >= SLOT
    hit = lane == row
    high = share.astype(BF16).astype(F32)
    low = share - high
    zero = jnp.zeros(shape, F32)
    first_hit = hit & ~second
    pieces = (
        jnp.where(first_hit, high, zero),
        jnp.where(hit & second, 1.0, zero),
        jnp.where(first_hit, low, zero),
    )
    table = jnp.concatenate([p.reshape(n_slots, tok_rows).astype(BF16) for p in pieces], axis=1)
    sums = mm(table, slots_ref[:n_slots], 0, 0) + mm(table, slots_ref[n_slots:], 0, 0)
    layer_ref[...] = (sums[:tok_rows] + sums[2 * tok_rows :]).astype(BF16)
    grad_ref[...] = sums[tok_rows : 2 * tok_rows].astype(BF16)


def expert_body(
    list0_ref,
    list1_ref,
    recv_hbm,
    w0_hbm,
    w1_hbm,
    w2_hbm,
    w3_hbm,
    slots_hbm,
    saved_hbm,
    recv_ref,
    w_ref,
    slots_ref,
    saved_ref,
    recv_sems,
    w_sems,
    slot_sems,
    saved_sem,
):
    cap = list0_ref.shape[1]
    n_rows = N_HALF * cap
    n_slots = recv_ref.shape[0] // N_HALF
    n_experts = n_slots // (2 * SLOT)
    width = w_ref.shape[1] // 3
    spans = [pl.ds(h * n_slots, n_slots) for h in range(N_HALF)]
    w_copies = [
        pltpu.make_async_copy(w_hbm, w_ref.at[i], w_sems.at[i])
        for i, w_hbm in enumerate((w0_hbm, w1_hbm, w2_hbm, w3_hbm))
    ]
    recv_copies = [
        pltpu.make_async_copy(recv_hbm.at[span, :], recv_ref.at[span, :], recv_sems.at[h])
        for h, span in enumerate(spans)
    ]
    for copy in recv_copies + w_copies:
        copy.start()
    places = [place_table(ref[...], n_experts) for ref in (list0_ref, list1_ref)]
    for h, span in enumerate(spans):
        recv_copies[h].wait()
        rows = mm(places[h], recv_ref[span, :], 0, 0).astype(BF16)
        saved_ref[h * cap : (h + 1) * cap] = rows[:cap]
        saved_ref[n_rows + h * cap : n_rows + (h + 1) * cap] = rows[cap:]
    chosen, weighted = saved_ref[:n_rows], saved_ref[n_rows : 2 * n_rows]
    out = jnp.zeros(chosen.shape, F32)
    back = jnp.zeros(chosen.shape, F32)
    for i, copy in enumerate(w_copies):
        copy.wait()
        w_both, w_down = w_ref[i, : 2 * width], w_ref[i, 2 * width :]
        pre = mm(chosen, w_both, 1, 1)
        d_hidden = mm(weighted, w_down, 1, 1)
        gate, up = pre[:, :width], pre[:, width:]
        sigma = jax.nn.sigmoid(gate)
        silu = gate * sigma
        hidden = (silu * up).astype(BF16)
        d_gate = (d_hidden * up * sigma * (1.0 + gate * (1.0 - sigma))).astype(BF16)
        d_up = (d_hidden * silu).astype(BF16)
        d_both = jnp.concatenate([d_gate, d_up], axis=1)
        out = out + mm(hidden, w_down, 1, 0)
        back = back + mm(d_both, w_both, 1, 0)
        saved_ref[2 * n_rows : 3 * n_rows, i * 2 * width : (i + 1) * 2 * width] = d_both
        saved_ref[3 * n_rows :, i * width : (i + 1) * width] = hidden
    saved_ref[3 * n_rows :, len(w_copies) * width :] = jnp.zeros(
        (n_rows, saved_ref.shape[1] - len(w_copies) * width), BF16
    )
    copies = [pltpu.make_async_copy(saved_ref, saved_hbm, saved_sem.at[0])]
    for h, span in enumerate(spans):
        total = jnp.concatenate(
            [out[h * cap : (h + 1) * cap], back[h * cap : (h + 1) * cap]], axis=0
        ).astype(BF16)
        slots_ref[span, :] = mm(places[h], total, 1, 0).astype(BF16)
        copy = pltpu.make_async_copy(
            slots_ref.at[span, :], slots_hbm.at[span, :], slot_sems.at[h]
        )
        copy.start()
        copies.append(copy)
    copies[0].start()
    for copy in copies:
        copy.wait()


def grads_body(saved_ref, *g_refs):
    n_rows = saved_ref.shape[0] // 4
    width = g_refs[0].shape[0] // 3
    chosen, weighted = saved_ref[:n_rows], saved_ref[n_rows : 2 * n_rows]
    for i, g_ref in enumerate(g_refs):
        d_both = saved_ref[2 * n_rows : 3 * n_rows, i * 2 * width : (i + 1) * 2 * width]
        hidden = saved_ref[3 * n_rows :, i * width : (i + 1) * width]
        g_ref[: 2 * width] = mm(d_both, chosen, 0, 0).astype(BF16)
        g_ref[2 * width :] = mm(hidden, weighted, 0, 0).astype(BF16)


def weight_sum_body(g_own, g1, g2, g3, gate_ref, up_ref, down_ref):
    width = gate_ref.shape[0]
    for i, ref in enumerate((gate_ref, up_ref, down_ref)):
        piece = pl.ds(i * width, width)
        ref[...] = (
            g_own[piece, :].astype(F32)
            + g1[piece, :].astype(F32)
            + g2[piece, :].astype(F32)
            + g3[piece, :].astype(F32)
        ).astype(BF16)


def per_device(tokens, cotangent, pick_lists, combine, w_gate, w_up, w_down):
    n_experts = lax.axis_size("expert")
    tok_rows, feat = tokens.shape
    cap = pick_lists.shape[2]
    width = w_gate.shape[1]
    n_peers = N_HALF * n_experts
    n_slots = n_peers * 2 * SLOT
    my = lax.axis_index("expert").astype(jnp.int32).reshape(1)
    half = lax.axis_index("dp") // N_X
    sds = jax.ShapeDtypeStruct
    picks, shares = pick_lists[0], combine[0]
    slot_rows = sds((n_slots, feat), BF16)
    groups = [
        [(h * N_X + x) * n_experts + e for h in range(N_HALF) for e in range(n_experts)]
        for x in range(N_X)
    ]

    def exchange(rows):
        out = lax.all_to_all(
            rows.reshape(n_peers, 2 * SLOT, feat),
            ("dp", "expert"),
            split_axis=0,
            concat_axis=0,
            axis_index_groups=groups,
            tiled=True,
        )
        return out.reshape(n_slots, feat)

    hbm = pl.BlockSpec(memory_space=pl.ANY)
    send = pl.pallas_call(
        send_body,
        out_shape=slot_rows,
        in_specs=[pl.BlockSpec(memory_space=pltpu.SMEM)] + [hbm] * 4,
        out_specs=pl.BlockSpec(memory_space=pltpu.VMEM),
        scratch_shapes=[
            pltpu.VMEM(picks.shape, picks.dtype),
            pltpu.VMEM(shares.shape, shares.dtype),
            pltpu.VMEM((2 * tok_rows, feat), BF16),
            pltpu.SemaphoreType.DMA((4,)),
        ],
        cost_estimate=pl.CostEstimate(flops=3 * 10**8, bytes_accessed=3 * 10**6, transcendentals=0),
    )(my, picks, shares, tokens, cotangent)
    recv = exchange(send)
    w_own = jnp.concatenate([w_gate[0], w_up[0], w_down[0]], axis=0)
    w_all = [w_own] + [lax.ppermute(w_own, "dp", x_shift(s)) for s in (1, -1, 2)]
    list_here = lax.dynamic_slice_in_dim(picks, my[0], 1, 0)
    list_there = lax.ppermute(list_here, "dp", HALF_SWAP)
    lists = [jnp.where(half == h, list_here, list_there) for h in range(N_HALF)]
    n_rows = N_HALF * cap
    n_blocks = len(w_all)
    saved_rows = sds((4 * n_rows, feat), BF16)
    vmem = pl.BlockSpec(memory_space=pltpu.VMEM)
    slots, saved = pl.pallas_call(
        expert_body,
        out_shape=(slot_rows, saved_rows),
        in_specs=[vmem] * N_HALF + [hbm] * (1 + n_blocks),
        out_specs=(hbm, hbm),
        scratch_shapes=[
            pltpu.VMEM(slot_rows.shape, BF16),
            pltpu.VMEM((n_blocks, 3 * width, feat), BF16),
            pltpu.VMEM(slot_rows.shape, BF16),
            pltpu.VMEM(saved_rows.shape, BF16),
        ]
        + [pltpu.SemaphoreType.DMA((n,)) for n in (N_HALF, n_blocks, N_HALF, 1)],
        cost_estimate=pl.CostEstimate(
            flops=3 * 10**9, bytes_accessed=10**7, transcendentals=0
        ),
        compiler_params=pltpu.CompilerParams(vmem_limit_bytes=62 * 1024 * 1024),
    )(*lists, recv, *w_all)
    returned = exchange(slots)
    g_own, *g_others = kernel_call(
        grads_body, (sds((3 * width, feat), BF16),) * n_blocks, 0, 1, 2 * 10**9, 5 * 10**6
    )(saved)
    g_home = [lax.ppermute(g, "dp", x_shift(-s)) for g, s in zip(g_others, (1, -1, 2))]
    layer_out, tokens_grad = kernel_call(
        combine_body, (sds((tok_rows, feat), BF16),) * 2, 1, 3, 8 * 10**8, 3 * 10**6
    )(my, picks, shares, returned)
    w_grads = kernel_call(
        weight_sum_body, (sds((width, feat), BF16),) * 3, 0, 4, 10**6, 5 * 10**6
    )(g_own, *g_home)
    return (layer_out, tokens_grad) + tuple(g[None] for g in w_grads)


def solution(mesh):
    rows = P(("dp", "expert"), None)
    lists = P("dp", None, None)
    weights = P("expert", "dp", None)
    return jax.shard_map(
        per_device,
        mesh=mesh,
        in_specs=(rows, rows, lists, lists, weights, weights, weights),
        out_specs=(rows, rows, weights, weights, weights),
        check_vma=False,
    )
```

time: 167 us -> 149 us (0.89); the launches traced: 165 us -> 149 us
  starting transfers between devices: 79.5 us -> 54.5 us
  waiting for transfers between devices: 67.8 us -> 75.5 us
    all_to_all x2, starting transfers between devices: 44.7 us -> 27.2 us  [exchange(): lax.all_to_all(rows.reshape(n_peers, 2 * SLOT, feat), ('dp', 'expert'), s...]
    ppermute x2 -> x1, starting transfers between devices: 15 us -> 7.49 us  [per_device(): list_there = lax.ppermute(list_here, 'dp', HALF_SWAP)]
    ppermute x2 -> x1, waiting for transfers between devices: 15.1 us -> 20.5 us  [per_device(): list_there = lax.ppermute(list_here, 'dp', HALF_SWAP)]
    all_to_all x2, waiting for transfers between devices: 18.2 us -> 22.2 us  [exchange(): lax.all_to_all(rows.reshape(n_peers, 2 * SLOT, feat), ('dp', 'expert'), s...]
    ppermute x3, waiting for transfers between devices: 2.94 us -> 1.27 us  [per_device(): lax.ppermute(w_own, 'dp', x_shift(s))]
    pallas_call x8 -> x3, Pallas kernels: 12 us -> 11.4 us  [the longest x1 8.31 us: per_device(): pl.pallas_call(expert_body, out_shape=(slot_rows, saved_rows), in_specs=[...]
  transfers between devices with their start and end apart: 10 -> 9, of which waited for: 8 -> 8; matrix products, arithmetic and copies ran while one was open for 0% -> 0% of each run, Pallas kernels for 4% -> 1%
where the time goes in v5:
time: 149 us
  waiting for transfers between devices  75.5 us (51%)
  starting transfers between devices  54.5 us (37%)
  Pallas kernels  15.5 us (10%)
  local copies, waits for them, and re-layouts  1.64 us (1%)
    ppermute x3, waiting for transfers between devices, per_device(): lax.ppermute(g, 'dp', x_shift(-s))  31.4 us
    all_to_all x2, starting transfers between devices, exchange(): lax.all_to_all(rows.reshape(n_peers, 2 * SLOT, feat), ('dp', 'expert'), s...  27.2 us
    all_to_all x2, waiting for transfers between devices, exchange(): lax.all_to_all(rows.reshape(n_peers, 2 * SLOT, feat), ('dp', 'expert'), s...  22.2 us
    ppermute x1, waiting for transfers between devices, per_device(): list_there = lax.ppermute(list_here, 'dp', HALF_SWAP)  20.5 us
    ppermute x3, starting transfers between devices, per_device(): lax.ppermute(g, 'dp', x_shift(-s))  9.93 us
    ppermute x3, starting transfers between devices, per_device(): lax.ppermute(w_own, 'dp', x_shift(s))  9.93 us
    pallas_call x1, Pallas kernels, per_device(): pl.pallas_call(expert_body, out_shape=(slot_rows, saved_rows), in_specs=[...  8.31 us
    ppermute x1, starting transfers between devices, per_device(): list_there = lax.ppermute(list_here, 'dp', HALF_SWAP)  7.49 us
  transfers between devices with their start and end apart: 9, of which 8 were waited for; matrix products, arithmetic and copies ran while one was open for 0% of the time, Pallas kernels for 1%

profile of v5, /device:TPU:1, one launch (start us, length us, event | category | flops | bytes accessed | tf_op | source)
XLA Modules:
  0.0 148.6 jit_solution(16482097895819674024)
XLA Ops:
  0.6 2.9 %shard_map.110 = bf16[1024,1024]{1,0:T(8,128)(2,1)} custom-call(s32[1]{0:T(128)} %bitcast.my_ref, s32[64,128]{1,0:T(8,128)} %bitcast.18, f32[64,128]{1,0:T(8,128)} %bitcast.20, bf16[128,1024]{1,0:T(8,128)(2,1)} %tok_hbm.1, bf16[128,1024]{1,0:T(8,128)(2,1)} %cot_hbm.1), custom_call_target="tpu_custom_call" | custom-call | flops 300000000 | bytes 3000000 | tf_op jit(solution)/shard_map/pallas_call | solution.py:271
  3.6 0.0 copy-start.4
  3.6 0.0 copy-start.5
  3.6 0.0 copy-start.6
  3.6 0.0 copy-start
  3.6 19.0 %all-to-all-start = ((bf16[128,8,1024]{2,1,0:T(8,128)(2,1)}), bf16[128,8,1024]{2,1,0:T(8,128)(2,1)}, u32[]{:S(2)}, u32[]{:S(2)}) async-start(bf16[128,8,1024]{2,1,0:T(8,128)(2,1)} %bitcast.22), calls=%async_computation | async-start | bytes 4194304 | tf_op jit(solution)/shard_map/all_to_all | solution.py:260
  22.6 0.0 copy-done.4
  22.7 0.0 copy-done.5
  22.7 0.0 copy-done.6
  22.7 0.1 pad_maximum_fusion.w0_hbm
  22.7 0.0 copy-start.3
  22.7 4.6 %collective-permute-start.3 = (bf16[384,1024]{1,0:T(8,128)(2,1)S(1)}, bf16[384,1024]{1,0:T(8,128)(2,1)S(1)}, u32[]{:S(2)}, u32[]{:S(2)}) collective-permute-start(bf16[384,1024]{1,0:T(8,128)(2,1)S(1)} %pad_maximum_fusion.w0_hbm), channel_id=1, source_target_pairs={{0,128},{64,192},{128,0},{192,64},{256,384},{320,448},{384,256},{4... | collective-permute-start | bytes 2359304 | tf_op jit(solution)/shard_map/ppermute | solution.py:286
  27.4 2.8 %collective-permute-start.2 = (bf16[384,1024]{1,0:T(8,128)(2,1)S(1)}, bf16[384,1024]{1,0:T(8,128)(2,1)S(1)}, u32[]{:S(2)}, u32[]{:S(2)}) collective-permute-start(bf16[384,1024]{1,0:T(8,128)(2,1)S(1)} %pad_maximum_fusion.w0_hbm), channel_id=1, source_target_pairs={{0,192},{64,0},{128,64},{192,128},{256,448},{320,256},{384,320},{4... | collective-permute-start | bytes 2359304 | tf_op jit(solution)/shard_map/ppermute | solution.py:286
  30.2 2.5 %collective-permute-start.1 = (bf16[384,1024]{1,0:T(8,128)(2,1)S(1)}, bf16[384,1024]{1,0:T(8,128)(2,1)}, u32[]{:S(2)}, u32[]{:S(2)}) collective-permute-start(bf16[384,1024]{1,0:T(8,128)(2,1)S(1)} %pad_maximum_fusion.w0_hbm), channel_id=1, source_target_pairs={{0,64},{64,128},{128,192},{192,0},{256,320},{320,384},{384,448},{4... | collective-permute-start | bytes 2359304 | tf_op jit(solution)/shard_map/ppermute | solution.py:286
  32.7 0.0 copy-done
  32.7 7.5 %collective-permute-start = (s32[1,128]{1,0:T(1,128)S(1)}, s32[1,128]{1,0:T(1,128)S(1)}, u32[]{:S(2)}, u32[]{:S(2)}) collective-permute-start(s32[1,128]{1,0:T(1,128)S(1)} %dynamic-slice_bitcast_fusion), channel_id=1, source_target_pairs={{0,256},{64,320},{128,384},{192,448},{256,0},{320,64},{384,128},{4... | collective-permute-start | bytes 1544 | tf_op jit(solution)/shard_map/ppermute | solution.py:288
  40.2 20.5 %collective-permute-done = s32[1,128]{1,0:T(1,128)S(1)} collective-permute-done((s32[1,128]{1,0:T(1,128)S(1)}, s32[1,128]{1,0:T(1,128)S(1)}, u32[]{:S(2)}, u32[]{:S(2)}) %collective-permute-start) | collective-permute-done | bytes 544 | tf_op jit(solution)/shard_map/ppermute | solution.py:288
  60.8 0.5 broadcast_select_fusion
  61.3 0.0 collective-permute-done.3.w3_hbm
  61.3 0.0 copy-start.7
  61.3 0.2 collective-permute-done.2.w2_hbm
  61.5 0.0 copy-start.8
  61.5 1.0 collective-permute-done.1.w1_hbm
  62.6 0.0 copy-done.8
  62.6 13.6 %all-to-all-done = bf16[128,8,1024]{2,1,0:T(8,128)(2,1)} async-done(((bf16[128,8,1024]{2,1,0:T(8,128)(2,1)}), bf16[128,8,1024]{2,1,0:T(8,128)(2,1)}, u32[]{:S(2)}, u32[]{:S(2)}) %all-to-all-start) | async-done | bytes 2097184 | tf_op jit(solution)/shard_map/all_to_all | solution.py:260
  76.1 0.0 copy-done.3
  76.1 0.0 copy-done.7
  76.1 8.3 %shard_map.111 = (bf16[1024,1024]{1,0:T(8,128)(2,1)}, bf16[1024,1024]{1,0:T(8,128)(2,1)}) custom-call(s32[1,128]{1,0:T(1,128)} %get-tuple-element.28.list0_ref, s32[1,128]{1,0:T(1,128)} %get-tuple-element.27.list1_ref, bf16[1024,1024]{1,0:T(8,128)(2,1)} %bitcast.5.recv_hbm, bf16[384,1024]{1,0:T(8,128)(2,1)} %copy-done.3, ...), custom_call_target="tpu_custom_call" | custom-call | flops 3000000000 | bytes 10000000 | tf_op jit(solution)/shard_map/pallas_call | solution.py:294
  84.5 8.2 %all-to-all-start.1 = ((bf16[128,8,1024]{2,1,0:T(8,128)(2,1)}), bf16[128,8,1024]{2,1,0:T(8,128)(2,1)S(1)}, u32[]{:S(2)}, u32[]{:S(2)}) async-start(bf16[128,8,1024]{2,1,0:T(8,128)(2,1)} %bitcast.23), calls=%async_computation.1 | async-start | bytes 4194304 | tf_op jit(solution)/shard_map/all_to_all | solution.py:260
  92.6 0.0 copy-start.2
  92.6 1.6 %copy-done.2 = bf16[1024,1024]{1,0:T(8,128)(2,1)S(1)} copy-done((bf16[1024,1024]{1,0:T(8,128)(2,1)S(1)}, bf16[1024,1024]{1,0:T(8,128)(2,1)}, u32[]{:S(2)}) %copy-start.2) | copy-done | bytes 2097176
  94.2 1.0 shard_map.113
  95.2 0.0 copy-start.1
  95.3 4.4 %collective-permute-start.4 = (bf16[384,1024]{1,0:T(8,128)(2,1)S(1)}, bf16[384,1024]{1,0:T(8,128)(2,1)S(1)}, u32[]{:S(2)}, u32[]{:S(2)}) collective-permute-start(bf16[384,1024]{1,0:T(8,128)(2,1)S(1)} %get-tuple-element.21), channel_id=1, source_target_pairs={{0,192},{64,0},{128,64},{192,128},{256,448},{320,256},{384,320},{4... | collective-permute-start | bytes 2359304 | tf_op jit(solution)/shard_map/ppermute | solution.py:315
  99.6 1.9 %collective-permute-start.5 = (bf16[384,1024]{1,0:T(8,128)(2,1)S(1)}, bf16[384,1024]{1,0:T(8,128)(2,1)S(1)}, u32[]{:S(2)}, u32[]{:S(2)}) collective-permute-start(bf16[384,1024]{1,0:T(8,128)(2,1)S(1)} %get-tuple-element.22), channel_id=1, source_target_pairs={{0,64},{64,128},{128,192},{192,0},{256,320},{320,384},{384,448},{4... | collective-permute-start | bytes 2359304 | tf_op jit(solution)/shard_map/ppermute | solution.py:315
  101.6 3.6 %collective-permute-start.6 = (bf16[384,1024]{1,0:T(8,128)(2,1)S(1)}, bf16[384,1024]{1,0:T(8,128)(2,1)S(1)}, u32[]{:S(2)}, u32[]{:S(2)}) collective-permute-start(bf16[384,1024]{1,0:T(8,128)(2,1)S(1)} %get-tuple-element.23), channel_id=1, source_target_pairs={{0,128},{64,192},{128,0},{192,64},{256,384},{320,448},{384,256},{4... | collective-permute-start | bytes 2359304 | tf_op jit(solution)/shard_map/ppermute | solution.py:315
  105.2 11.2 %collective-permute-done.4.g1 = bf16[384,1024]{1,0:T(8,128)(2,1)S(1)} collective-permute-done((bf16[384,1024]{1,0:T(8,128)(2,1)S(1)}, bf16[384,1024]{1,0:T(8,128)(2,1)S(1)}, u32[]{:S(2)}, u32[]{:S(2)}) %collective-permute-start.4) | collective-permute-done | bytes 786464 | tf_op jit(solution)/shard_map/ppermute | solution.py:315
  116.4 5.2 %collective-permute-done.5.g2 = bf16[384,1024]{1,0:T(8,128)(2,1)S(1)} collective-permute-done((bf16[384,1024]{1,0:T(8,128)(2,1)S(1)}, bf16[384,1024]{1,0:T(8,128)(2,1)S(1)}, u32[]{:S(2)}, u32[]{:S(2)}) %collective-permute-start.5) | collective-permute-done | bytes 786464 | tf_op jit(solution)/shard_map/ppermute | solution.py:315
  121.6 15.0 %collective-permute-done.6.g3 = bf16[384,1024]{1,0:T(8,128)(2,1)S(1)} collective-permute-done((bf16[384,1024]{1,0:T(8,128)(2,1)S(1)}, bf16[384,1024]{1,0:T(8,128)(2,1)S(1)}, u32[]{:S(2)}, u32[]{:S(2)}) %collective-permute-start.6) | collective-permute-done | bytes 786464 | tf_op jit(solution)/shard_map/ppermute | solution.py:315
  136.6 1.2 shard_map.114
  137.8 8.7 %all-to-all-done.1 = bf16[128,8,1024]{2,1,0:T(8,128)(2,1)S(1)} async-done(((bf16[128,8,1024]{2,1,0:T(8,128)(2,1)}), bf16[128,8,1024]{2,1,0:T(8,128)(2,1)S(1)}, u32[]{:S(2)}, u32[]{:S(2)}) %all-to-all-start.1) | async-done | bytes 2097184 | tf_op jit(solution)/shard_map/all_to_all | solution.py:260
  146.5 0.0 copy-done.1
  146.5 2.1 %shard_map.112 = (bf16[128,1024]{1,0:T(8,128)(2,1)}, bf16[128,1024]{1,0:T(8,128)(2,1)}) custom-call(s32[1]{0:T(128)} %bitcast.my_ref, s32[64,128]{1,0:T(8,128)S(1)} %bitcast.19, f32[64,128]{1,0:T(8,128)S(1)} %bitcast.21, bf16[1024,1024]{1,0:T(8,128)(2,1)S(1)} %bitcast.17), custom_call_target="tpu_custom_call" | custom-call | flops 800000000 | bytes 3000000 | tf_op jit(solution)/shard_map/pallas_call | solution.py:316
  (1 shorter events, 0.0 us)
Async XLA Ops:
  3.6 19.1 %copy-start.4 = (bf16[1,128,1024]{2,1,0:T(8,128)(2,1)S(1)}, bf16[1,128,1024]{2,1,0:T(8,128)(2,1)}, u32[]{:S(2)}) copy-start(bf16[1,128,1024]{2,1,0:T(8,128)(2,1)} %param.13) | copy-start | bytes 786436
  3.6 19.1 %copy-start.5 = (bf16[1,128,1024]{2,1,0:T(8,128)(2,1)S(1)}, bf16[1,128,1024]{2,1,0:T(8,128)(2,1)}, u32[]{:S(2)}) copy-start(bf16[1,128,1024]{2,1,0:T(8,128)(2,1)} %param.12) | copy-start | bytes 786436
  3.6 19.1 %copy-start.6 = (bf16[1,128,1024]{2,1,0:T(8,128)(2,1)S(1)}, bf16[1,128,1024]{2,1,0:T(8,128)(2,1)}, u32[]{:S(2)}) copy-start(bf16[1,128,1024]{2,1,0:T(8,128)(2,1)} %param.11) | copy-start | bytes 786436
  3.6 29.1 %copy-start = (s32[1,64,128]{2,1,0:T(8,128)S(1)}, s32[1,64,128]{2,1,0:T(8,128)}, u32[]{:S(2)}) copy-start(s32[1,64,128]{2,1,0:T(8,128)} %param.9) | copy-start | bytes 98308
  3.6 72.5 %all-to-all-start = ((bf16[128,8,1024]{2,1,0:T(8,128)(2,1)}), bf16[128,8,1024]{2,1,0:T(8,128)(2,1)}, u32[]{:S(2)}, u32[]{:S(2)}) async-start(bf16[128,8,1024]{2,1,0:T(8,128)(2,1)} %bitcast.22), calls=%async_computation | async-start | bytes 4194304 | tf_op jit(solution)/shard_map/all_to_all | solution.py:260
  22.7 53.4 %copy-start.3 = (bf16[384,1024]{1,0:T(8,128)(2,1)}, bf16[384,1024]{1,0:T(8,128)(2,1)S(1)}, u32[]{:S(2)}) copy-start(bf16[384,1024]{1,0:T(8,128)(2,1)S(1)} %pad_maximum_fusion.w0_hbm) | copy-start | bytes 2359300
  22.7 38.5 %collective-permute-start.3 = (bf16[384,1024]{1,0:T(8,128)(2,1)S(1)}, bf16[384,1024]{1,0:T(8,128)(2,1)S(1)}, u32[]{:S(2)}, u32[]{:S(2)}) collective-permute-start(bf16[384,1024]{1,0:T(8,128)(2,1)S(1)} %pad_maximum_fusion.w0_hbm), channel_id=1, source_target_pairs={{0,128},{64,192},{128,0},{192,64},{256,384},{320,448},{384,256},{4... | collective-permute-start | bytes 2359304 | tf_op jit(solution)/shard_map/ppermute | solution.py:286
  27.4 34.1 %collective-permute-start.2 = (bf16[384,1024]{1,0:T(8,128)(2,1)S(1)}, bf16[384,1024]{1,0:T(8,128)(2,1)S(1)}, u32[]{:S(2)}, u32[]{:S(2)}) collective-permute-start(bf16[384,1024]{1,0:T(8,128)(2,1)S(1)} %pad_maximum_fusion.w0_hbm), channel_id=1, source_target_pairs={{0,192},{64,0},{128,64},{192,128},{256,448},{320,256},{384,320},{4... | collective-permute-start | bytes 2359304 | tf_op jit(solution)/shard_map/ppermute | solution.py:286
  30.2 32.4 %collective-permute-start.1 = (bf16[384,1024]{1,0:T(8,128)(2,1)S(1)}, bf16[384,1024]{1,0:T(8,128)(2,1)}, u32[]{:S(2)}, u32[]{:S(2)}) collective-permute-start(bf16[384,1024]{1,0:T(8,128)(2,1)S(1)} %pad_maximum_fusion.w0_hbm), channel_id=1, source_target_pairs={{0,64},{64,128},{128,192},{192,0},{256,320},{320,384},{384,448},{4... | collective-permute-start | bytes 2359304 | tf_op jit(solution)/shard_map/ppermute | solution.py:286
  32.7 28.0 %collective-permute-start = (s32[1,128]{1,0:T(1,128)S(1)}, s32[1,128]{1,0:T(1,128)S(1)}, u32[]{:S(2)}, u32[]{:S(2)}) collective-permute-start(s32[1,128]{1,0:T(1,128)S(1)} %dynamic-slice_bitcast_fusion), channel_id=1, source_target_pairs={{0,256},{64,320},{128,384},{192,448},{256,0},{320,64},{384,128},{4... | collective-permute-start | bytes 1544 | tf_op jit(solution)/shard_map/ppermute | solution.py:288
  61.3 14.9 %copy-start.7 = (bf16[384,1024]{1,0:T(8,128)(2,1)}, bf16[384,1024]{1,0:T(8,128)(2,1)S(1)}, u32[]{:S(2)}) copy-start(bf16[384,1024]{1,0:T(8,128)(2,1)S(1)} %collective-permute-done.3.w3_hbm) | copy-start | bytes 2359300
  61.5 1.0 copy-start.8
  84.5 62.0 %all-to-all-start.1 = ((bf16[128,8,1024]{2,1,0:T(8,128)(2,1)}), bf16[128,8,1024]{2,1,0:T(8,128)(2,1)S(1)}, u32[]{:S(2)}, u32[]{:S(2)}) async-start(bf16[128,8,1024]{2,1,0:T(8,128)(2,1)} %bitcast.23), calls=%async_computation.1 | async-start | bytes 4194304 | tf_op jit(solution)/shard_map/all_to_all | solution.py:260
  92.6 1.6 %copy-start.2 = (bf16[1024,1024]{1,0:T(8,128)(2,1)S(1)}, bf16[1024,1024]{1,0:T(8,128)(2,1)}, u32[]{:S(2)}) copy-start(bf16[1024,1024]{1,0:T(8,128)(2,1)} %get-tuple-element.19.saved_ref) | copy-start | bytes 6291460
  95.2 51.2 %copy-start.1 = (f32[1,64,128]{2,1,0:T(8,128)S(1)}, f32[1,64,128]{2,1,0:T(8,128)}, u32[]{:S(2)}) copy-start(f32[1,64,128]{2,1,0:T(8,128)} %param.10) | copy-start | bytes 98308
  95.3 21.2 %collective-permute-start.4 = (bf16[384,1024]{1,0:T(8,128)(2,1)S(1)}, bf16[384,1024]{1,0:T(8,128)(2,1)S(1)}, u32[]{:S(2)}, u32[]{:S(2)}) collective-permute-start(bf16[384,1024]{1,0:T(8,128)(2,1)S(1)} %get-tuple-element.21), channel_id=1, source_target_pairs={{0,192},{64,0},{128,64},{192,128},{256,448},{320,256},{384,320},{4... | collective-permute-start | bytes 2359304 | tf_op jit(solution)/shard_map/ppermute | solution.py:315
  99.6 22.0 %collective-permute-start.5 = (bf16[384,1024]{1,0:T(8,128)(2,1)S(1)}, bf16[384,1024]{1,0:T(8,128)(2,1)S(1)}, u32[]{:S(2)}, u32[]{:S(2)}) collective-permute-start(bf16[384,1024]{1,0:T(8,128)(2,1)S(1)} %get-tuple-element.22), channel_id=1, source_target_pairs={{0,64},{64,128},{128,192},{192,0},{256,320},{320,384},{384,448},{4... | collective-permute-start | bytes 2359304 | tf_op jit(solution)/shard_map/ppermute | solution.py:315
  101.6 35.1 %collective-permute-start.6 = (bf16[384,1024]{1,0:T(8,128)(2,1)S(1)}, bf16[384,1024]{1,0:T(8,128)(2,1)S(1)}, u32[]{:S(2)}, u32[]{:S(2)}) collective-permute-start(bf16[384,1024]{1,0:T(8,128)(2,1)S(1)} %get-tuple-element.23), channel_id=1, source_target_pairs={{0,128},{64,192},{128,0},{192,64},{256,384},{320,448},{384,256},{4... | collective-permute-start | bytes 2359304 | tf_op jit(solution)/shard_map/ppermute | solution.py:315

commit v6 on v4

--- a/solution.py
+++ b/solution.py
@@ -24,6 +24,9 @@
     return lax.dot_general(
         a, b, (((contract_a,), (contract_b,)), ((), ())), preferred_element_type=F32
     )
+
+
+SMALL = pltpu.CompilerParams(vmem_limit_bytes=24 * 1024 * 1024)
 
 
 def kernel_call(body, out_shapes, n_smem, n_vmem, flops, nbytes):
@@ -34,7 +37,7 @@
         + [pl.BlockSpec(memory_space=pltpu.VMEM)] * n_vmem,
         out_specs=jax.tree.map(lambda _: pl.BlockSpec(memory_space=pltpu.VMEM), out_shapes),
         cost_estimate=pl.CostEstimate(flops=flops, bytes_accessed=nbytes, transcendentals=0),
-        compiler_params=pltpu.CompilerParams(vmem_limit_bytes=24 * 1024 * 1024),
+        compiler_params=SMALL,
     )
 
 
@@ -63,8 +66,32 @@
     return row - 1.0, share
 
 
+def stream_out(buffer, hbm, sems, piece):
+    n = sems.shape[0]
+    rows = buffer.shape[0] // n
+    copies = []
+    for c in range(n):
+        span = pl.ds(c * rows, rows)
+        buffer[span, :] = piece(c * rows, rows)
+        copies.append(pltpu.make_async_copy(buffer.at[span, :], hbm.at[span, :], sems.at[c]))
+        copies[-1].start()
+    for copy in copies:
+        copy.wait()
+
+
 def send_body(
-    my_ref, pick_hbm, weight_hbm, tok_hbm, cot_hbm, out_ref, pick_ref, weight_ref, both_ref, sems
+    my_ref,
+    pick_hbm,
+    weight_hbm,
+    tok_hbm,
+    cot_hbm,
+    out_hbm,
+    pick_ref,
+    weight_ref,
+    both_ref,
+    out_ref,
+    sems,
+    out_sems,
 ):
     tok_rows = tok_hbm.shape[0]
     copies = [
@@ -89,10 +116,15 @@
     scale = jnp.broadcast_to(scale, (n_experts, 2 * SLOT, 128)).reshape(n_slots, 128)
     copies[2].wait()
     copies[3].wait()
-    rows = mm(select, both_ref[...], 1, 0)
-    for c in range(rows.shape[1] // 128):
-        part = rows[:, c * 128 : (c + 1) * 128] * scale
-        out_ref[:, c * 128 : (c + 1) * 128] = part.astype(BF16)
+
+    def piece(start, n):
+        rows = mm(select[start : start + n], both_ref[...], 1, 0)
+        factor = scale[start : start + n]
+        return jnp.concatenate(
+            [rows[:, c : c + 128] * factor for c in range(0, rows.shape[1], 128)], axis=1
+        ).astype(BF16)
+
+    stream_out(out_ref, out_hbm, out_sems, piece)
 
 
 def place_table(my, pick_ref):
@@ -137,8 +169,22 @@
     grad_ref[...] = sums[tok_rows : 2 * tok_rows].astype(BF16)
 
 
-def compact_body(my_ref, pick_ref, recv_ref, chosen_ref, weighted_ref):
-    rows = mm(place_table(my_ref[0], pick_ref), recv_ref[...], 0, 0).astype(BF16)
+def compact_body(my_ref, pick_ref, recv_hbm, chosen_ref, weighted_ref, recv_ref, sems):
+    n = sems.shape[0]
+    n_rows = recv_ref.shape[0] // n
+    spans = [pl.ds(c * n_rows, n_rows) for c in range(n)]
+    copies = [
+        pltpu.make_async_copy(recv_hbm.at[span, :], recv_ref.at[span, :], sems.at[c])
+        for c, span in enumerate(spans)
+    ]
+    for copy in copies:
+        copy.start()
+    place = place_table(my_ref[0], pick_ref)
+    rows = jnp.zeros((place.shape[1], recv_ref.shape[1]), F32)
+    for c, copy in enumerate(copies):
+        copy.wait()
+        rows = rows + mm(place[c * n_rows : (c + 1) * n_rows], recv_ref[spans[c], :], 0, 0)
+    rows = rows.astype(BF16)
     cap = chosen_ref.shape[0]
     chosen_ref[...] = rows[:cap]
     weighted_ref[...] = rows[cap:]
@@ -211,10 +257,15 @@
         g_ref[n:] = mm(hidden, weighted, 0, 0).astype(g_ref.dtype)
 
 
-def expand_body(my_ref, pick_ref, own_ref, out_ref, back_ref, slots_ref):
+def expand_body(my_ref, pick_ref, own_ref, out_ref, back_ref, slots_hbm, slots_ref, sems):
     other = jnp.concatenate([out_ref[...], back_ref[...]], axis=0)
     total = (own_ref[...] + other.astype(F32)).astype(BF16)
-    slots_ref[...] = mm(place_table(my_ref[0], pick_ref), total, 1, 0).astype(BF16)
+    place = place_table(my_ref[0], pick_ref)
+
+    def piece(start, n):
+        return mm(place[start : start + n], total, 1, 0).astype(BF16)
+
+    stream_out(slots_ref, slots_hbm, sems, piece)
 
 
 def weight_sum_body(g_own, g1, g2, g3, gate_ref, up_ref, down_ref):
@@ -245,17 +296,23 @@
         out = lax.all_to_all(parts, "expert", split_axis=0, concat_axis=0, tiled=True)
         return out.reshape(n_slots, feat)
 
+    smem = pl.BlockSpec(memory_space=pltpu.SMEM)
+    vmem = pl.BlockSpec(memory_space=pltpu.VMEM)
     hbm = pl.BlockSpec(memory_space=pl.ANY)
+    dma = pltpu.SemaphoreType.DMA
+    slot_buffer = pltpu.VMEM(slot_rows.shape, slot_rows.dtype)
     send = pl.pallas_call(
         send_body,
         out_shape=slot_rows,
-        in_specs=[pl.BlockSpec(memory_space=pltpu.SMEM)] + [hbm] * 4,
-        out_specs=pl.BlockSpec(memory_space=pltpu.VMEM),
+        in_specs=[smem] + [hbm] * 4,
+        out_specs=hbm,
         scratch_shapes=[
             pltpu.VMEM(picks.shape, picks.dtype),
             pltpu.VMEM(shares.shape, shares.dtype),
             pltpu.VMEM((2 * tok_rows, feat), BF16),
-            pltpu.SemaphoreType.DMA((4,)),
+            slot_buffer,
+            dma((4,)),
+            dma((4,)),
         ],
         cost_estimate=pl.CostEstimate(flops=3 * 10**8, bytes_accessed=2 * 10**6, transcendentals=0),
     )(my, picks, shares, tokens, cotangent)
@@ -270,9 +327,15 @@
     def swap(rows):
         return lax.ppermute(rows, "dp", HALF_SWAP)
 
-    chosen, weighted = kernel_call(compact_body, (block,) * 2, 1, 2, 3 * 10**8, 2 * 10**6)(
-        my, picks, recv
-    )
+    chosen, weighted = pl.pallas_call(
+        compact_body,
+        out_shape=(block, block),
+        in_specs=[smem, vmem, hbm],
+        out_specs=(vmem, vmem),
+        scratch_shapes=[slot_buffer, dma((4,))],
+        cost_estimate=pl.CostEstimate(flops=3 * 10**8, bytes_accessed=2 * 10**6, transcendentals=0),
+        compiler_params=SMALL,
+    )(my, picks, recv)
     chosen_there = swap(chosen)
     weighted_there = swap(weighted)
     out_there, hidden_there, factors = kernel_call(
@@ -306,12 +369,18 @@
         grads, (sds(g_shape, BF16),) * 4, 0, 8, 10**9, 6 * 10**6
     )(chosen, chosen_there, weighted, weighted_there, hidden_here, hidden_there, d_here, d_there)
     g3 = lax.ppermute(g_far, "dp", x_shift(-2))
-    slots = kernel_call(expand_body, slot_rows, 1, 4, 3 * 10**8, 4 * 10**6)(
-        my, picks, part_here, out_back, back_back
-    )
-    returned = exchange(slots)
     g1 = lax.ppermute(g_right, "dp", x_shift(-1))
     g2 = lax.ppermute(g_left, "dp", x_shift(1))
+    slots = pl.pallas_call(
+        expand_body,
+        out_shape=slot_rows,
+        in_specs=[smem] + [vmem] * 4,
+        out_specs=hbm,
+        scratch_shapes=[slot_buffer, dma((4,))],
+        cost_estimate=pl.CostEstimate(flops=3 * 10**8, bytes_accessed=4 * 10**6, transcendentals=0),
+        compiler_params=SMALL,
+    )(my, picks, part_here, out_back, back_back)
+    returned = exchange(slots)
     layer_out, tokens_grad = kernel_call(
         combine_body, (sds((tok_rows, feat), BF16),) * 2, 1, 3, 4 * 10**8, 2 * 10**6
     )(my, picks, shares, returned)

time: 159 us -> 159 us (level)
  no operation moved by 1% of the time
where the time goes in v6:
time: 159 us; the launch traced here: 157 us
  starting transfers between devices  74.5 us (47%)
  waiting for transfers between devices  64.4 us (41%)
  Pallas kernels  14.6 us (9%)
  local copies, waits for them, and re-layouts  2.37 us (1%)
    all_to_all x2, starting transfers between devices, exchange(): lax.all_to_all(parts, 'expert', split_axis=0, concat_axis=0, tiled=True)  32.4 us
    ppermute x4, starting transfers between devices, swap(): return lax.ppermute(rows, 'dp', HALF_SWAP)  22.2 us
    all_to_all x2, waiting for transfers between devices, exchange(): lax.all_to_all(parts, 'expert', split_axis=0, concat_axis=0, tiled=True)  18.4 us
    ppermute x1, waiting for transfers between devices, per_device(): g3 = lax.ppermute(g_far, 'dp', x_shift(-2))  15 us
    ppermute x4, waiting for transfers between devices, swap(): return lax.ppermute(rows, 'dp', HALF_SWAP)  14.1 us
    ppermute x1, waiting for transfers between devices, per_device(): g1 = lax.ppermute(g_right, 'dp', x_shift(-1))  11.6 us
    ppermute x3, starting transfers between devices, per_device(): lax.ppermute(w_own, 'dp', x_shift(s))  9.94 us
    ppermute x1, waiting for transfers between devices, per_device(): g2 = lax.ppermute(g_left, 'dp', x_shift(1))  5.21 us
  transfers between devices with their start and end apart: 12, of which 6 were waited for; matrix products, arithmetic and copies ran while one was open for 0% of the time, Pallas kernels for 6%

profile of v6, /device:TPU:1, one launch (start us, length us, event | category | flops | bytes accessed | tf_op | source)
XLA Modules:
  0.0 157.0 jit_solution(13505397081681105579)
XLA Ops:
  0.6 2.4 %shard_map.110 = bf16[512,1024]{1,0:T(8,128)(2,1)} custom-call(s32[1]{0:T(128)} %bitcast.my_ref, s32[64,128]{1,0:T(8,128)} %bitcast.14, f32[64,128]{1,0:T(8,128)} %bitcast.18, bf16[128,1024]{1,0:T(8,128)(2,1)} %tok_hbm.1, bf16[128,1024]{1,0:T(8,128)(2,1)} %cot_hbm.1), custom_call_target="tpu_custom_call" | custom-call | flops 300000000 | bytes 2000000 | tf_op jit(solution)/shard_map/pallas_call | solution.py:304
  3.1 0.0 copy-start.16
  3.1 0.0 copy-start.17
  3.1 0.0 copy-start.18
  3.1 14.9 %all-to-all-start = ((bf16[64,8,1024]{2,1,0:T(8,128)(2,1)}), bf16[64,8,1024]{2,1,0:T(8,128)(2,1)}, u32[]{:S(2)}, u32[]{:S(2)}) async-start(bf16[64,8,1024]{2,1,0:T(8,128)(2,1)} %bitcast.20), calls=%async_computation | async-start | bytes 2097152 | tf_op jit(solution)/shard_map/all_to_all | solution.py:296
  18.0 0.0 copy-start.2
  18.1 0.1 pad_maximum_fusion.w0
  18.1 4.7 %collective-permute-start.2 = (bf16[384,1024]{1,0:T(8,128)(2,1)S(1)}, bf16[384,1024]{1,0:T(8,128)(2,1)S(1)}, u32[]{:S(2)}, u32[]{:S(2)}) collective-permute-start(bf16[384,1024]{1,0:T(8,128)(2,1)S(1)} %pad_maximum_fusion.w0), channel_id=1, source_target_pairs={{0,128},{64,192},{128,0},{192,64},{256,384},{320,448},{384,256},{4... | collective-permute-start | bytes 2359304 | tf_op jit(solution)/shard_map/ppermute | solution.py:321
  22.8 2.8 %collective-permute-start.1 = (bf16[384,1024]{1,0:T(8,128)(2,1)S(1)}, bf16[384,1024]{1,0:T(8,128)(2,1)S(1)}, u32[]{:S(2)}, u32[]{:S(2)}) collective-permute-start(bf16[384,1024]{1,0:T(8,128)(2,1)S(1)} %pad_maximum_fusion.w0), channel_id=1, source_target_pairs={{0,192},{64,0},{128,64},{192,128},{256,448},{320,256},{384,320},{4... | collective-permute-start | bytes 2359304 | tf_op jit(solution)/shard_map/ppermute | solution.py:321
  25.6 2.5 %collective-permute-start = (bf16[384,1024]{1,0:T(8,128)(2,1)S(1)}, bf16[384,1024]{1,0:T(8,128)(2,1)S(1)}, u32[]{:S(2)}, u32[]{:S(2)}) collective-permute-start(bf16[384,1024]{1,0:T(8,128)(2,1)S(1)} %pad_maximum_fusion.w0), channel_id=1, source_target_pairs={{0,64},{64,128},{128,192},{192,0},{256,320},{320,384},{384,448},{4... | collective-permute-start | bytes 2359304 | tf_op jit(solution)/shard_map/ppermute | solution.py:321
  28.1 18.4 %all-to-all-done = bf16[64,8,1024]{2,1,0:T(8,128)(2,1)} async-done(((bf16[64,8,1024]{2,1,0:T(8,128)(2,1)}), bf16[64,8,1024]{2,1,0:T(8,128)(2,1)}, u32[]{:S(2)}, u32[]{:S(2)}) %all-to-all-start) | async-done | bytes 1048608 | tf_op jit(solution)/shard_map/all_to_all | solution.py:296
  46.5 2.0 %shard_map.111 = (bf16[128,1024]{1,0:T(8,128)(2,1)S(1)}, bf16[128,1024]{1,0:T(8,128)(2,1)S(1)}) custom-call(s32[1]{0:T(128)} %bitcast.my_ref, s32[64,128]{1,0:T(8,128)S(1)} %bitcast.15, bf16[512,1024]{1,0:T(8,128)(2,1)} %bitcast.4.recv_hbm), custom_call_target="tpu_custom_call" | custom-call | flops 300000000 | bytes 2000000 | tf_op jit(solution)/shard_map/pallas_call | solution.py:330
  48.5 0.0 copy-start.4
  48.5 0.0 copy-start.6
  48.6 7.9 %collective-permute-start.3 = (bf16[128,1024]{1,0:T(8,128)(2,1)S(1)}, bf16[128,1024]{1,0:T(8,128)(2,1)S(1)}, u32[]{:S(2)}, u32[]{:S(2)}) collective-permute-start(bf16[128,1024]{1,0:T(8,128)(2,1)S(1)} %get-tuple-element.24.chosen_ref.refs_0_), channel_id=1, source_target_pairs={{0,256},{64,320},{128,384},{192,448},{256,0},{320,64},{384,128},{4... | collective-permute-start | bytes 786440 | tf_op jit(solution)/shard_map/ppermute | solution.py:328
  56.5 1.9 %collective-permute-start.5 = (bf16[128,1024]{1,0:T(8,128)(2,1)S(1)}, bf16[128,1024]{1,0:T(8,128)(2,1)S(1)}, u32[]{:S(2)}, u32[]{:S(2)}) collective-permute-start(bf16[128,1024]{1,0:T(8,128)(2,1)S(1)} %get-tuple-element.25.weighted_ref.refs_2_), channel_id=1, source_target_pairs={{0,256},{64,320},{128,384},{192,448},{256,0},{320,64},{384,128},{4... | collective-permute-start | bytes 786440 | tf_op jit(solution)/shard_map/ppermute | solution.py:328
  58.4 0.0 collective-permute-done.2.w3
  58.5 0.0 collective-permute-done.w1
  58.5 5.0 %collective-permute-done.3.chosen_ref.refs_1_ = bf16[128,1024]{1,0:T(8,128)(2,1)S(1)} collective-permute-done((bf16[128,1024]{1,0:T(8,128)(2,1)S(1)}, bf16[128,1024]{1,0:T(8,128)(2,1)S(1)}, u32[]{:S(2)}, u32[]{:S(2)}) %collective-permute-start.3) | collective-permute-done | bytes 262176 | tf_op jit(solution)/shard_map/ppermute | solution.py:328
  63.5 1.7 %shard_map.113 = (bf16[128,1024]{1,0:T(8,128)(2,1)S(1)}, bf16[4,128,128]{2,1,0:T(8,128)(2,1)S(1)}, f32[4,128,256]{2,1,0:T(8,128)S(1)}) custom-call(bf16[128,1024]{1,0:T(8,128)(2,1)S(1)} %collective-permute-done.3.chosen_ref.refs_1_, bf16[384,1024]{1,0:T(8,128)(2,1)S(1)} %pad_maximum_fusion.w0, bf16[384,1024]{1,0:T(8,128)(2,1)S(1)} %collective-permute-done.w1, ...), custom_call_target="tpu_custom_call" | custom-call | flops 500000000 | bytes 5000000 | tf_op jit(solution)/shard_map/pallas_call | solution.py:341
  65.2 0.6 copy-done.10
  65.8 7.0 %collective-permute-start.4 = (bf16[128,1024]{1,0:T(8,128)(2,1)S(1)}, bf16[128,1024]{1,0:T(8,128)(2,1)S(1)}, u32[]{:S(2)}, u32[]{:S(2)}) collective-permute-start(bf16[128,1024]{1,0:T(8,128)(2,1)S(1)} %get-tuple-element.27), channel_id=1, source_target_pairs={{0,256},{64,320},{128,384},{192,448},{256,0},{320,64},{384,128},{4... | collective-permute-start | bytes 786440 | tf_op jit(solution)/shard_map/ppermute | solution.py:328
  72.8 0.0 collective-permute-done.5.weighted_ref.refs_3_
  72.8 0.0 copy-start
  72.9 1.2 shard_map.114
  74.0 0.0 copy-start.8
  74.1 5.3 %collective-permute-start.6 = (bf16[128,1024]{1,0:T(8,128)(2,1)S(1)}, bf16[128,1024]{1,0:T(8,128)(2,1)S(1)}, u32[]{:S(2)}, u32[]{:S(2)}) collective-permute-start(bf16[128,1024]{1,0:T(8,128)(2,1)S(1)} %get-tuple-element.29), channel_id=1, source_target_pairs={{0,256},{64,320},{128,384},{192,448},{256,0},{320,64},{384,128},{4... | collective-permute-start | bytes 786440 | tf_op jit(solution)/shard_map/ppermute | solution.py:328
  79.4 2.1 %shard_map.112 = (f32[256,1024]{1,0:T(8,128)S(1)}, bf16[4,128,128]{2,1,0:T(8,128)(2,1)S(1)}, bf16[4,128,256]{2,1,0:T(8,128)(2,1)S(1)}) custom-call(bf16[128,1024]{1,0:T(8,128)(2,1)S(1)} %get-tuple-element.24.chosen_ref.refs_0_, bf16[128,1024]{1,0:T(8,128)(2,1)S(1)} %get-tuple-element.25.weighted_ref.refs_2_, bf16[384,1024]{1,0:T(8,128)(2,1)S(1)} %pad_maximum_fusion.w0, ...), custom_call_target="tpu_custom_call" | custom-call | flops 1000000000 | bytes 6000000 | tf_op jit(solution)/shard_map/pallas_call | solution.py:354
  81.6 0.0 copy-start.12
  81.6 0.7 copy-done.12
  82.3 9.1 %collective-permute-done.6.back_ref = bf16[128,1024]{1,0:T(8,128)(2,1)S(1)} collective-permute-done((bf16[128,1024]{1,0:T(8,128)(2,1)S(1)}, bf16[128,1024]{1,0:T(8,128)(2,1)S(1)}, u32[]{:S(2)}, u32[]{:S(2)}) %collective-permute-start.6) | collective-permute-done | bytes 262176 | tf_op jit(solution)/shard_map/ppermute | solution.py:328
  91.4 1.4 shard_map.115
  92.8 0.0 copy-start.1
  92.8 0.0 copy-start.5
  92.8 0.0 copy-start.7
  92.8 0.0 copy-start.9
  92.8 17.5 %all-to-all-start.1 = ((bf16[64,8,1024]{2,1,0:T(8,128)(2,1)}), bf16[64,8,1024]{2,1,0:T(8,128)(2,1)S(1)}, u32[]{:S(2)}, u32[]{:S(2)}) async-start(bf16[64,8,1024]{2,1,0:T(8,128)(2,1)} %bitcast.8), calls=%async_computation.1 | async-start | bytes 2097152 | tf_op jit(solution)/shard_map/all_to_all | solution.py:296
  110.4 0.0 copy-start.13
  110.4 0.9 copy-done.13
  111.4 1.0 shard_map.117
  112.4 4.4 %collective-permute-start.7 = (bf16[384,1024]{1,0:T(8,128)(2,1)S(1)}, bf16[384,1024]{1,0:T(8,128)(2,1)S(1)}, u32[]{:S(2)}, u32[]{:S(2)}) collective-permute-start(bf16[384,1024]{1,0:T(8,128)(2,1)S(1)} %get-tuple-element.37), channel_id=1, source_target_pairs={{0,192},{64,0},{128,64},{192,128},{256,448},{320,256},{384,320},{4... | collective-permute-start | bytes 2359304 | tf_op jit(solution)/shard_map/ppermute | solution.py:372
  116.8 1.9 %collective-permute-start.8 = (bf16[384,1024]{1,0:T(8,128)(2,1)S(1)}, bf16[384,1024]{1,0:T(8,128)(2,1)S(1)}, u32[]{:S(2)}, u32[]{:S(2)}) collective-permute-start(bf16[384,1024]{1,0:T(8,128)(2,1)S(1)} %get-tuple-element.38), channel_id=1, source_target_pairs={{0,64},{64,128},{128,192},{192,0},{256,320},{320,384},{384,448},{4... | collective-permute-start | bytes 2359304 | tf_op jit(solution)/shard_map/ppermute | solution.py:373
  118.7 3.6 %collective-permute-start.9 = (bf16[384,1024]{1,0:T(8,128)(2,1)S(1)}, bf16[384,1024]{1,0:T(8,128)(2,1)S(1)}, u32[]{:S(2)}, u32[]{:S(2)}) collective-permute-start(bf16[384,1024]{1,0:T(8,128)(2,1)S(1)} %get-tuple-element.39), channel_id=1, source_target_pairs={{0,128},{64,192},{128,0},{192,64},{256,384},{320,448},{384,256},{4... | collective-permute-start | bytes 2359304 | tf_op jit(solution)/shard_map/ppermute | solution.py:371
  122.3 11.6 %collective-permute-done.7.g1 = bf16[384,1024]{1,0:T(8,128)(2,1)S(1)} collective-permute-done((bf16[384,1024]{1,0:T(8,128)(2,1)S(1)}, bf16[384,1024]{1,0:T(8,128)(2,1)S(1)}, u32[]{:S(2)}, u32[]{:S(2)}) %collective-permute-start.7) | collective-permute-done | bytes 786464 | tf_op jit(solution)/shard_map/ppermute | solution.py:372
  134.0 5.2 %collective-permute-done.8.g2 = bf16[384,1024]{1,0:T(8,128)(2,1)S(1)} collective-permute-done((bf16[384,1024]{1,0:T(8,128)(2,1)S(1)}, bf16[384,1024]{1,0:T(8,128)(2,1)S(1)}, u32[]{:S(2)}, u32[]{:S(2)}) %collective-permute-start.8) | collective-permute-done | bytes 786464 | tf_op jit(solution)/shard_map/ppermute | solution.py:373
  139.2 15.0 %collective-permute-done.9.g3 = bf16[384,1024]{1,0:T(8,128)(2,1)S(1)} collective-permute-done((bf16[384,1024]{1,0:T(8,128)(2,1)S(1)}, bf16[384,1024]{1,0:T(8,128)(2,1)S(1)}, u32[]{:S(2)}, u32[]{:S(2)}) %collective-permute-start.9) | collective-permute-done | bytes 786464 | tf_op jit(solution)/shard_map/ppermute | solution.py:371
  154.2 1.2 shard_map.118
  155.4 1.7 %shard_map.116 = (bf16[128,1024]{1,0:T(8,128)(2,1)}, bf16[128,1024]{1,0:T(8,128)(2,1)}) custom-call(s32[1]{0:T(128)} %bitcast.my_ref, s32[64,128]{1,0:T(8,128)S(1)} %bitcast.17, f32[64,128]{1,0:T(8,128)S(1)} %bitcast.19, bf16[512,1024]{1,0:T(8,128)(2,1)S(1)} %bitcast.13), custom_call_target="tpu_custom_call" | custom-call | flops 400000000 | bytes 2000000 | tf_op jit(solution)/shard_map/pallas_call | solution.py:384
  (24 shorter events, 0.1 us)
Async XLA Ops:
  3.1 15.0 %copy-start.16 = (bf16[1,128,1024]{2,1,0:T(8,128)(2,1)S(1)}, bf16[1,128,1024]{2,1,0:T(8,128)(2,1)}, u32[]{:S(2)}) copy-start(bf16[1,128,1024]{2,1,0:T(8,128)(2,1)} %param.13) | copy-start | bytes 786436
  3.1 15.0 %copy-start.17 = (bf16[1,128,1024]{2,1,0:T(8,128)(2,1)S(1)}, bf16[1,128,1024]{2,1,0:T(8,128)(2,1)}, u32[]{:S(2)}) copy-start(bf16[1,128,1024]{2,1,0:T(8,128)(2,1)} %param.12) | copy-start | bytes 786436
  3.1 15.0 %copy-start.18 = (bf16[1,128,1024]{2,1,0:T(8,128)(2,1)S(1)}, bf16[1,128,1024]{2,1,0:T(8,128)(2,1)}, u32[]{:S(2)}) copy-start(bf16[1,128,1024]{2,1,0:T(8,128)(2,1)} %param.11) | copy-start | bytes 786436
  3.1 43.4 %all-to-all-start = ((bf16[64,8,1024]{2,1,0:T(8,128)(2,1)}), bf16[64,8,1024]{2,1,0:T(8,128)(2,1)}, u32[]{:S(2)}, u32[]{:S(2)}) async-start(bf16[64,8,1024]{2,1,0:T(8,128)(2,1)} %bitcast.20), calls=%async_computation | async-start | bytes 2097152 | tf_op jit(solution)/shard_map/all_to_all | solution.py:296
  18.0 28.5 %copy-start.2 = (s32[1,64,128]{2,1,0:T(8,128)S(1)}, s32[1,64,128]{2,1,0:T(8,128)}, u32[]{:S(2)}) copy-start(s32[1,64,128]{2,1,0:T(8,128)} %param.9) | copy-start | bytes 98308
  18.1 40.3 %collective-permute-start.2 = (bf16[384,1024]{1,0:T(8,128)(2,1)S(1)}, bf16[384,1024]{1,0:T(8,128)(2,1)S(1)}, u32[]{:S(2)}, u32[]{:S(2)}) collective-permute-start(bf16[384,1024]{1,0:T(8,128)(2,1)S(1)} %pad_maximum_fusion.w0), channel_id=1, source_target_pairs={{0,128},{64,192},{128,0},{192,64},{256,384},{320,448},{384,256},{4... | collective-permute-start | bytes 2359304 | tf_op jit(solution)/shard_map/ppermute | solution.py:321
  22.8 35.7 %collective-permute-start.1 = (bf16[384,1024]{1,0:T(8,128)(2,1)S(1)}, bf16[384,1024]{1,0:T(8,128)(2,1)S(1)}, u32[]{:S(2)}, u32[]{:S(2)}) collective-permute-start(bf16[384,1024]{1,0:T(8,128)(2,1)S(1)} %pad_maximum_fusion.w0), channel_id=1, source_target_pairs={{0,192},{64,0},{128,64},{192,128},{256,448},{320,256},{384,320},{4... | collective-permute-start | bytes 2359304 | tf_op jit(solution)/shard_map/ppermute | solution.py:321
  25.6 32.9 %collective-permute-start = (bf16[384,1024]{1,0:T(8,128)(2,1)S(1)}, bf16[384,1024]{1,0:T(8,128)(2,1)S(1)}, u32[]{:S(2)}, u32[]{:S(2)}) collective-permute-start(bf16[384,1024]{1,0:T(8,128)(2,1)S(1)} %pad_maximum_fusion.w0), channel_id=1, source_target_pairs={{0,64},{64,128},{128,192},{192,0},{256,320},{320,384},{384,448},{4... | collective-permute-start | bytes 2359304 | tf_op jit(solution)/shard_map/ppermute | solution.py:321
  48.5 30.9 %copy-start.4 = (bf16[128,1024]{1,0:T(8,128)(2,1)}, bf16[128,1024]{1,0:T(8,128)(2,1)S(1)}, u32[]{:S(2)}) copy-start(bf16[128,1024]{1,0:T(8,128)(2,1)S(1)} %get-tuple-element.24.chosen_ref.refs_0_) | copy-start | bytes 786436
  48.5 30.9 %copy-start.6 = (bf16[128,1024]{1,0:T(8,128)(2,1)}, bf16[128,1024]{1,0:T(8,128)(2,1)S(1)}, u32[]{:S(2)}) copy-start(bf16[128,1024]{1,0:T(8,128)(2,1)S(1)} %get-tuple-element.25.weighted_ref.refs_2_) | copy-start | bytes 786436
  48.6 14.9 %collective-permute-start.3 = (bf16[128,1024]{1,0:T(8,128)(2,1)S(1)}, bf16[128,1024]{1,0:T(8,128)(2,1)S(1)}, u32[]{:S(2)}, u32[]{:S(2)}) collective-permute-start(bf16[128,1024]{1,0:T(8,128)(2,1)S(1)} %get-tuple-element.24.chosen_ref.refs_0_), channel_id=1, source_target_pairs={{0,256},{64,320},{128,384},{192,448},{256,0},{320,64},{384,128},{4... | collective-permute-start | bytes 786440 | tf_op jit(solution)/shard_map/ppermute | solution.py:328
  56.5 16.3 %collective-permute-start.5 = (bf16[128,1024]{1,0:T(8,128)(2,1)S(1)}, bf16[128,1024]{1,0:T(8,128)(2,1)S(1)}, u32[]{:S(2)}, u32[]{:S(2)}) collective-permute-start(bf16[128,1024]{1,0:T(8,128)(2,1)S(1)} %get-tuple-element.25.weighted_ref.refs_2_), channel_id=1, source_target_pairs={{0,256},{64,320},{128,384},{192,448},{256,0},{320,64},{384,128},{4... | collective-permute-start | bytes 786440 | tf_op jit(solution)/shard_map/ppermute | solution.py:328
  65.2 0.6 copy-start.10
  65.8 16.5 %collective-permute-start.4 = (bf16[128,1024]{1,0:T(8,128)(2,1)S(1)}, bf16[128,1024]{1,0:T(8,128)(2,1)S(1)}, u32[]{:S(2)}, u32[]{:S(2)}) collective-permute-start(bf16[128,1024]{1,0:T(8,128)(2,1)S(1)} %get-tuple-element.27), channel_id=1, source_target_pairs={{0,256},{64,320},{128,384},{192,448},{256,0},{320,64},{384,128},{4... | collective-permute-start | bytes 786440 | tf_op jit(solution)/shard_map/ppermute | solution.py:328
  72.8 1.2 copy-start
  74.0 7.5 %copy-start.8 = (bf16[4,128,256]{2,1,0:T(8,128)(2,1)}, bf16[4,128,256]{2,1,0:T(8,128)(2,1)S(1)}, u32[]{:S(2)}) copy-start(bf16[4,128,256]{2,1,0:T(8,128)(2,1)S(1)} %get-tuple-element.35.refs_7_) | copy-start | bytes 786436
  74.1 17.3 %collective-permute-start.6 = (bf16[128,1024]{1,0:T(8,128)(2,1)S(1)}, bf16[128,1024]{1,0:T(8,128)(2,1)S(1)}, u32[]{:S(2)}, u32[]{:S(2)}) collective-permute-start(bf16[128,1024]{1,0:T(8,128)(2,1)S(1)} %get-tuple-element.29), channel_id=1, source_target_pairs={{0,256},{64,320},{128,384},{192,448},{256,0},{320,64},{384,128},{4... | collective-permute-start | bytes 786440 | tf_op jit(solution)/shard_map/ppermute | solution.py:328
  81.6 0.7 copy-start.12
  82.3 10.5 %copy-start.14 = (bf16[4,128,128]{2,1,0:T(8,128)(2,1)}, bf16[4,128,128]{2,1,0:T(8,128)(2,1)S(1)}, u32[]{:S(2)}) copy-start(bf16[4,128,128]{2,1,0:T(8,128)(2,1)S(1)} %get-tuple-element.32.refs_4_) | copy-start | bytes 393220
  92.8 17.6 %copy-start.1 = (bf16[128,1024]{1,0:T(8,128)(2,1)S(1)}, bf16[128,1024]{1,0:T(8,128)(2,1)}, u32[]{:S(2)}) copy-start(bf16[128,1024]{1,0:T(8,128)(2,1)} %copy-done) | copy-start | bytes 786436
  92.8 17.6 %copy-start.5 = (bf16[128,1024]{1,0:T(8,128)(2,1)S(1)}, bf16[128,1024]{1,0:T(8,128)(2,1)}, u32[]{:S(2)}) copy-start(bf16[128,1024]{1,0:T(8,128)(2,1)} %copy-done.4) | copy-start | bytes 786436
  92.8 17.6 %copy-start.7 = (bf16[128,1024]{1,0:T(8,128)(2,1)S(1)}, bf16[128,1024]{1,0:T(8,128)(2,1)}, u32[]{:S(2)}) copy-start(bf16[128,1024]{1,0:T(8,128)(2,1)} %copy-done.6) | copy-start | bytes 786436
  92.8 17.6 %copy-start.9 = (bf16[4,128,256]{2,1,0:T(8,128)(2,1)S(1)}, bf16[4,128,256]{2,1,0:T(8,128)(2,1)}, u32[]{:S(2)}) copy-start(bf16[4,128,256]{2,1,0:T(8,128)(2,1)} %copy-done.8) | copy-start | bytes 786436
  92.8 17.6 %copy-start.11 = (bf16[4,128,128]{2,1,0:T(8,128)(2,1)S(1)}, bf16[4,128,128]{2,1,0:T(8,128)(2,1)}, u32[]{:S(2)}) copy-start(bf16[4,128,128]{2,1,0:T(8,128)(2,1)} %copy-done.10) | copy-start | bytes 393220
  92.8 17.6 %copy-start.15 = (bf16[4,128,128]{2,1,0:T(8,128)(2,1)S(1)}, bf16[4,128,128]{2,1,0:T(8,128)(2,1)}, u32[]{:S(2)}) copy-start(bf16[4,128,128]{2,1,0:T(8,128)(2,1)} %copy-done.14) | copy-start | bytes 393220
  92.8 62.5 %all-to-all-start.1 = ((bf16[64,8,1024]{2,1,0:T(8,128)(2,1)}), bf16[64,8,1024]{2,1,0:T(8,128)(2,1)S(1)}, u32[]{:S(2)}, u32[]{:S(2)}) async-start(bf16[64,8,1024]{2,1,0:T(8,128)(2,1)} %bitcast.8), calls=%async_computation.1 | async-start | bytes 2097152 | tf_op jit(solution)/shard_map/all_to_all | solution.py:296
  110.4 1.0 copy-start.13
  112.4 21.6 %collective-permute-start.7 = (bf16[384,1024]{1,0:T(8,128)(2,1)S(1)}, bf16[384,1024]{1,0:T(8,128)(2,1)S(1)}, u32[]{:S(2)}, u32[]{:S(2)}) collective-permute-start(bf16[384,1024]{1,0:T(8,128)(2,1)S(1)} %get-tuple-element.37), channel_id=1, source_target_pairs={{0,192},{64,0},{128,64},{192,128},{256,448},{320,256},{384,320},{4... | collective-permute-start | bytes 2359304 | tf_op jit(solution)/shard_map/ppermute | solution.py:372
  116.8 22.4 %collective-permute-start.8 = (bf16[384,1024]{1,0:T(8,128)(2,1)S(1)}, bf16[384,1024]{1,0:T(8,128)(2,1)S(1)}, u32[]{:S(2)}, u32[]{:S(2)}) collective-permute-start(bf16[384,1024]{1,0:T(8,128)(2,1)S(1)} %get-tuple-element.38), channel_id=1, source_target_pairs={{0,64},{64,128},{128,192},{192,0},{256,320},{320,384},{384,448},{4... | collective-permute-start | bytes 2359304 | tf_op jit(solution)/shard_map/ppermute | solution.py:373
  118.7 35.5 %collective-permute-start.9 = (bf16[384,1024]{1,0:T(8,128)(2,1)S(1)}, bf16[384,1024]{1,0:T(8,128)(2,1)S(1)}, u32[]{:S(2)}, u32[]{:S(2)}) collective-permute-start(bf16[384,1024]{1,0:T(8,128)(2,1)S(1)} %get-tuple-element.39), channel_id=1, source_target_pairs={{0,128},{64,192},{128,0},{192,64},{256,384},{320,448},{384,256},{4... | collective-permute-start | bytes 2359304 | tf_op jit(solution)/shard_map/ppermute | solution.py:371
  154.2 1.2 copy-start.3
